TPU v7x, 128 devices: a whole 4x4x4 slice. The times are simulated.
128 devices in a mesh: fluid: 32 (over x, y, core), solid: 4 (over z).
Axes of the slice: x: 4, y: 4, z: 4, core: 2. Of those that a mesh axis runs over, the one named last changes fastest.
Arguments:
- rbf_blocks: bfloat16 [13312, 256, 256], P(('fluid', 'solid')), may hold values from -0.375 to 0.375
- fluid_traction: bfloat16 [13312, 768], P(('fluid', 'solid')), may hold values from -24 to 24
- fluid_mass: bfloat16 [13312, 768], P(('fluid', 'solid')), may hold values from 0.19921875 to 2
- route: int32 [13312, 1], P(('fluid', 'solid')), may hold values from 0 to 127; in each aligned block of 104 rows (0 to 103, 104 to 207, ...) at most 2 rows name the same one
- slot: int32 [13312], P(('fluid', 'solid')), may hold values from 0 to 7
- shell_inverse: bfloat16 [1024, 768, 768], P(('fluid', 'solid')), may hold values from -0.0078125 to 0.0078125
- robin_coef: float32 [1024, 768], P(('fluid', 'solid')), may hold values from 1 to 27
- shell_start: float32 [1024, 768], P(('fluid', 'solid')), may hold values from -3 to 3
Outputs:
- shell_displacement: float32 [1024, 768], P(('fluid', 'solid'))
- fluid_load: bfloat16 [13312, 768], P(('fluid', 'solid'))
- residual_norms: float32 [6], replicated
Inputs may be any that keep to these rules, and one draw needn't show every extreme that they name: `route`: among the 104 blocks of one device at most 2 name the same owner device.
All inputs are finite; a program needn't handle non-finite values.
Results may differ from a plain program's by a relative error of at most 0.009.
Values may be sent and summed in bfloat16 or wider, within the bound.
No kernel may reach another device: no remote copies, remote signals or barrier semaphores. Data moves between devices by JAX's collectives and lax.ppermute only.
A program may use at most 128 MiB of HBM per device.

v0:
```python
import jax
import jax.numpy as jnp
from jax import lax
from jax.sharding import Mesh
from jax.sharding import PartitionSpec as P

ITERS = 6
FLUID_SOLID = ("fluid_0", "fluid_1", "fluid_2", "solid")
FLUID = ("fluid_0", "fluid_1", "fluid_2")


RELAX = 0.3
EPSILON = 1e-06


def over_axes(array, axes):
    for axis in axes:
        array = lax.psum(array, axis)
    return array


def transport(buffer, devices, capacity):
    breadth = buffer.shape[1]
    moved = lax.all_to_all(
        buffer.reshape(devices, capacity, breadth),
        FLUID_SOLID,
        split_axis=0,
        concat_axis=0,
        tiled=True,
    )
    return moved.reshape(devices * capacity, breadth)


def least_squares(gram, target_side):
    order = gram.shape[0]
    lower = [[None] * order for _ in range(order)]
    for row in range(order):
        for column in range(row + 1):
            total = gram[row, column]
            for inner in range(column):
                total = total - lower[row][inner] * lower[column][inner]
            if row == column:
                lower[row][row] = jnp.sqrt(total)
            else:
                lower[row][column] = total / lower[column][column]
    middle = []
    for row in range(order):
        total = target_side[row]
        for inner in range(row):
            total = total - lower[row][inner] * middle[inner]
        middle.append(total / lower[row][row])
    result = [None] * order
    for row in reversed(range(order)):
        total = middle[row]
        for inner in range(row + 1, order):
            total = total - lower[inner][row] * result[inner]
        result[row] = total / lower[row][row]
    return jnp.stack(result)


def per_device(
    rbf_blocks, fluid_traction, fluid_mass, route, slot, shell_inverse, robin_coef, shell_start
):
    devices = lax.axis_size(FLUID) * lax.axis_size("solid")
    blocks = rbf_blocks.shape[0]
    nodes = rbf_blocks.shape[1]
    breadth = 3 * nodes
    shells = shell_inverse.shape[0]
    capacity = max(2, 2 * blocks // devices)
    slots_all = devices * capacity
    destination = route[:, 0]
    block_order = jnp.arange(blocks, dtype=jnp.int32)
    earlier = (destination[:, None] == destination[None, :]) & (
        block_order[None, :] < block_order[:, None]
    )
    slot_rank = jnp.sum(earlier.astype(jnp.int32), axis=1)
    position = destination * capacity + slot_rank
    positions = jnp.arange(slots_all, dtype=jnp.int32)
    placing = positions[:, None] == position[None, :]
    place_out = placing.astype(jnp.bfloat16)
    place_in = (position[:, None] == positions[None, :]).astype(jnp.bfloat16)
    wanted = jnp.max(jnp.where(placing, slot[None, :] + 1, 0), axis=1) - 1
    asked = lax.all_to_all(
        wanted.reshape(devices, capacity), FLUID_SOLID, split_axis=0, concat_axis=0, tiled=True
    ).reshape(slots_all)
    shell_ids = jnp.arange(shells, dtype=jnp.int32)
    picking = (asked[:, None] == shell_ids[None, :]).astype(jnp.bfloat16)
    collecting = (shell_ids[:, None] == asked[None, :]).astype(jnp.bfloat16)
    traction = fluid_traction.astype(jnp.float32)
    massive = fluid_mass.astype(jnp.float32)
    count = shells * devices * breadth
    current = shell_start
    residuals = []
    images = []
    norms = []
    last_load = None
    for iteration in range(ITERS):
        current_half = current.astype(jnp.bfloat16)
        outgoing = jnp.dot(picking, current_half, preferred_element_type=jnp.float32).astype(
            jnp.bfloat16
        )
        incoming = transport(outgoing, devices, capacity)
        displaced = jnp.dot(place_in, incoming, preferred_element_type=jnp.float32).astype(
            jnp.bfloat16
        )
        moved = jnp.einsum(
            "bcj,bij->bci",
            displaced.reshape(blocks, 3, nodes),
            rbf_blocks,
            preferred_element_type=jnp.float32,
        ).reshape(blocks, breadth)
        load = (traction - massive * moved).astype(jnp.bfloat16)
        last_load = load
        mapped = (
            jnp.einsum(
                "bci,bij->bcj",
                load.reshape(blocks, 3, nodes),
                rbf_blocks,
                preferred_element_type=jnp.float32,
            )
            .reshape(blocks, breadth)
            .astype(jnp.bfloat16)
        )
        sending = jnp.dot(place_out, mapped, preferred_element_type=jnp.float32).astype(
            jnp.bfloat16
        )
        arrived = transport(sending, devices, capacity)
        shell_load = jnp.dot(collecting, arrived, preferred_element_type=jnp.float32)
        forcing = (shell_load + robin_coef * current).astype(jnp.bfloat16)
        image = jnp.einsum("bi,bij->bj", forcing, shell_inverse, preferred_element_type=jnp.float32)
        residual = image - current
        residuals.append(residual)
        images.append(image)
        squares_local = jnp.sum(residual * residual)
        if iteration == 0:
            gram_local = jnp.zeros((1, 1), jnp.float32)
            rhs_local = jnp.zeros((1,), jnp.float32)
        else:
            changes = jnp.stack(
                [(residuals[i + 1] - residuals[i]).reshape(-1) for i in range(iteration)]
            )
            gram_local = jnp.dot(changes, changes.T, precision=lax.Precision.HIGHEST)
            rhs_local = jnp.dot(changes, residual.reshape(-1), precision=lax.Precision.HIGHEST)
        gram, rhs, squares = (
            over_axes(gram_local, FLUID_SOLID),
            over_axes(rhs_local, FLUID_SOLID),
            over_axes(squares_local, FLUID_SOLID),
        )
        norms.append(jnp.sqrt(squares / count + EPSILON))
        if iteration == 0:
            current = current + RELAX * residual
        else:
            image_changes = jnp.stack([images[i + 1] - images[i] for i in range(iteration)])
            coefs = least_squares(gram, -rhs)
            current = image + jnp.tensordot(
                coefs, image_changes, axes=1, precision=lax.Precision.HIGHEST
            )
    return (current, last_load, jnp.stack(norms))


def solution(mesh):
    split = Mesh(
        mesh.devices.reshape(4, 4, 2, mesh.shape["solid"]),
        ("fluid_0", "fluid_1", "fluid_2", "solid"),
    )
    placed = (
        P(FLUID_SOLID, None, None),
        P(FLUID_SOLID, None),
        P(FLUID_SOLID, None),
        P(FLUID_SOLID, None),
        P(FLUID_SOLID),
        P(FLUID_SOLID, None, None),
        P(FLUID_SOLID, None),
        P(FLUID_SOLID, None),
    )
    return jax.shard_map(
        per_device,
        mesh=split,
        in_specs=placed,
        out_specs=(P(FLUID_SOLID, None), P(FLUID_SOLID, None), P()),
        check_vma=False,
    )
```

profile of v0, /device:TPU:1, one launch (start us, length us, event | category | flops | bytes accessed | tf_op | source)
XLA Modules:
  0.0 565.8 jit_solution(6310580616104771973)
XLA Ops:
  2.5 21.0 %all_to_all.66 = s32[128,1,2]{2,1,0:T(1,128)S(1)} all-to-all(s32[128,1,2]{2,1,0:T(1,128)S(1)} %bitcast.371), channel_id=1, replica_groups=mesh['fluid_0'=4,'fluid_1'=4,'fluid_2'=2,'solid'=4] {'fluid_0','fluid_1'..., dimensions={0} | all-to-all | bytes 2048 | tf_op jit(solution)/shard_map/all_to_all | solution.py:83
  34.0 9.7 %all-to-all-done.1 = bf16[128,2,768]{2,1,0:T(2,128)(2,1)S(1)} async-done(((bf16[128,2,768]{2,1,0:T(2,128)(2,1)}), bf16[128,2,768]{2,1,0:T(2,128)(2,1)S(1)}, u32[]{:S(2)}, u32[]{:S(2)}) %all-to-all-start.1) | async-done | bytes 393248 | tf_op jit(solution)/shard_map/all_to_all | solution.py:24
  44.5 8.5 %fusion.118 = f32[104,3,256]{2,1,0:T(4,128)S(1)} fusion(bf16[104,3,256]{2,1,0:T(4,128)(2,1)S(1)} %copy.82, bf16[104,256,256]{2,1,0:T(8,128)(2,1)} %param.8), kind=kOutput, calls=%fused_computation.215 | convolution fusion | flops 40894464 | bytes 14110720 | tf_op jit(solution)/shard_map/bcj,bij->bci/dot_general | solution.py:106
  53.5 6.7 %convolution_convert_fusion.17 = bf16[104,3,256]{2,1,0:T(4,128)(2,1)S(1)} fusion(bf16[104,3,256]{2,1,0:T(4,128)(2,1)S(1)} %copy.84, bf16[104,256,256]{2,1,0:T(8,128)(2,1)} %param.8), kind=kOutput, calls=%fused_computation.17 | convolution fusion | flops 40974336 | bytes 13950976 | tf_op jit(solution)/shard_map/bci,bij->bcj/dot_general | solution.py:115
  60.9 16.5 %all_to_all.67 = bf16[128,2,768]{2,1,0:T(2,128)(2,1)S(1)} all-to-all(bf16[128,2,768]{2,1,0:T(2,128)(2,1)S(1)} %reshape.214), channel_id=1, replica_groups=mesh['fluid_0'=4,'fluid_1'=4,'fluid_2'=2,'solid'=4] {'fluid_0','fluid_1'..., dimensions={0} | all-to-all | bytes 786432 | tf_op jit(solution)/shard_map/all_to_all | solution.py:24
  77.8 5.0 fusion.65
  83.3 16.7 %all_to_all.68 = bf16[128,2,768]{2,1,0:T(2,128)(2,1)S(1)} all-to-all(bf16[128,2,768]{2,1,0:T(2,128)(2,1)S(1)} %reshape.216), channel_id=1, replica_groups=mesh['fluid_0'=4,'fluid_1'=4,'fluid_2'=2,'solid'=4] {'fluid_0','fluid_1'..., dimensions={0} | all-to-all | bytes 786432 | tf_op jit(solution)/shard_map/all_to_all | solution.py:24
  100.8 8.5 %fusion.119 = f32[104,3,256]{2,1,0:T(4,128)S(1)} fusion(bf16[104,3,256]{2,1,0:T(4,128)(2,1)S(1)} %copy.87, bf16[104,256,256]{2,1,0:T(8,128)(2,1)} %param.8), kind=kOutput, calls=%fused_computation.216 | convolution fusion | flops 40894464 | bytes 14110720 | tf_op jit(solution)/shard_map/bcj,bij->bci/dot_general | solution.py:106
  109.7 6.7 %convolution_convert_fusion.16 = bf16[104,3,256]{2,1,0:T(4,128)(2,1)S(1)} fusion(bf16[104,3,256]{2,1,0:T(4,128)(2,1)S(1)} %copy.89, bf16[104,256,256]{2,1,0:T(8,128)(2,1)} %param.8), kind=kOutput, calls=%fused_computation.16 | convolution fusion | flops 40974336 | bytes 13950976 | tf_op jit(solution)/shard_map/bci,bij->bcj/dot_general | solution.py:115
  117.2 16.5 %all_to_all.69 = bf16[128,2,768]{2,1,0:T(2,128)(2,1)S(1)} all-to-all(bf16[128,2,768]{2,1,0:T(2,128)(2,1)S(1)} %reshape.221), channel_id=1, replica_groups=mesh['fluid_0'=4,'fluid_1'=4,'fluid_2'=2,'solid'=4] {'fluid_0','fluid_1'..., dimensions={0} | all-to-all | bytes 786432 | tf_op jit(solution)/shard_map/all_to_all | solution.py:24
  134.0 5.0 fusion.63
  139.7 7.5 %all-reduce.14 = (f32[1]{0:T(128)}, f32[1,1]{1,0:T(1,128)}) all-reduce(f32[1]{0:T(128)} %bitcast.16, f32[1,1]{1,0:T(1,128)} %bitcast.18), channel_id=1, replica_groups=mesh['fluid_0'=4,'fluid_1'=4,'fluid_2'=2,'solid'=4] {'fluid_0'}, use_global_device_ids=true, to_apply=%region_2.3 | all-reduce | flops 2 | bytes 16 | tf_op jit(solution)/shard_map/psum | solution.py:18
  147.2 6.9 %all-reduce.9 = (f32[1]{0:T(128)}, f32[1,1]{1,0:T(1,128)}) all-reduce(f32[1]{0:T(128)} %get-tuple-element.62, f32[1,1]{1,0:T(1,128)} %get-tuple-element.63), channel_id=1, replica_groups=mesh['fluid_0'=4,'fluid_1'=4,'fluid_2'=2,'solid'=4] {'fluid_1'}, use_global_device_ids=true, to_apply=%region_3.4 | all-reduce | flops 2 | bytes 16 | tf_op jit(solution)/shard_map/psum | solution.py:18
  154.1 7.8 %all-reduce.19 = (f32[1]{0:T(128)}, f32[1,1]{1,0:T(1,128)}) all-reduce(f32[1]{0:T(128)} %get-tuple-element.46, f32[1,1]{1,0:T(1,128)} %get-tuple-element.47), channel_id=1, replica_groups=mesh['fluid_0'=4,'fluid_1'=4,'fluid_2'=2,'solid'=4] {'fluid_2'}, use_global_device_ids=true, to_apply=%region_4.5 | all-reduce | flops 2 | bytes 16 | tf_op jit(solution)/shard_map/psum | solution.py:18
  162.0 7.2 %all-reduce.4 = (f32[1]{0:T(128)}, f32[1,1]{1,0:T(1,128)}) all-reduce(f32[1]{0:T(128)} %get-tuple-element.78, f32[1,1]{1,0:T(1,128)} %get-tuple-element.79), channel_id=1, replica_groups=mesh['fluid_0'=4,'fluid_1'=4,'fluid_2'=2,'solid'=4] {'solid'}, use_global_device_ids=true, to_apply=%region_5.6 | all-reduce | flops 2 | bytes 16 | tf_op jit(solution)/shard_map/psum | solution.py:18
  171.0 18.2 %all_to_all.70 = bf16[128,2,768]{2,1,0:T(2,128)(2,1)S(1)} all-to-all(bf16[128,2,768]{2,1,0:T(2,128)(2,1)S(1)} %reshape.224), channel_id=1, replica_groups=mesh['fluid_0'=4,'fluid_1'=4,'fluid_2'=2,'solid'=4] {'fluid_0','fluid_1'..., dimensions={0} | all-to-all | bytes 786432 | tf_op jit(solution)/shard_map/all_to_all | solution.py:24
  190.0 8.5 %fusion.120 = f32[104,3,256]{2,1,0:T(4,128)S(1)} fusion(bf16[104,3,256]{2,1,0:T(4,128)(2,1)S(1)} %copy.92, bf16[104,256,256]{2,1,0:T(8,128)(2,1)} %param.8), kind=kOutput, calls=%fused_computation.217 | convolution fusion | flops 40894464 | bytes 14110720 | tf_op jit(solution)/shard_map/bcj,bij->bci/dot_general | solution.py:106
  199.0 6.7 %convolution_convert_fusion.15 = bf16[104,3,256]{2,1,0:T(4,128)(2,1)S(1)} fusion(bf16[104,3,256]{2,1,0:T(4,128)(2,1)S(1)} %copy.94, bf16[104,256,256]{2,1,0:T(8,128)(2,1)} %param.8), kind=kOutput, calls=%fused_computation.15 | convolution fusion | flops 40974336 | bytes 13950976 | tf_op jit(solution)/shard_map/bci,bij->bcj/dot_general | solution.py:115
  211.3 12.5 %all-to-all-done.6 = bf16[128,2,768]{2,1,0:T(2,128)(2,1)S(1)} async-done(((bf16[128,2,768]{2,1,0:T(2,128)(2,1)}), bf16[128,2,768]{2,1,0:T(2,128)(2,1)S(1)}, u32[]{:S(2)}, u32[]{:S(2)}) %all-to-all-start.6) | async-done | bytes 393248 | tf_op jit(solution)/shard_map/all_to_all | solution.py:24
  231.0 6.9 %all-reduce.13 = (f32[2]{0:T(128)S(1)}, f32[2,2]{1,0:T(2,128)S(1)}) all-reduce(f32[2]{0:T(128)S(1)} %convolution_bitcast_fusion.3, f32[2,2]{1,0:T(2,128)S(1)} %fusion.69), channel_id=1, replica_groups=mesh['fluid_0'=4,'fluid_1'=4,'fluid_2'=2,'solid'=4] {'fluid_0'}, use_global_device_ids=true, to_apply=%region_10.11 | all-reduce | flops 6 | bytes 48 | tf_op jit(solution)/shard_map/psum | solution.py:18
  237.9 6.3 %all-reduce.8 = (f32[2]{0:T(128)S(1)}, f32[2,2]{1,0:T(2,128)S(1)}) all-reduce(f32[2]{0:T(128)S(1)} %get-tuple-element.60, f32[2,2]{1,0:T(2,128)S(1)} %get-tuple-element.61), channel_id=1, replica_groups=mesh['fluid_0'=4,'fluid_1'=4,'fluid_2'=2,'solid'=4] {'fluid_1'}, use_global_device_ids=true, to_apply=%region_11.12 | all-reduce | flops 6 | bytes 48 | tf_op jit(solution)/shard_map/psum | solution.py:18
  244.1 7.2 %all-reduce.18 = (f32[2]{0:T(128)S(1)}, f32[2,2]{1,0:T(2,128)S(1)}) all-reduce(f32[2]{0:T(128)S(1)} %get-tuple-element.44, f32[2,2]{1,0:T(2,128)S(1)} %get-tuple-element.45), channel_id=1, replica_groups=mesh['fluid_0'=4,'fluid_1'=4,'fluid_2'=2,'solid'=4] {'fluid_2'}, use_global_device_ids=true, to_apply=%region_12.13 | all-reduce | flops 6 | bytes 48 | tf_op jit(solution)/shard_map/psum | solution.py:18
  251.3 6.5 %all-reduce.3 = (f32[2]{0:T(128)S(1)}, f32[2,2]{1,0:T(2,128)S(1)}) all-reduce(f32[2]{0:T(128)S(1)} %get-tuple-element.76, f32[2,2]{1,0:T(2,128)S(1)} %get-tuple-element.77), channel_id=1, replica_groups=mesh['fluid_0'=4,'fluid_1'=4,'fluid_2'=2,'solid'=4] {'solid'}, use_global_device_ids=true, to_apply=%region_13.14 | all-reduce | flops 6 | bytes 48 | tf_op jit(solution)/shard_map/psum | solution.py:18
  263.4 18.0 %all_to_all.71 = bf16[128,2,768]{2,1,0:T(2,128)(2,1)S(1)} all-to-all(bf16[128,2,768]{2,1,0:T(2,128)(2,1)S(1)} %reshape.232), channel_id=1, replica_groups=mesh['fluid_0'=4,'fluid_1'=4,'fluid_2'=2,'solid'=4] {'fluid_0','fluid_1'..., dimensions={0} | all-to-all | bytes 786432 | tf_op jit(solution)/shard_map/all_to_all | solution.py:24
  282.1 8.5 %fusion.121 = f32[104,3,256]{2,1,0:T(4,128)S(1)} fusion(bf16[104,3,256]{2,1,0:T(4,128)(2,1)S(1)} %copy.97, bf16[104,256,256]{2,1,0:T(8,128)(2,1)} %param.8), kind=kOutput, calls=%fused_computation.218 | convolution fusion | flops 40894464 | bytes 14110720 | tf_op jit(solution)/shard_map/bcj,bij->bci/dot_general | solution.py:106
  291.1 6.7 %convolution_convert_fusion.14 = bf16[104,3,256]{2,1,0:T(4,128)(2,1)S(1)} fusion(bf16[104,3,256]{2,1,0:T(4,128)(2,1)S(1)} %copy.99, bf16[104,256,256]{2,1,0:T(8,128)(2,1)} %param.8), kind=kOutput, calls=%fused_computation.14 | convolution fusion | flops 40974336 | bytes 13950976 | tf_op jit(solution)/shard_map/bci,bij->bcj/dot_general | solution.py:115
  298.6 16.5 %all_to_all.72 = bf16[128,2,768]{2,1,0:T(2,128)(2,1)S(1)} all-to-all(bf16[128,2,768]{2,1,0:T(2,128)(2,1)S(1)} %reshape.237), channel_id=1, replica_groups=mesh['fluid_0'=4,'fluid_1'=4,'fluid_2'=2,'solid'=4] {'fluid_0','fluid_1'..., dimensions={0} | all-to-all | bytes 786432 | tf_op jit(solution)/shard_map/all_to_all | solution.py:24
  315.4 5.0 fusion.59
  322.2 6.9 %all-reduce.12 = (f32[3]{0:T(128)S(1)}, f32[3,3]{1,0:T(4,128)S(1)}) all-reduce(f32[3]{0:T(128)S(1)} %convolution_bitcast_fusion.2, f32[3,3]{1,0:T(4,128)S(1)} %fusion.49), channel_id=1, replica_groups=mesh['fluid_0'=4,'fluid_1'=4,'fluid_2'=2,'solid'=4] {'fluid_0'}, use_global_device_ids=true, to_apply=%region_18.19 | all-reduce | flops 12 | bytes 96 | tf_op jit(solution)/shard_map/psum | solution.py:18
  329.0 6.3 %all-reduce.7 = (f32[3]{0:T(128)S(1)}, f32[3,3]{1,0:T(4,128)S(1)}) all-reduce(f32[3]{0:T(128)S(1)} %get-tuple-element.58, f32[3,3]{1,0:T(4,128)S(1)} %get-tuple-element.59), channel_id=1, replica_groups=mesh['fluid_0'=4,'fluid_1'=4,'fluid_2'=2,'solid'=4] {'fluid_1'}, use_global_device_ids=true, to_apply=%region_19.20 | all-reduce | flops 12 | bytes 96 | tf_op jit(solution)/shard_map/psum | solution.py:18
  335.3 7.2 %all-reduce.17 = (f32[3]{0:T(128)S(1)}, f32[3,3]{1,0:T(4,128)S(1)}) all-reduce(f32[3]{0:T(128)S(1)} %get-tuple-element.42, f32[3,3]{1,0:T(4,128)S(1)} %get-tuple-element.43), channel_id=1, replica_groups=mesh['fluid_0'=4,'fluid_1'=4,'fluid_2'=2,'solid'=4] {'fluid_2'}, use_global_device_ids=true, to_apply=%region_20.21 | all-reduce | flops 12 | bytes 96 | tf_op jit(solution)/shard_map/psum | solution.py:18
  342.5 6.5 %all-reduce.2 = (f32[3]{0:T(128)S(1)}, f32[3,3]{1,0:T(4,128)S(1)}) all-reduce(f32[3]{0:T(128)S(1)} %get-tuple-element.74, f32[3,3]{1,0:T(4,128)S(1)} %get-tuple-element.75), channel_id=1, replica_groups=mesh['fluid_0'=4,'fluid_1'=4,'fluid_2'=2,'solid'=4] {'solid'}, use_global_device_ids=true, to_apply=%region_21.22 | all-reduce | flops 12 | bytes 96 | tf_op jit(solution)/shard_map/psum | solution.py:18
  357.3 18.0 %all_to_all.73 = bf16[128,2,768]{2,1,0:T(2,128)(2,1)S(1)} all-to-all(bf16[128,2,768]{2,1,0:T(2,128)(2,1)S(1)} %reshape.240), channel_id=1, replica_groups=mesh['fluid_0'=4,'fluid_1'=4,'fluid_2'=2,'solid'=4] {'fluid_0','fluid_1'..., dimensions={0} | all-to-all | bytes 786432 | tf_op jit(solution)/shard_map/all_to_all | solution.py:24
  376.1 8.5 %fusion.122 = f32[104,3,256]{2,1,0:T(4,128)S(1)} fusion(bf16[104,3,256]{2,1,0:T(4,128)(2,1)S(1)} %copy.102, bf16[104,256,256]{2,1,0:T(8,128)(2,1)} %param.8), kind=kOutput, calls=%fused_computation.219 | convolution fusion | flops 40894464 | bytes 14110720 | tf_op jit(solution)/shard_map/bcj,bij->bci/dot_general | solution.py:106
  385.1 6.7 %convolution_convert_fusion.13 = bf16[104,3,256]{2,1,0:T(4,128)(2,1)S(1)} fusion(bf16[104,3,256]{2,1,0:T(4,128)(2,1)S(1)} %copy.104, bf16[104,256,256]{2,1,0:T(8,128)(2,1)} %param.8), kind=kOutput, calls=%fused_computation.13 | convolution fusion | flops 40974336 | bytes 13950976 | tf_op jit(solution)/shard_map/bci,bij->bcj/dot_general | solution.py:115
  392.6 16.5 %all_to_all.74 = bf16[128,2,768]{2,1,0:T(2,128)(2,1)S(1)} all-to-all(bf16[128,2,768]{2,1,0:T(2,128)(2,1)S(1)} %reshape.245), channel_id=1, replica_groups=mesh['fluid_0'=4,'fluid_1'=4,'fluid_2'=2,'solid'=4] {'fluid_0','fluid_1'..., dimensions={0} | all-to-all | bytes 786432 | tf_op jit(solution)/shard_map/all_to_all | solution.py:24
  416.3 6.9 %all-reduce.11 = (f32[4]{0:T(128)S(1)}, f32[4,4]{1,0:T(4,128)S(1)}) all-reduce(f32[4]{0:T(128)S(1)} %convolution_bitcast_fusion.1, f32[4,4]{1,0:T(4,128)S(1)} %fusion.68), channel_id=1, replica_groups=mesh['fluid_0'=4,'fluid_1'=4,'fluid_2'=2,'solid'=4] {'fluid_0'}, use_global_device_ids=true, to_apply=%region_26.27 | all-reduce | flops 20 | bytes 160 | tf_op jit(solution)/shard_map/psum | solution.py:18
  423.1 6.3 %all-reduce.6 = (f32[4]{0:T(128)S(1)}, f32[4,4]{1,0:T(4,128)S(1)}) all-reduce(f32[4]{0:T(128)S(1)} %get-tuple-element.56, f32[4,4]{1,0:T(4,128)S(1)} %get-tuple-element.57), channel_id=1, replica_groups=mesh['fluid_0'=4,'fluid_1'=4,'fluid_2'=2,'solid'=4] {'fluid_1'}, use_global_device_ids=true, to_apply=%region_27.28 | all-reduce | flops 20 | bytes 160 | tf_op jit(solution)/shard_map/psum | solution.py:18
  429.4 7.2 %all-reduce.16 = (f32[4]{0:T(128)S(1)}, f32[4,4]{1,0:T(4,128)S(1)}) all-reduce(f32[4]{0:T(128)S(1)} %get-tuple-element.40, f32[4,4]{1,0:T(4,128)S(1)} %get-tuple-element.41), channel_id=1, replica_groups=mesh['fluid_0'=4,'fluid_1'=4,'fluid_2'=2,'solid'=4] {'fluid_2'}, use_global_device_ids=true, to_apply=%region_28.29 | all-reduce | flops 20 | bytes 160 | tf_op jit(solution)/shard_map/psum | solution.py:18
  436.6 6.5 %all-reduce.1 = (f32[4]{0:T(128)S(1)}, f32[4,4]{1,0:T(4,128)S(1)}) all-reduce(f32[4]{0:T(128)S(1)} %get-tuple-element.72, f32[4,4]{1,0:T(4,128)S(1)} %get-tuple-element.73), channel_id=1, replica_groups=mesh['fluid_0'=4,'fluid_1'=4,'fluid_2'=2,'solid'=4] {'solid'}, use_global_device_ids=true, to_apply=%region_29.30 | all-reduce | flops 20 | bytes 160 | tf_op jit(solution)/shard_map/psum | solution.py:18
  454.8 18.1 %all_to_all.75 = bf16[128,2,768]{2,1,0:T(2,128)(2,1)S(1)} all-to-all(bf16[128,2,768]{2,1,0:T(2,128)(2,1)S(1)} %reshape.248), channel_id=1, replica_groups=mesh['fluid_0'=4,'fluid_1'=4,'fluid_2'=2,'solid'=4] {'fluid_0','fluid_1'..., dimensions={0} | all-to-all | bytes 786432 | tf_op jit(solution)/shard_map/all_to_all | solution.py:24
  473.6 8.5 %fusion.123 = f32[104,3,256]{2,1,0:T(4,128)S(1)} fusion(bf16[104,3,256]{2,1,0:T(4,128)(2,1)S(1)} %copy.107, bf16[104,256,256]{2,1,0:T(8,128)(2,1)} %param.8), kind=kOutput, calls=%fused_computation.220 | convolution fusion | flops 40894464 | bytes 14110720 | tf_op jit(solution)/shard_map/bcj,bij->bci/dot_general | solution.py:106
  482.6 6.7 %convolution_convert_fusion.12 = bf16[104,3,256]{2,1,0:T(4,128)(2,1)S(1)} fusion(bf16[104,3,256]{2,1,0:T(4,128)(2,1)S(1)} %copy.109, bf16[104,256,256]{2,1,0:T(8,128)(2,1)} %param.8), kind=kOutput, calls=%fused_computation.12 | convolution fusion | flops 40974336 | bytes 13950976 | tf_op jit(solution)/shard_map/bci,bij->bcj/dot_general | solution.py:115
  495.7 11.8 %all-to-all-done.12 = bf16[128,2,768]{2,1,0:T(2,128)(2,1)S(1)} async-done(((bf16[128,2,768]{2,1,0:T(2,128)(2,1)}), bf16[128,2,768]{2,1,0:T(2,128)(2,1)S(1)}, u32[]{:S(2)}, u32[]{:S(2)}) %all-to-all-start.12) | async-done | bytes 393248 | tf_op jit(solution)/shard_map/all_to_all | solution.py:24
  514.8 7.7 %all-reduce.10 = (f32[5]{0:T(128)S(1)}, f32[5,5]{1,0:T(8,128)S(1)}, f32[]{:T(128)}, f32[]{:T(128)}, f32[]{:T(128)}, /*index=5*/f32[]{:T(128)}, f32[]{:T(128)}, f32[]{:T(128)}) all-reduce(f32[5]{0:T(128)S(1)} %convolution_bitcast_fusion, ...), channel_id=1, replica_groups=mesh['fluid_0'=4,'fluid_1'=4,'fluid_2'=2,'solid'=4] {'fluid_0'}, use_global_device_ids=true, to_apply=%region_34.35 | all-reduce | flops 36 | bytes 288 | tf_op jit(solution)/shard_map/psum | solution.py:18
  522.5 7.1 %all-reduce.5 = (f32[5]{0:T(128)S(1)}, f32[5,5]{1,0:T(8,128)S(1)}, f32[]{:T(128)}, f32[]{:T(128)}, f32[]{:T(128)}, /*index=5*/f32[]{:T(128)}, f32[]{:T(128)}, f32[]{:T(128)}) all-reduce(f32[5]{0:T(128)S(1)} %get-tuple-element.48, ...), channel_id=1, replica_groups=mesh['fluid_0'=4,'fluid_1'=4,'fluid_2'=2,'solid'=4] {'fluid_1'}, use_global_device_ids=true, to_apply=%region_35.36 | all-reduce | flops 36 | bytes 288 | tf_op jit(solution)/shard_map/psum | solution.py:18
  529.6 7.9 %all-reduce.15 = (f32[5]{0:T(128)S(1)}, f32[5,5]{1,0:T(8,128)S(1)}, f32[]{:T(128)}, f32[]{:T(128)}, f32[]{:T(128)}, /*index=5*/f32[]{:T(128)}, f32[]{:T(128)}, f32[]{:T(128)}) all-reduce(f32[5]{0:T(128)S(1)} %get-tuple-element.32, ...), channel_id=1, replica_groups=mesh['fluid_0'=4,'fluid_1'=4,'fluid_2'=2,'solid'=4] {'fluid_2'}, use_global_device_ids=true, to_apply=%region_36.37 | all-reduce | flops 36 | bytes 288 | tf_op jit(solution)/shard_map/psum | solution.py:18
  537.5 7.4 %all-reduce = (f32[5]{0:T(128)S(1)}, f32[5,5]{1,0:T(8,128)S(1)}, f32[]{:T(128)}, f32[]{:T(128)}, f32[]{:T(128)}, /*index=5*/f32[]{:T(128)}, f32[]{:T(128)}, f32[]{:T(128)}) all-reduce(f32[5]{0:T(128)S(1)} %get-tuple-element.64, ...), channel_id=1, replica_groups=mesh['fluid_0'=4,'fluid_1'=4,'fluid_2'=2,'solid'=4] {'solid'}, use_global_device_ids=true, to_apply=%region_37.38 | all-reduce | flops 36 | bytes 288 | tf_op jit(solution)/shard_map/psum | solution.py:18
  (163 shorter events, 69.8 us)
Async XLA Ops:
  26.9 16.8 %all-to-all-start.1 = ((bf16[128,2,768]{2,1,0:T(2,128)(2,1)}), bf16[128,2,768]{2,1,0:T(2,128)(2,1)S(1)}, u32[]{:S(2)}, u32[]{:S(2)}) async-start(bf16[128,2,768]{2,1,0:T(2,128)(2,1)} %reshape.209), calls=%async_computation.1 | async-start | bytes 786432 | tf_op jit(solution)/shard_map/all_to_all | solution.py:24
  53.2 24.4 %copy-start = (f32[8,768]{1,0:T(8,128)S(1)}, f32[8,768]{1,0:T(8,128)}, u32[]{:S(2)}) copy-start(f32[8,768]{1,0:T(8,128)} %param.14) | copy-start | bytes 73732
  53.2 24.4 %copy-start.1 = (f32[8,768]{1,0:T(8,128)S(1)}, f32[8,768]{1,0:T(8,128)}, u32[]{:S(2)}) copy-start(f32[8,768]{1,0:T(8,128)} %param.15) | copy-start | bytes 73732
  207.2 16.7 %all-to-all-start.6 = ((bf16[128,2,768]{2,1,0:T(2,128)(2,1)}), bf16[128,2,768]{2,1,0:T(2,128)(2,1)S(1)}, u32[]{:S(2)}, u32[]{:S(2)}) async-start(bf16[128,2,768]{2,1,0:T(2,128)(2,1)} %reshape.229), calls=%async_computation.6 | async-start | bytes 786432 | tf_op jit(solution)/shard_map/all_to_all | solution.py:24
  490.8 16.7 %all-to-all-start.12 = ((bf16[128,2,768]{2,1,0:T(2,128)(2,1)}), bf16[128,2,768]{2,1,0:T(2,128)(2,1)S(1)}, u32[]{:S(2)}, u32[]{:S(2)}) async-start(bf16[128,2,768]{2,1,0:T(2,128)(2,1)} %reshape.253), calls=%async_computation.12 | async-start | bytes 786432 | tf_op jit(solution)/shard_map/all_to_all | solution.py:24
where the time goes:
time: 576 us; the launch traced here: 566 us
  blocking collectives  316 us (55%)
  matrix products  134 us (23%)
  between operations  39.4 us (7%)
  waiting for transfers between devices  34 us (6%)
  local copies, waits for them, and re-layouts  21.6 us (4%)
  starting transfers between devices  12.5 us (2%)
  other arithmetic  7.59 us (1%)
    all_to_all x9, blocking collectives, transport(): lax.all_to_all(buffer.reshape(devices, capacity, breadth), FLUID_SOLID, s...  155 us
    psum x20, blocking collectives, over_axes(): array = lax.psum(array, axis)  140 us
    dot_general x6, matrix products, per_device(): jnp.einsum('bcj,bij->bci', displaced.reshape(blocks, 3, nodes), rbf_block...  50.9 us
    dot_general x6, matrix products, per_device(): jnp.einsum('bci,bij->bcj', load.reshape(blocks, 3, nodes), rbf_blocks, pr...  40.5 us
    all_to_all x3, waiting for transfers between devices, transport(): lax.all_to_all(buffer.reshape(devices, capacity, breadth), FLUID_SOLID, s...  34 us
    dot_general x6, matrix products, per_device(): jnp.einsum('bi,bij->bj', forcing, shell_inverse, preferred_element_type=j...  30.1 us
    all_to_all x1, blocking collectives, per_device(): lax.all_to_all(wanted.reshape(devices, capacity), FLUID_SOLID, split_axis...  21 us
    all_to_all x3, starting transfers between devices, transport(): lax.all_to_all(buffer.reshape(devices, capacity, breadth), FLUID_SOLID, s...  12.5 us
  transfers between devices with their start and end apart: 3, of which 3 were waited for; matrix products, arithmetic and copies ran while one was open for 1% of the time, Pallas kernels for 0%

commit v1 on v0

v1 whole, which is shorter than its diff:
```python
import jax
import jax.numpy as jnp
from jax import lax
from jax.experimental import pallas as pl
from jax.experimental.pallas import tpu as pltpu
from jax.sharding import Mesh
from jax.sharding import PartitionSpec as P

ITERS = 6
FLUID_SOLID = ("fluid_0", "fluid_1", "fluid_2", "solid")
FLUID = ("fluid_0", "fluid_1", "fluid_2")

RELAX = 0.3
EPSILON = 1e-06

LANES = 128
RHS_AT = 5
SQUARES_AT = 10
PIECE = 32
ROWS = 16


def least_squares(gram, target_side):
    order = len(target_side)
    lower = [[None] * order for _ in range(order)]
    for row in range(order):
        for column in range(row + 1):
            total = gram[row][column]
            for inner in range(column):
                total = total - lower[row][inner] * lower[column][inner]
            if row == column:
                lower[row][row] = jnp.sqrt(total)
            else:
                lower[row][column] = total / lower[column][column]
    middle = []
    for row in range(order):
        total = target_side[row]
        for inner in range(row):
            total = total - lower[row][inner] * middle[inner]
        middle.append(total / lower[row][row])
    result = [None] * order
    for row in reversed(range(order)):
        total = middle[row]
        for inner in range(row + 1, order):
            total = total - lower[inner][row] * result[inner]
        result[row] = total / lower[row][row]
    return result


def spread_sums(line):
    whole = line + pltpu.roll(line, LANES - PIECE, 1) + pltpu.roll(line, LANES - 2 * PIECE, 1)
    row = lax.broadcasted_iota(jnp.int32, (ROWS, LANES), 0)
    lane = lax.broadcasted_iota(jnp.int32, (ROWS, LANES), 1)
    picked = jnp.where(row == lane, jnp.broadcast_to(whole, (ROWS, LANES)), 0.0)
    return jnp.broadcast_to(jnp.sum(picked, axis=1, keepdims=True), (ROWS, LANES))


def solve_coefficients(sums):
    order = len(sums)
    gram = [[sums[row][column : column + 1] for column in range(row + 1)] for row in range(order)]
    target_side = [-sums[-1][RHS_AT + i : RHS_AT + i + 1] for i in range(order)]
    return least_squares(gram, target_side)


def lane_chunks(breadth):
    return [slice(at, at + LANES) for at in range(0, breadth, LANES)]


def fluid_call(
    step_index, incoming, base, changes, sums, rbf_blocks, traction, massive, group, last
):
    blocks, nodes, _ = rbf_blocks.shape
    breadth = 3 * nodes
    steps = blocks // group
    halves = nodes // LANES
    n_changes = len(changes)
    n_sums = len(sums)
    solving = step_index >= 2
    keep = 0 < step_index < ITERS - 1

    def body(*refs):
        refs = list(refs)
        incoming_ref = refs.pop(0)
        base_ref = refs.pop(0) if step_index else None
        change_refs = [refs.pop(0) for _ in range(n_changes)]
        sum_refs = [refs.pop(0) for _ in range(n_sums)]
        rbf_ref, traction_ref, mass_ref = refs.pop(0), refs.pop(0), refs.pop(0)
        mapped_ref = refs.pop(0)
        load_ref = refs.pop(0) if last else None
        base_out = refs.pop(0) if keep else None
        sums_out = refs.pop(0) if step_index else None
        coefs_out = refs.pop(0) if step_index else None
        spread_ref, result_ref = refs.pop(0), refs.pop(0)
        kept_ref = refs.pop(0) if last else None
        step = pl.program_id(0)

        @pl.when(step == 0)
        def _():
            spread_ref[...] = jnp.zeros_like(spread_ref)
            coefs = []
            if step_index:
                fresh = spread_sums(incoming_ref[blocks : blocks + 1, breadth : breadth + LANES])
                sums_out[...] = fresh
                coefs_out[...] = jnp.zeros_like(coefs_out)
                if solving:
                    coefs = solve_coefficients([ref[...] for ref in sum_refs] + [fresh])
                    for i, coef in enumerate(coefs):
                        coefs_out[i : i + 1, :] = coef
            for at, cut in enumerate(lane_chunks(breadth)):
                change = incoming_ref[:blocks, cut]
                if step_index == 0:
                    shown = change
                elif step_index == 1:
                    shown = base_ref[:blocks, cut] + RELAX * change
                    base_out[:, cut] = base_ref[:blocks, cut] + change
                else:
                    run = base_ref[:blocks, cut] + change
                    if keep:
                        base_out[:, cut] = run
                    shown = run + coefs[-1] * change
                    for coef, ref in zip(coefs, change_refs):
                        shown = shown + coef * ref[:blocks, cut]
                component, half = divmod(at, halves)
                spread_ref[half, pl.ds(component, blocks, stride=8), :] = shown

        loads = []
        for block in range(group):
            rows = pl.ds(pl.multiple_of((step * group + block) * 8, 8), 8)
            shown = jnp.concatenate(
                [spread_ref[half, rows, :] for half in range(halves)], axis=1
            ).astype(jnp.bfloat16)
            moved = lax.dot_general(
                shown, rbf_ref[block], (((1,), (1,)), ((), ())), preferred_element_type=jnp.float32
            )
            here = slice(block * 8, block * 8 + 8)
            load = traction_ref[here, :] - mass_ref[here, :] * moved
            loads.append(load.astype(jnp.bfloat16))
        for block in range(group):
            rows = pl.ds(pl.multiple_of((step * group + block) * 8, 8), 8)
            result = jnp.dot(loads[block], rbf_ref[block], preferred_element_type=jnp.float32)
            for half in range(halves):
                lanes = slice(half * LANES, (half + 1) * LANES)
                result_ref[half, rows, :] = result[:, lanes]
                if last:
                    kept_ref[half, rows, :] = loads[block][:, lanes].astype(jnp.float32)

        @pl.when(step == steps - 1)
        def _():
            for at, cut in enumerate(lane_chunks(breadth)):
                component, half = divmod(at, halves)
                rows = pl.ds(component, blocks, stride=8)
                mapped_ref[:, cut] = result_ref[half, rows, :].astype(jnp.bfloat16)
                if last:
                    load_ref[:, cut] = kept_ref[half, rows, :].astype(jnp.bfloat16)

    def whole(array):
        return pl.BlockSpec(array.shape, lambda s: (0,) * array.ndim)

    small = [incoming] + ([base] if step_index else []) + list(changes) + list(sums)
    out_shape = [jax.ShapeDtypeStruct((blocks, breadth), jnp.bfloat16)]
    if last:
        out_shape.append(jax.ShapeDtypeStruct((blocks, breadth), jnp.bfloat16))
    if keep:
        out_shape.append(jax.ShapeDtypeStruct((blocks, breadth), jnp.float32))
    if step_index:
        out_shape += [jax.ShapeDtypeStruct((ROWS, LANES), jnp.float32)] * 2
    scratch = [pltpu.VMEM((halves, blocks * 8, LANES), jnp.float32)] * (3 if last else 2)
    out = pl.pallas_call(
        body,
        grid=(steps,),
        in_specs=[whole(a) for a in small]
        + [
            pl.BlockSpec((group, nodes, nodes), lambda s: (s, 0, 0)),
            pl.BlockSpec((group * 8, nodes), lambda s: (s, 0)),
            pl.BlockSpec((group * 8, nodes), lambda s: (s, 0)),
        ],
        out_specs=[whole(a) for a in out_shape],
        out_shape=out_shape,
        scratch_shapes=scratch,
        compiler_params=pltpu.CompilerParams(vmem_limit_bytes=24 * 2**20),
        name="fluid_side",
    )(*small, rbf_blocks, traction, massive)
    out = list(out)
    mapped = out.pop(0)
    load = out.pop(0) if last else None
    base_next = out.pop(0) if keep else None
    fresh, coefs = (out.pop(0), out.pop(0)) if step_index else (None, None)
    return mapped, load, base_next, fresh, coefs


def full_sum(array):
    return jnp.sum(jnp.sum(array, axis=0, keepdims=True), axis=1, keepdims=True)


def next_current(step_index, coef, current, residual, images, cut):
    if step_index == 1:
        return current[:, cut] + RELAX * residual[:, cut]
    moving = images[-1][:, cut]
    for i in range(len(images) - 1):
        moving = moving + coef[i : i + 1, :] * (images[i + 1][:, cut] - images[i][:, cut])
    return moving


def shell_call(step_index, loads, coefs, shown, residuals, images, start, robin_coef, shell_inverse):
    shells, breadth, _ = shell_inverse.shape
    history = step_index

    def body(*refs):
        refs = list(refs)
        load_ref = refs.pop(0)
        coef_ref = refs.pop(0) if step_index else None
        shown_ref = refs.pop(0)
        residual_refs = [refs.pop(0) for _ in range(history)]
        image_refs = [refs.pop(0) for _ in range(history)]
        start_ref, robin_ref, inverse_ref = refs.pop(0), refs.pop(0), refs.pop(0)
        message_ref, image_ref, residual_ref, run_ref = [refs.pop(0) for _ in range(4)]
        current_ref, forcing_ref = refs.pop(0), refs.pop(0)
        step = pl.program_id(0)

        @pl.when(step == 0)
        def _():
            for cut in lane_chunks(breadth):
                if step_index:
                    moving = next_current(
                        step_index,
                        coef_ref[...],
                        start_ref,
                        residual_refs[-1],
                        image_refs,
                        cut,
                    )
                else:
                    moving = start_ref[:, cut]
                current_ref[:, cut] = moving
                forcing_ref[:, cut] = load_ref[:, cut] + robin_ref[:, cut] * moving
            image_ref[...] = jnp.zeros_like(image_ref)

        product = jnp.dot(
            forcing_ref[...].astype(jnp.bfloat16),
            inverse_ref[0],
            preferred_element_type=jnp.float32,
        )
        mine = lax.broadcasted_iota(jnp.int32, (shells, breadth), 0) == step
        image_ref[...] = jnp.where(mine, product, image_ref[...])

        @pl.when(step == shells - 1)
        def _():
            image = image_ref[...]
            residual = image - current_ref[...]
            residual_ref[...] = residual
            lane = lax.broadcasted_iota(jnp.int32, (1, LANES), 1)
            line = jnp.where(lane == SQUARES_AT, full_sum(residual * residual), 0.0)
            if step_index:
                chain = [ref[...] for ref in residual_refs] + [residual]
                changes = [chain[i + 1] - chain[i] for i in range(step_index)]
                for i, change in enumerate(changes):
                    line = line + jnp.where(lane == i, full_sum(changes[-1] * change), 0.0)
                    line = line + jnp.where(
                        lane == RHS_AT + i, full_sum(change * residual), 0.0
                    )
            head = line.astype(jnp.bfloat16).astype(jnp.float32)
            rest = line - head
            middle = rest.astype(jnp.bfloat16).astype(jnp.float32)
            tail = (rest - middle).astype(jnp.bfloat16).astype(jnp.float32)
            pieces = head + pltpu.roll(middle, PIECE, 1) + pltpu.roll(tail, 2 * PIECE, 1)
            difference = (image - shown_ref[...]).astype(jnp.bfloat16)
            run_ref[...] = shown_ref[...] + difference.astype(jnp.float32)
            row = lax.broadcasted_iota(jnp.int32, (8, LANES), 0)
            lower = jnp.where(row == 0, jnp.broadcast_to(pieces, (8, LANES)), 0.0)
            zeros = jnp.zeros((8, breadth), jnp.float32)
            message_ref[:, :breadth] = jnp.concatenate(
                [difference.astype(jnp.float32), zeros], axis=0
            ).astype(jnp.bfloat16)
            message_ref[:, breadth:] = jnp.concatenate(
                [jnp.zeros((8, LANES), jnp.float32), lower], axis=0
            ).astype(jnp.bfloat16)

    def whole(array):
        return pl.BlockSpec(array.shape, lambda s: (0,) * array.ndim)

    small = (
        [loads]
        + ([coefs] if step_index else [])
        + [shown]
        + list(residuals)
        + list(images)
        + [start, robin_coef]
    )
    out_shape = [jax.ShapeDtypeStruct((ROWS, breadth + LANES), jnp.bfloat16)] + [
        jax.ShapeDtypeStruct((shells, breadth), jnp.float32)
    ] * 3
    return pl.pallas_call(
        body,
        grid=(shells,),
        in_specs=[whole(a) for a in small]
        + [pl.BlockSpec((1, breadth, breadth), lambda s: (s, 0, 0))],
        out_specs=[whole(a) for a in out_shape],
        out_shape=out_shape,
        scratch_shapes=[pltpu.VMEM((shells, breadth), jnp.float32)] * 2,
        compiler_params=pltpu.CompilerParams(vmem_limit_bytes=24 * 2**20),
        name="shell_side",
    )(*small, shell_inverse)


def closing_call(line, sums, images, count):
    shells, breadth = images[0].shape
    n_sums = len(sums)

    def body(*refs):
        refs = list(refs)
        line_ref = refs.pop(0)
        sum_refs = [refs.pop(0) for _ in range(n_sums)]
        image_refs = [refs.pop(0) for _ in range(len(images))]
        current_ref, norm_ref = refs
        fresh = spread_sums(line_ref[0:1, :])
        every = [ref[...] for ref in sum_refs] + [fresh]
        coefs = solve_coefficients(every[1:])
        for cut in lane_chunks(breadth):
            moving = image_refs[-1][:, cut]
            for i, coef in enumerate(coefs):
                moving = moving + coef * (image_refs[i + 1][:, cut] - image_refs[i][:, cut])
            current_ref[:, cut] = moving
        lane = lax.broadcasted_iota(jnp.int32, (1, LANES), 1)
        squares = jnp.zeros((1, LANES), jnp.float32)
        for i, part in enumerate(every):
            squares = jnp.where(lane == i, part[SQUARES_AT : SQUARES_AT + 1], squares)
        norm_ref[...] = jnp.sqrt(squares / count + EPSILON)

    return pl.pallas_call(
        body,
        out_shape=[
            jax.ShapeDtypeStruct((shells, breadth), jnp.float32),
            jax.ShapeDtypeStruct((1, LANES), jnp.float32),
        ],
        name="closing",
    )(line, *sums, *images)


def spread_components(array, blocks, nodes):
    wide = array.astype(jnp.float32).reshape(blocks, 3, nodes)
    return jnp.pad(wide, ((0, 0), (0, 5), (0, 0))).reshape(blocks * 8, nodes)


def per_device(
    rbf_blocks, fluid_traction, fluid_mass, route, slot, shell_inverse, robin_coef, shell_start
):
    devices = lax.axis_size(FLUID) * lax.axis_size("solid")
    blocks = rbf_blocks.shape[0]
    nodes = rbf_blocks.shape[1]
    breadth = 3 * nodes
    shells = shell_inverse.shape[0]
    capacity = max(2, 2 * blocks // devices)
    slots_all = devices * capacity
    count = shells * devices * breadth

    def transport(buffer):
        width = buffer.shape[1]
        moved = lax.all_to_all(
            buffer.reshape(devices, capacity, width),
            FLUID_SOLID,
            split_axis=0,
            concat_axis=0,
            tiled=True,
        )
        return moved.reshape(devices * capacity, width)

    destination = route[:, 0]
    block_order = jnp.arange(blocks, dtype=jnp.int32)
    earlier = (destination[:, None] == destination[None, :]) & (
        block_order[None, :] < block_order[:, None]
    )
    slot_rank = jnp.sum(earlier.astype(jnp.int32), axis=1)
    position = destination * capacity + slot_rank
    positions = jnp.arange(slots_all, dtype=jnp.int32)
    placing = positions[:, None] == position[None, :]
    place_out = placing.astype(jnp.bfloat16)
    place_in = (position[:, None] == positions[None, :]).astype(jnp.bfloat16)
    adding = (jnp.arange(8) == 0).astype(jnp.bfloat16) / capacity
    place_in = jnp.concatenate(
        [place_in, jnp.broadcast_to(adding[:, None], (8, slots_all)).astype(jnp.bfloat16)]
    )
    wanted = jnp.max(jnp.where(placing, slot[None, :] + 1, 0), axis=1) - 1
    asked = lax.all_to_all(
        wanted.reshape(devices, capacity), FLUID_SOLID, split_axis=0, concat_axis=0, tiled=True
    ).reshape(slots_all)
    shell_ids = jnp.arange(ROWS, dtype=jnp.int32)
    picking = (
        (asked[:, None] == shell_ids[None, :]) | (shell_ids[None, :] == shells)
    ).astype(jnp.bfloat16)
    collecting = (shell_ids[:shells, None] == asked[None, :]).astype(jnp.bfloat16)
    traction = spread_components(fluid_traction, blocks, nodes)
    massive = spread_components(fluid_mass, blocks, nodes)
    group = next(n for n in (8, 4, 2, 1) if blocks % n == 0)

    start_half = shell_start.astype(jnp.bfloat16)
    message = jnp.pad(start_half, ((0, ROWS - shells), (0, 0)))
    shown = start_half.astype(jnp.float32)
    base = None
    changes = []
    sums = []
    residuals = []
    images = []
    last_load = None
    for iteration in range(ITERS):
        outgoing = jnp.dot(picking, message, preferred_element_type=jnp.float32).astype(
            jnp.bfloat16
        )
        incoming = jnp.dot(
            place_in, transport(outgoing), preferred_element_type=jnp.float32
        )
        last = iteration == ITERS - 1
        mapped, load, base_next, fresh, coefs = fluid_call(
            iteration,
            incoming,
            base,
            changes[1:],
            sums[1:],
            rbf_blocks,
            traction,
            massive,
            group,
            last,
        )
        if iteration == 0:
            base = incoming
        else:
            changes.append(incoming)
            base = base_next
            sums.append(fresh)
        last_load = load
        sending = jnp.dot(place_out, mapped, preferred_element_type=jnp.float32).astype(
            jnp.bfloat16
        )
        arrived = transport(sending)
        shell_load = jnp.dot(collecting, arrived, preferred_element_type=jnp.float32)
        message, image, residual, shown = shell_call(
            iteration,
            shell_load,
            coefs,
            shown,
            residuals,
            images,
            shell_start,
            robin_coef,
            shell_inverse,
        )
        residuals.append(residual)
        images.append(image)
    ending = jnp.broadcast_to(
        message[shells : shells + 1, breadth:], (slots_all, LANES)
    )
    line = jnp.dot(place_in[blocks:], transport(ending), preferred_element_type=jnp.float32)
    current, norms = closing_call(line, sums, images, count)
    return (current, last_load, norms[0, :ITERS])


def solution(mesh):
    split = Mesh(
        mesh.devices.reshape(4, 4, 2, mesh.shape["solid"]),
        ("fluid_0", "fluid_1", "fluid_2", "solid"),
    )
    placed = (
        P(FLUID_SOLID, None, None),
        P(FLUID_SOLID, None),
        P(FLUID_SOLID, None),
        P(FLUID_SOLID, None),
        P(FLUID_SOLID),
        P(FLUID_SOLID, None, None),
        P(FLUID_SOLID, None),
        P(FLUID_SOLID, None),
    )
    return jax.shard_map(
        per_device,
        mesh=split,
        in_specs=placed,
        out_specs=(P(FLUID_SOLID, None), P(FLUID_SOLID, None), P()),
        check_vma=False,
    )
```

time: 576 us -> 419 us (0.73); the launches traced: 566 us -> 417 us
  blocking collectives: 316 us -> 204 us
  matrix products: 134 us -> 22.9 us
  local copies, waits for them, and re-layouts: 21.6 us -> 90.5 us
  Pallas kernels: 0 us -> 61 us
  between operations: 39.4 us -> 1.14 us
  waiting for transfers between devices: 34 us -> 17.9 us
    psum x20 -> x0, blocking collectives: 140 us -> none  [over_axes(): array = lax.psum(array, axis)]
    dot_general x42 -> x13, matrix products: 131 us -> 11.8 us  [the longest x6 5.41 us: per_device(): jnp.dot(place_in, transport(outgoing), preferred_element_type=jnp.float32)]
    pallas_call x0 -> x13, Pallas kernels: none -> 61 us  [the longest x6 43.7 us: fluid_call(): pl.pallas_call(body, grid=(steps,), in_specs=[whole(a) for a in small] +...]
    unnamed x16 -> x78, local copies, waits for them, and re-layouts: 3.25 us -> 59.2 us
    all_to_all x10 -> x12, blocking collectives: 176 us -> 204 us  [transport(): lax.all_to_all(buffer.reshape(devices, capacity, width), FLUID_SOLID, spl...]
    reshape x36 -> x27, local copies, waits for them, and re-layouts: 7.94 us -> 28.6 us  [the longest x12 15 us: transport(): return moved.reshape(devices * capacity, width)]
    all_to_all x3 -> x2, waiting for transfers between devices: 34 us -> 17.9 us  [the longest x1 9.71 us: transport(): lax.all_to_all(buffer.reshape(devices, capacity, width), FLUID_SOLID, spl...]
    all_to_all x3 -> x2, starting transfers between devices: 12.5 us -> 15.8 us  [the longest x1 11.5 us: per_device(): lax.all_to_all(wanted.reshape(devices, capacity), FLUID_SOLID, split_axis...]
  transfers between devices with their start and end apart: 3 -> 2, of which waited for: 3 -> 2; matrix products, arithmetic and copies ran while one was open for 1% -> 1% of each run, Pallas kernels for 0% -> 0%
where the time goes in v1:
time: 419 us; the launch traced here: 417 us
  blocking collectives  204 us (49%)
  local copies, waits for them, and re-layouts  90.5 us (22%)
  Pallas kernels  61 us (15%)
  matrix products  22.9 us (5%)
  waiting for transfers between devices  17.9 us (4%)
  starting transfers between devices  15.8 us (4%)
    all_to_all x12, blocking collectives, transport(): lax.all_to_all(buffer.reshape(devices, capacity, width), FLUID_SOLID, spl...  204 us
    unnamed x78, local copies, waits for them, and re-layouts  59.2 us
    pallas_call x6, Pallas kernels, fluid_call(): pl.pallas_call(body, grid=(steps,), in_specs=[whole(a) for a in small] +...  43.7 us
    pallas_call x6, Pallas kernels, shell_call(): pl.pallas_call(body, grid=(shells,), in_specs=[whole(a) for a in small] +...  15.6 us
    reshape x12, local copies, waits for them, and re-layouts, transport(): return moved.reshape(devices * capacity, width)  15 us
    reshape x13, local copies, waits for them, and re-layouts, transport(): buffer.reshape(devices, capacity, width)  13.2 us
    all_to_all x1, starting transfers between devices, per_device(): lax.all_to_all(wanted.reshape(devices, capacity), FLUID_SOLID, split_axis...  11.5 us
    all_to_all x1, waiting for transfers between devices, transport(): lax.all_to_all(buffer.reshape(devices, capacity, width), FLUID_SOLID, spl...  9.71 us
  transfers between devices with their start and end apart: 2, of which 2 were waited for; matrix products, arithmetic and copies ran while one was open for 1% of the time, Pallas kernels for 0%

profile of v1, /device:TPU:1, one launch (start us, length us, event | category | flops | bytes accessed | tf_op | source)
XLA Modules:
  0.0 417.1 jit_solution(6897479049342789817)
XLA Ops:
  3.1 11.5 %all-to-all-start = ((s32[128,1,2]{2,1,0:T(1,128)}), s32[128,1,2]{2,1,0:T(1,128)S(1)}, u32[]{:S(2)}, u32[]{:S(2)}) async-start(s32[128,1,2]{2,1,0:T(1,128)} %bitcast.1), calls=%async_computation | async-start | bytes 131072 | tf_op jit(solution)/shard_map/all_to_all | solution.py:383
  16.1 8.2 %all-to-all-done = s32[128,1,2]{2,1,0:T(1,128)S(1)} async-done(((s32[128,1,2]{2,1,0:T(1,128)}), s32[128,1,2]{2,1,0:T(1,128)S(1)}, u32[]{:S(2)}, u32[]{:S(2)}) %all-to-all-start) | async-done | bytes 1056 | tf_op jit(solution)/shard_map/all_to_all | solution.py:383
  26.9 4.3 %all-to-all-start.1 = ((bf16[128,2,768]{2,1,0:T(2,128)(2,1)}), bf16[128,2,768]{2,1,0:T(2,128)(2,1)S(1)}, u32[]{:S(2)}, u32[]{:S(2)}) async-start(bf16[128,2,768]{2,1,0:T(2,128)(2,1)} %reshape.145), calls=%async_computation.1 | async-start | bytes 786432 | tf_op jit(solution)/shard_map/all_to_all | solution.py:358
  34.1 9.7 %all-to-all-done.1 = bf16[128,2,768]{2,1,0:T(2,128)(2,1)S(1)} async-done(((bf16[128,2,768]{2,1,0:T(2,128)(2,1)}), bf16[128,2,768]{2,1,0:T(2,128)(2,1)S(1)}, u32[]{:S(2)}, u32[]{:S(2)}) %all-to-all-start.1) | async-done | bytes 393248 | tf_op jit(solution)/shard_map/all_to_all | solution.py:358
  44.2 4.9 %copy-done = bf16[104,256,256]{2,1,0:T(8,128)(2,1)S(1)} copy-done((bf16[104,256,256]{2,1,0:T(8,128)(2,1)S(1)}, bf16[104,256,256]{2,1,0:T(8,128)(2,1)}, u32[]{:S(2)}) %copy-start) | copy-done | bytes 13631512
  49.1 7.0 %fluid_side.6 = bf16[104,768]{1,0:T(8,128)(2,1)S(1)} custom-call(f32[112,768]{1,0:T(8,128)S(1)} %fusion.61.refs_0_.refs_1_, bf16[104,256,256]{2,1,0:T(8,128)(2,1)S(1)} %copy-done, f32[832,256]{1,0:T(8,128)S(1)} %get-tuple-element.96.refs_2_.refs_3_.refs_5_.refs_7_.refs_9_, f32[832,256]{1,0:T(8,128)S(1)} %get-tuple-element.95.refs_3_.refs_4_.refs_6_.refs_8_.refs_10_), custom_call_target="tpu_custom_call" | custom-call | tf_op jit(solution)/shard_map/fluid_side/pallas_call | solution.py:168
  56.7 16.6 %all_to_all.71 = bf16[128,2,768]{2,1,0:T(2,128)(2,1)} all-to-all(bf16[128,2,768]{2,1,0:T(2,128)(2,1)S(1)} %reshape.153), channel_id=1, replica_groups=mesh['fluid_0'=4,'fluid_1'=4,'fluid_2'=2,'solid'=4] {'fluid_0','fluid_1'..., dimensions={0} | all-to-all | bytes 786432 | tf_op jit(solution)/shard_map/all_to_all | solution.py:358
  74.7 3.7 copy-done.6
  78.4 2.5 shell_side.6
  81.3 17.2 %all_to_all.72 = bf16[128,2,896]{2,1,0:T(2,128)(2,1)S(1)} all-to-all(bf16[128,2,896]{2,1,0:T(2,128)(2,1)S(1)} %reshape.155), channel_id=1, replica_groups=mesh['fluid_0'=4,'fluid_1'=4,'fluid_2'=2,'solid'=4] {'fluid_0','fluid_1'..., dimensions={0} | all-to-all | bytes 917504 | tf_op jit(solution)/shard_map/all_to_all | solution.py:358
  99.0 4.9 %copy-done.1 = bf16[104,256,256]{2,1,0:T(8,128)(2,1)S(1)} copy-done((bf16[104,256,256]{2,1,0:T(8,128)(2,1)S(1)}, bf16[104,256,256]{2,1,0:T(8,128)(2,1)}, u32[]{:S(2)}) %copy-start.1) | copy-done | bytes 13631512
  103.8 7.1 %fluid_side.7 = (bf16[104,768]{1,0:T(8,128)(2,1)S(1)}, f32[104,768]{1,0:T(8,128)S(1)}, f32[16,128]{1,0:T(8,128)S(1)}, f32[16,128]{1,0:T(8,128)S(1)}) custom-call(f32[112,896]{1,0:T(8,128)S(1)} %fusion.60.refs_0_, f32[112,768]{1,0:T(8,128)S(1)} %fusion.61.refs_0_.refs_1_, bf16[104,256,256]{2,1,0:T(8,128)(2,1)S(1)} %copy-done.1, ...), custom_call_target="tpu_custom_call" | custom-call | tf_op jit(solution)/shard_map/fluid_side/pallas_call | solution.py:168
  112.2 16.7 %all_to_all.73 = bf16[128,2,768]{2,1,0:T(2,128)(2,1)S(1)} all-to-all(bf16[128,2,768]{2,1,0:T(2,128)(2,1)} %reshape.157), channel_id=1, replica_groups=mesh['fluid_0'=4,'fluid_1'=4,'fluid_2'=2,'solid'=4] {'fluid_0','fluid_1'..., dimensions={0} | all-to-all | bytes 786432 | tf_op jit(solution)/shard_map/all_to_all | solution.py:358
  131.1 3.7 copy-done.7
  134.8 2.5 shell_side.7
  137.8 17.2 %all_to_all.74 = bf16[128,2,896]{2,1,0:T(2,128)(2,1)S(1)} all-to-all(bf16[128,2,896]{2,1,0:T(2,128)(2,1)S(1)} %reshape.159), channel_id=1, replica_groups=mesh['fluid_0'=4,'fluid_1'=4,'fluid_2'=2,'solid'=4] {'fluid_0','fluid_1'..., dimensions={0} | all-to-all | bytes 917504 | tf_op jit(solution)/shard_map/all_to_all | solution.py:358
  157.2 4.9 %copy-done.2 = bf16[104,256,256]{2,1,0:T(8,128)(2,1)S(1)} copy-done((bf16[104,256,256]{2,1,0:T(8,128)(2,1)S(1)}, bf16[104,256,256]{2,1,0:T(8,128)(2,1)}, u32[]{:S(2)}) %copy-start.2) | copy-done | bytes 13631512
  162.0 7.2 %fluid_side.8 = (bf16[104,768]{1,0:T(8,128)(2,1)S(1)}, f32[104,768]{1,0:T(8,128)S(1)}, f32[16,128]{1,0:T(8,128)S(1)}, f32[16,128]{1,0:T(8,128)S(1)}) custom-call(f32[112,896]{1,0:T(8,128)S(1)} %fusion.59.refs_0_.refs_2_, f32[104,768]{1,0:T(8,128)S(1)} %get-tuple-element.54.refs_1_, bf16[104,256,256]{2,1,0:T(8,128)(2,1)S(1)} %copy-done.2, ...), custom_call_target="tpu_custom_call" | custom-call | tf_op jit(solution)/shard_map/fluid_side/pallas_call | solution.py:168
  172.3 17.4 %all_to_all.75 = bf16[128,2,768]{2,1,0:T(2,128)(2,1)} all-to-all(bf16[128,2,768]{2,1,0:T(2,128)(2,1)} %reshape.161), channel_id=1, replica_groups=mesh['fluid_0'=4,'fluid_1'=4,'fluid_2'=2,'solid'=4] {'fluid_0','fluid_1'..., dimensions={0} | all-to-all | bytes 786432 | tf_op jit(solution)/shard_map/all_to_all | solution.py:358
  189.7 1.9 reshape.162
  192.8 3.7 copy-done.8
  196.5 2.5 shell_side.8
  201.2 17.3 %all_to_all.76 = bf16[128,2,896]{2,1,0:T(2,128)(2,1)} all-to-all(bf16[128,2,896]{2,1,0:T(2,128)(2,1)S(1)} %reshape.163), channel_id=1, replica_groups=mesh['fluid_0'=4,'fluid_1'=4,'fluid_2'=2,'solid'=4] {'fluid_0','fluid_1'..., dimensions={0} | all-to-all | bytes 917504 | tf_op jit(solution)/shard_map/all_to_all | solution.py:358
  218.6 2.0 reshape.164
  221.8 4.9 %copy-done.3 = bf16[104,256,256]{2,1,0:T(8,128)(2,1)S(1)} copy-done((bf16[104,256,256]{2,1,0:T(8,128)(2,1)S(1)}, bf16[104,256,256]{2,1,0:T(8,128)(2,1)}, u32[]{:S(2)}) %copy-start.3) | copy-done | bytes 13631512
  226.7 7.2 %fluid_side.9 = (bf16[104,768]{1,0:T(8,128)(2,1)S(1)}, f32[104,768]{1,0:T(8,128)S(1)}, f32[16,128]{1,0:T(8,128)S(1)}, f32[16,128]{1,0:T(8,128)S(1)}) custom-call(f32[112,896]{1,0:T(8,128)S(1)} %fusion.58.refs_0_.refs_3_, f32[104,768]{1,0:T(8,128)S(1)} %get-tuple-element.61.refs_1_, f32[112,896]{1,0:T(8,128)S(1)} %fusion.59.refs_0_.refs_2_, ...), custom_call_target="tpu_custom_call" | custom-call | tf_op jit(solution)/shard_map/fluid_side/pallas_call | solution.py:168
  237.6 17.4 %all_to_all.77 = bf16[128,2,768]{2,1,0:T(2,128)(2,1)} all-to-all(bf16[128,2,768]{2,1,0:T(2,128)(2,1)} %reshape.165), channel_id=1, replica_groups=mesh['fluid_0'=4,'fluid_1'=4,'fluid_2'=2,'solid'=4] {'fluid_0','fluid_1'..., dimensions={0} | all-to-all | bytes 786432 | tf_op jit(solution)/shard_map/all_to_all | solution.py:358
  255.0 1.9 reshape.166
  258.1 3.7 copy-done.9
  261.8 2.5 shell_side.9
  266.0 2.0 reshape.167
  268.0 18.1 %all_to_all.78 = bf16[128,2,896]{2,1,0:T(2,128)(2,1)} all-to-all(bf16[128,2,896]{2,1,0:T(2,128)(2,1)} %reshape.167), channel_id=1, replica_groups=mesh['fluid_0'=4,'fluid_1'=4,'fluid_2'=2,'solid'=4] {'fluid_0','fluid_1'..., dimensions={0} | all-to-all | bytes 917504 | tf_op jit(solution)/shard_map/all_to_all | solution.py:358
  286.1 2.0 reshape.168
  289.4 4.9 %copy-done.4 = bf16[104,256,256]{2,1,0:T(8,128)(2,1)S(1)} copy-done((bf16[104,256,256]{2,1,0:T(8,128)(2,1)S(1)}, bf16[104,256,256]{2,1,0:T(8,128)(2,1)}, u32[]{:S(2)}) %copy-start.4) | copy-done | bytes 13631512
  295.2 7.2 %fluid_side.10 = (bf16[104,768]{1,0:T(8,128)(2,1)S(1)}, f32[104,768]{1,0:T(8,128)S(1)}, f32[16,128]{1,0:T(8,128)S(1)}, f32[16,128]{1,0:T(8,128)S(1)}) custom-call(f32[112,896]{1,0:T(8,128)S(1)} %fusion.57.refs_0_.refs_4_, f32[104,768]{1,0:T(8,128)S(1)} %copy-done.18, f32[112,896]{1,0:T(8,128)S(1)} %fusion.59.refs_0_.refs_2_, ...), custom_call_target="tpu_custom_call" | custom-call | tf_op jit(solution)/shard_map/fluid_side/pallas_call | solution.py:168
  305.5 17.4 %all_to_all.79 = bf16[128,2,768]{2,1,0:T(2,128)(2,1)} all-to-all(bf16[128,2,768]{2,1,0:T(2,128)(2,1)} %reshape.169), channel_id=1, replica_groups=mesh['fluid_0'=4,'fluid_1'=4,'fluid_2'=2,'solid'=4] {'fluid_0','fluid_1'..., dimensions={0} | all-to-all | bytes 786432 | tf_op jit(solution)/shard_map/all_to_all | solution.py:358
  322.9 1.9 reshape.170
  326.0 3.7 copy-done.10
  330.4 2.5 shell_side.10
  335.3 2.0 reshape.171
  337.3 18.1 %all_to_all.80 = bf16[128,2,896]{2,1,0:T(2,128)(2,1)} all-to-all(bf16[128,2,896]{2,1,0:T(2,128)(2,1)} %reshape.171), channel_id=1, replica_groups=mesh['fluid_0'=4,'fluid_1'=4,'fluid_2'=2,'solid'=4] {'fluid_0','fluid_1'..., dimensions={0} | all-to-all | bytes 917504 | tf_op jit(solution)/shard_map/all_to_all | solution.py:358
  355.4 2.0 reshape.172
  358.7 4.9 %copy-done.5 = bf16[104,256,256]{2,1,0:T(8,128)(2,1)S(1)} copy-done((bf16[104,256,256]{2,1,0:T(8,128)(2,1)S(1)}, bf16[104,256,256]{2,1,0:T(8,128)(2,1)}, u32[]{:S(2)}) %copy-start.5) | copy-done | bytes 13631512
  363.6 8.0 %fluid_side.11 = (bf16[104,768]{1,0:T(8,128)(2,1)S(1)}, bf16[104,768]{1,0:T(8,128)(2,1)}, f32[16,128]{1,0:T(8,128)S(1)}, f32[16,128]{1,0:T(8,128)S(1)}) custom-call(f32[112,896]{1,0:T(8,128)S(1)} %fusion.56.refs_0_, f32[104,768]{1,0:T(8,128)S(1)} %get-tuple-element.77.refs_1_, f32[112,896]{1,0:T(8,128)S(1)} %fusion.59.refs_0_.refs_2_, ...), custom_call_target="tpu_custom_call" | custom-call | tf_op jit(solution)/shard_map/fluid_side/pallas_call | solution.py:168
  373.4 16.5 %all_to_all.81 = bf16[128,2,768]{2,1,0:T(2,128)(2,1)S(1)} all-to-all(bf16[128,2,768]{2,1,0:T(2,128)(2,1)S(1)} %reshape.173), channel_id=1, replica_groups=mesh['fluid_0'=4,'fluid_1'=4,'fluid_2'=2,'solid'=4] {'fluid_0','fluid_1'..., dimensions={0} | all-to-all | bytes 786432 | tf_op jit(solution)/shard_map/all_to_all | solution.py:358
  390.9 3.7 copy-done.11
  395.3 3.2 shell_side.11
  399.2 13.6 %all_to_all.82 = bf16[128,2,128]{2,1,0:T(2,128)(2,1)S(1)} all-to-all(bf16[128,2,128]{2,1,0:T(2,128)(2,1)S(1)} %reshape.175), channel_id=1, replica_groups=mesh['fluid_0'=4,'fluid_1'=4,'fluid_2'=2,'solid'=4] {'fluid_0','fluid_1'..., dimensions={0} | all-to-all | bytes 131072 | tf_op jit(solution)/shard_map/all_to_all | solution.py:358
  (129 shorter events, 52.4 us)
Async XLA Ops:
  0.6 74.0 %copy-start.12 = (f32[8,768]{1,0:T(8,128)S(1)}, f32[8,768]{1,0:T(8,128)}, u32[]{:S(2)}) copy-start(f32[8,768]{1,0:T(8,128)} %refs_13_.3) | copy-start | bytes 73732
  0.6 74.0 %copy-start.13 = (f32[8,768]{1,0:T(8,128)S(1)}, f32[8,768]{1,0:T(8,128)}, u32[]{:S(2)}) copy-start(f32[8,768]{1,0:T(8,128)} %refs_14_.1) | copy-start | bytes 73732
  2.3 300.2 %copy-start.34 = (s32[104]{0:T(128)}, s32[104]{0:T(128)S(1)}, u32[]{:S(2)}) copy-start(s32[104]{0:T(128)S(1)} %get-tuple-element.93) | copy-start | bytes 1252
  3.1 21.1 %all-to-all-start = ((s32[128,1,2]{2,1,0:T(1,128)}), s32[128,1,2]{2,1,0:T(1,128)S(1)}, u32[]{:S(2)}, u32[]{:S(2)}) async-start(s32[128,1,2]{2,1,0:T(1,128)} %bitcast.1), calls=%async_computation | async-start | bytes 131072 | tf_op jit(solution)/shard_map/all_to_all | solution.py:383
  16.1 248.9 %copy-start.35 = (pred[16]{0:T(512)(128)(4,1)}, pred[16]{0:T(512)(128)(4,1)S(1)}, u32[]{:S(2)}) copy-start(pred[16]{0:T(512)(128)(4,1)S(1)} %iota_compare_fusion.10) | copy-start | bytes 52
  25.7 299.1 %copy-start.33 = (s32[256]{0:T(256)}, s32[256]{0:T(256)S(1)}, u32[]{:S(2)}) copy-start(s32[256]{0:T(256)S(1)} %eq.94) | copy-start | bytes 3076
  26.9 16.8 %all-to-all-start.1 = ((bf16[128,2,768]{2,1,0:T(2,128)(2,1)}), bf16[128,2,768]{2,1,0:T(2,128)(2,1)S(1)}, u32[]{:S(2)}, u32[]{:S(2)}) async-start(bf16[128,2,768]{2,1,0:T(2,128)(2,1)} %reshape.145), calls=%async_computation.1 | async-start | bytes 786432 | tf_op jit(solution)/shard_map/all_to_all | solution.py:358
  31.2 49.6 %copy-start.37 = (bf16[8]{0:T(256)(128)(2,1)}, bf16[8]{0:T(256)(128)(2,1)S(1)}, u32[]{:S(2)}) copy-start(bf16[8]{0:T(256)(128)(2,1)S(1)} %compare_select_fusion) | copy-start | bytes 52
  34.1 254.0 %copy-start.31 = (bf16[104,256]{1,0:T(8,128)(2,1)}, bf16[104,256]{1,0:T(8,128)(2,1)S(1)}, u32[]{:S(2)}) copy-start(bf16[104,256]{1,0:T(8,128)(2,1)S(1)} %fusion.7) | copy-start | bytes 159748
  44.0 244.1 %copy-start.32 = (bf16[8,256]{1,0:T(8,128)(2,1)}, bf16[8,256]{1,0:T(8,128)(2,1)S(1)}, u32[]{:S(2)}) copy-start(bf16[8,256]{1,0:T(8,128)(2,1)S(1)} %broadcast_in_dim.14) | copy-start | bytes 12292
  44.2 4.9 %copy-start = (bf16[104,256,256]{2,1,0:T(8,128)(2,1)S(1)}, bf16[104,256,256]{2,1,0:T(8,128)(2,1)}, u32[]{:S(2)}) copy-start(bf16[104,256,256]{2,1,0:T(8,128)(2,1)} %refs_8_.3) | copy-start | bytes 40894468
  74.4 250.3 %copy-start.36 = (s32[16]{0:T(128)}, s32[16]{0:T(128)S(1)}, u32[]{:S(2)}) copy-start(s32[16]{0:T(128)S(1)} %iota.31) | copy-start | bytes 196
  74.7 3.7 copy-start.6
  80.8 310.1 %copy-start.14 = (f32[8,768]{1,0:T(8,128)}, f32[8,768]{1,0:T(8,128)S(1)}, u32[]{:S(2)}) copy-start(f32[8,768]{1,0:T(8,128)S(1)} %get-tuple-element.52.refs_4_.refs_5_.refs_6_.refs_7_.refs_8_) | copy-start | bytes 73732
  99.0 4.9 %copy-start.1 = (bf16[104,256,256]{2,1,0:T(8,128)(2,1)S(1)}, bf16[104,256,256]{2,1,0:T(8,128)(2,1)}, u32[]{:S(2)}) copy-start(bf16[104,256,256]{2,1,0:T(8,128)(2,1)} %refs_8_.3) | copy-start | bytes 40894468
  111.0 20.1 %copy-start.29 = (f32[16,128]{1,0:T(8,128)}, f32[16,128]{1,0:T(8,128)S(1)}, u32[]{:S(2)}) copy-start(f32[16,128]{1,0:T(8,128)S(1)} %get-tuple-element.85.refs_1_) | copy-start | bytes 24580
  131.1 3.7 copy-start.7
  137.2 253.6 %copy-start.15 = (f32[8,768]{1,0:T(8,128)}, f32[8,768]{1,0:T(8,128)S(1)}, u32[]{:S(2)}) copy-start(f32[8,768]{1,0:T(8,128)S(1)} %get-tuple-element.59.refs_6_.refs_7_.refs_8_.refs_9_) | copy-start | bytes 73732
  157.2 4.9 %copy-start.2 = (bf16[104,256,256]{2,1,0:T(8,128)(2,1)S(1)}, bf16[104,256,256]{2,1,0:T(8,128)(2,1)}, u32[]{:S(2)}) copy-start(bf16[104,256,256]{2,1,0:T(8,128)(2,1)} %refs_8_.3) | copy-start | bytes 40894468
  169.2 189.5 %copy-start.20 = (f32[16,128]{1,0:T(8,128)}, f32[16,128]{1,0:T(8,128)S(1)}, u32[]{:S(2)}) copy-start(f32[16,128]{1,0:T(8,128)S(1)} %get-tuple-element.62.refs_3_.refs_4_.refs_5_.refs_2_) | copy-start | bytes 24580
  192.8 3.7 copy-start.8
  198.9 192.0 %copy-start.16 = (f32[8,768]{1,0:T(8,128)}, f32[8,768]{1,0:T(8,128)S(1)}, u32[]{:S(2)}) copy-start(f32[8,768]{1,0:T(8,128)S(1)} %get-tuple-element.67.refs_8_.refs_9_.refs_10_) | copy-start | bytes 73732
  221.8 4.9 %copy-start.3 = (bf16[104,256,256]{2,1,0:T(8,128)(2,1)S(1)}, bf16[104,256,256]{2,1,0:T(8,128)(2,1)}, u32[]{:S(2)}) copy-start(bf16[104,256,256]{2,1,0:T(8,128)(2,1)} %refs_8_.3) | copy-start | bytes 40894468
  233.9 0.7 copy-start.17
  234.6 124.1 %copy-start.22 = (f32[16,128]{1,0:T(8,128)}, f32[16,128]{1,0:T(8,128)S(1)}, u32[]{:S(2)}) copy-start(f32[16,128]{1,0:T(8,128)S(1)} %get-tuple-element.70.refs_5_.refs_6_.refs_3_) | copy-start | bytes 24580
  258.1 3.7 copy-start.9
  264.3 0.6 copy-start.27
  264.9 126.0 %copy-start.19 = (f32[8,768]{1,0:T(8,128)}, f32[8,768]{1,0:T(8,128)S(1)}, u32[]{:S(2)}) copy-start(f32[8,768]{1,0:T(8,128)S(1)} %get-tuple-element.75.refs_10_.refs_11_.refs_9_) | copy-start | bytes 73732
  289.4 4.9 %copy-start.4 = (bf16[104,256,256]{2,1,0:T(8,128)(2,1)S(1)}, bf16[104,256,256]{2,1,0:T(8,128)(2,1)}, u32[]{:S(2)}) copy-start(bf16[104,256,256]{2,1,0:T(8,128)(2,1)} %refs_8_.3) | copy-start | bytes 40894468
  294.2 1.0 copy-start.18
  302.4 69.1 %copy-start.23 = (f32[16,128]{1,0:T(8,128)}, f32[16,128]{1,0:T(8,128)S(1)}, u32[]{:S(2)}) copy-start(f32[16,128]{1,0:T(8,128)S(1)} %get-tuple-element.78.refs_7_.refs_4_) | copy-start | bytes 24580
  326.0 3.7 copy-start.10
  329.7 0.7 copy-start.28
  332.9 0.6 copy-start.25
  333.6 65.0 %copy-start.21 = (f32[8,768]{1,0:T(8,128)}, f32[8,768]{1,0:T(8,128)S(1)}, u32[]{:S(2)}) copy-start(f32[8,768]{1,0:T(8,128)S(1)} %get-tuple-element.83.refs_12_.refs_10_) | copy-start | bytes 73732
  358.7 4.9 %copy-start.5 = (bf16[104,256,256]{2,1,0:T(8,128)(2,1)S(1)}, bf16[104,256,256]{2,1,0:T(8,128)(2,1)}, u32[]{:S(2)}) copy-start(bf16[104,256,256]{2,1,0:T(8,128)(2,1)} %refs_8_.3) | copy-start | bytes 40894468
  371.6 0.6 copy-start.30
  390.9 3.7 copy-start.11
  394.6 0.7 copy-start.26
  398.5 0.6 copy-start.24

commit v2 on v0

v2 whole, which is shorter than its diff:
```python
import jax
import jax.numpy as jnp
from jax import lax
from jax.experimental import pallas as pl
from jax.experimental.pallas import tpu as pltpu
from jax.sharding import Mesh
from jax.sharding import PartitionSpec as P

ITERS = 6
FLUID_SOLID = ("fluid_0", "fluid_1", "fluid_2", "solid")
FLUID = ("fluid_0", "fluid_1", "fluid_2")

RELAX = 0.3
EPSILON = 1e-06
VMEM_LIMIT = 16 * 2**20

LANES = 128
TILE = 16
RHS_AT = 5
SQUARES_AT = 10
PIECE = 32
ROWS = 16


def least_squares(gram, target_side):
    order = len(target_side)
    lower = [[None] * order for _ in range(order)]
    for row in range(order):
        for column in range(row + 1):
            total = gram[row][column]
            for inner in range(column):
                total = total - lower[row][inner] * lower[column][inner]
            if row == column:
                lower[row][row] = jnp.sqrt(total)
            else:
                lower[row][column] = total / lower[column][column]
    middle = []
    for row in range(order):
        total = target_side[row]
        for inner in range(row):
            total = total - lower[row][inner] * middle[inner]
        middle.append(total / lower[row][row])
    result = [None] * order
    for row in reversed(range(order)):
        total = middle[row]
        for inner in range(row + 1, order):
            total = total - lower[inner][row] * result[inner]
        result[row] = total / lower[row][row]
    return result


def spread_sums(line):
    whole = line + pltpu.roll(line, LANES - PIECE, 1) + pltpu.roll(line, LANES - 2 * PIECE, 1)
    row = lax.broadcasted_iota(jnp.int32, (ROWS, LANES), 0)
    lane = lax.broadcasted_iota(jnp.int32, (ROWS, LANES), 1)
    picked = jnp.where(row == lane, jnp.broadcast_to(whole, (ROWS, LANES)), 0.0)
    return jnp.broadcast_to(jnp.sum(picked, axis=1, keepdims=True), (ROWS, LANES))


def solve_coefficients(sums):
    order = len(sums)
    gram = [[sums[row][column : column + 1] for column in range(row + 1)] for row in range(order)]
    target_side = [-sums[-1][RHS_AT + i : RHS_AT + i + 1] for i in range(order)]
    return least_squares(gram, target_side)


def vmem():
    return pl.BlockSpec(memory_space=pltpu.VMEM)


def fluid_call(places, collect, messages, sums, rbf_blocks, traction, massive, group, last):
    blocks, nodes, _ = rbf_blocks.shape
    rows_all = messages[0].shape[0]
    chunks = 3 * nodes // LANES
    halves = nodes // LANES
    sum_row = collect.shape[0] - ROWS
    k = len(messages) - 1
    n_sums = len(sums)
    fold = 256

    def body(*refs):
        refs = list(refs)
        place_ref, collect_ref = refs.pop(0), refs.pop(0)
        message_refs = [refs.pop(0) for _ in range(k + 1)]
        sum_refs = [refs.pop(0) for _ in range(n_sums)]
        rbf_ref, traction_ref, mass_ref = refs.pop(0), refs.pop(0), refs.pop(0)
        sending_ref = refs.pop(0)
        load_ref = refs.pop(0) if last else None
        sums_out, coefs_out = (refs.pop(0), refs.pop(0)) if k else (None, None)
        shown_ref, result_ref = refs.pop(0), refs.pop(0)
        kept_ref = refs.pop(0) if last else None

        weights = []
        if k:
            line = jnp.dot(
                collect_ref[sum_row:, :], message_refs[-1][...], preferred_element_type=jnp.float32
            )
            fresh = spread_sums(line[:1])
            sums_out[...] = fresh
            coefs_out[...] = jnp.zeros_like(coefs_out)
            weights = [RELAX]
            if k >= 2:
                coefs = solve_coefficients([ref[...] for ref in sum_refs] + [fresh])
                for i, coef in enumerate(coefs):
                    coefs_out[i : i + 1, :] = coef
                weights = [None] + [1.0 + coef for coef in coefs]

        def show(at, carry):
            rows = pl.ds(pl.multiple_of(at * fold, fold), fold)
            shown = message_refs[0][rows, :].astype(jnp.float32)
            for weight, ref in zip(weights, message_refs[1:]):
                change = ref[rows, :].astype(jnp.float32)
                shown = shown + (change if weight is None else weight * change)
            shown_ref[rows, :] = shown
            result_ref[rows, :] = jnp.zeros((fold, LANES), jnp.float32)
            return carry

        lax.fori_loop(0, rows_all // fold, show, 0)
        shown_ref[rows_all:, :] = jnp.zeros((TILE, LANES), jnp.float32)

        def contract(at, carry):
            loads, spots = [], []
            for inner in range(group):
                block = at * group + inner
                spot = place_ref[block]
                spots.append(spot)
                shown = jnp.concatenate(
                    [shown_ref[pl.ds(spot + half, 8, stride=halves), :] for half in range(halves)],
                    axis=1,
                ).astype(jnp.bfloat16)
                moved = lax.dot_general(
                    shown,
                    rbf_ref[block],
                    (((1,), (1,)), ((), ())),
                    preferred_element_type=jnp.float32,
                )
                rows = pl.ds(pl.multiple_of(block * 8, 8), 8)
                load = (traction_ref[rows, :] - mass_ref[rows, :] * moved).astype(jnp.bfloat16)
                loads.append(load)
                if last:
                    for half in range(halves):
                        lanes = slice(half * LANES, (half + 1) * LANES)
                        kept_ref[half, rows, :] = load[:, lanes].astype(jnp.float32)
            for inner in range(group):
                block = at * group + inner
                result = jnp.dot(
                    loads[inner], rbf_ref[block], preferred_element_type=jnp.float32
                )
                for half in range(halves):
                    result_ref[pl.ds(spots[inner] + half, 3, stride=halves), :] = result[
                        :3, half * LANES : (half + 1) * LANES
                    ]
            return carry

        lax.fori_loop(0, blocks // group, contract, 0)
        sending_ref[...] = result_ref[...].astype(jnp.bfloat16)
        if last:
            for at in range(chunks):
                component, half = divmod(at, halves)
                load_ref[:, at * LANES : (at + 1) * LANES] = kept_ref[
                    half, pl.ds(component, blocks, stride=8), :
                ].astype(jnp.bfloat16)

    out_shape = [jax.ShapeDtypeStruct((rows_all, LANES), jnp.bfloat16)]
    if last:
        out_shape.append(jax.ShapeDtypeStruct((blocks, 3 * nodes), jnp.bfloat16))
    if k:
        out_shape += [jax.ShapeDtypeStruct((ROWS, LANES), jnp.float32)] * 2
    scratch = [
        pltpu.VMEM((rows_all + TILE, LANES), jnp.float32),
        pltpu.VMEM((rows_all, LANES), jnp.float32),
    ]
    if last:
        scratch.append(pltpu.VMEM((halves, blocks * 8, LANES), jnp.float32))
    inputs = (collect, *messages, *sums, rbf_blocks, traction, massive)
    out = pl.pallas_call(
        body,
        in_specs=[pl.BlockSpec(memory_space=pltpu.SMEM)] + [vmem()] * len(inputs),
        out_specs=[vmem()] * len(out_shape),
        out_shape=out_shape,
        scratch_shapes=scratch,
        compiler_params=pltpu.CompilerParams(vmem_limit_bytes=VMEM_LIMIT),
        name="fluid_side",
    )(places, *inputs)
    out = list(out)
    sending = out.pop(0)
    load = out.pop(0) if last else None
    fresh, coefs = (out.pop(0), out.pop(0)) if k else (None, None)
    return sending, load, fresh, coefs


def full_sum(array):
    return jnp.sum(jnp.sum(array, axis=0, keepdims=True), axis=1, keepdims=True)


def shell_call(
    arrived, coefs, shown, residuals, images, start, robin_coef, collect, pick, shell_inverse, last
):
    shells, breadth, _ = shell_inverse.shape
    chunks = breadth // LANES
    height = chunks * shells
    k = len(images)

    def body(*refs):
        refs = list(refs)
        arrived_ref = refs.pop(0)
        coef_ref = refs.pop(0) if k else None
        shown_ref = refs.pop(0)
        residual_refs = [refs.pop(0) for _ in range(k)]
        image_refs = [refs.pop(0) for _ in range(k)]
        start_ref, robin_ref, collect_ref, pick_ref, inverse_ref = [refs.pop(0) for _ in range(5)]
        message_ref, image_out = refs.pop(0), refs.pop(0)
        residual_out, shown_out = (None, None) if last else (refs.pop(0), refs.pop(0))

        load = jnp.dot(
            collect_ref[:height, :], arrived_ref[...], preferred_element_type=jnp.float32
        )
        if k == 0:
            current = start_ref[...]
        elif k == 1:
            current = start_ref[...] + RELAX * residual_refs[0][...]
        else:
            current = image_refs[-1][...]
            for i in range(k - 1):
                current = current + coef_ref[i : i + 1, :] * (
                    image_refs[i + 1][...] - image_refs[i][...]
                )
        forcing = load + robin_ref[...] * current
        forcing = jnp.concatenate(
            [forcing[t * shells : (t + 1) * shells] for t in range(chunks)], axis=1
        ).astype(jnp.bfloat16)
        row = lax.broadcasted_iota(jnp.int32, (shells, breadth), 0)

        def contract(s, picked):
            product = jnp.dot(forcing, inverse_ref[s], preferred_element_type=jnp.float32)
            return jnp.where(row == s, product, picked)

        wide = lax.fori_loop(
            0, shells, contract, jnp.zeros((shells, breadth), jnp.float32), unroll=2
        )
        image = jnp.concatenate([wide[:, t * LANES : (t + 1) * LANES] for t in range(chunks)], axis=0)
        image_out[...] = image
        residual = image - current
        lane = lax.broadcasted_iota(jnp.int32, (1, LANES), 1)
        line = jnp.where(lane == SQUARES_AT, full_sum(residual * residual), 0.0)
        if k:
            chain = [ref[...] for ref in residual_refs] + [residual]
            changes = [chain[i + 1] - chain[i] for i in range(k)]
            for i, change in enumerate(changes):
                line = line + jnp.where(lane == i, full_sum(changes[-1] * change), 0.0)
                line = line + jnp.where(lane == RHS_AT + i, full_sum(change * residual), 0.0)
        head = line.astype(jnp.bfloat16).astype(jnp.float32)
        rest = line - head
        middle = rest.astype(jnp.bfloat16).astype(jnp.float32)
        tail = (rest - middle).astype(jnp.bfloat16).astype(jnp.float32)
        pieces = head + pltpu.roll(middle, PIECE, 1) + pltpu.roll(tail, 2 * PIECE, 1)
        if last:
            message_ref[...] = jnp.broadcast_to(pieces, message_ref.shape).astype(jnp.bfloat16)
            return
        residual_out[...] = residual
        difference = (image - shown_ref[...]).astype(jnp.bfloat16)
        shown_out[...] = shown_ref[...] + difference.astype(jnp.float32)
        first = lax.broadcasted_iota(jnp.int32, (ROWS, LANES), 0) == 0
        below = jnp.where(first, jnp.broadcast_to(pieces, (ROWS, LANES)), 0.0).astype(jnp.bfloat16)
        message_ref[...] = jnp.dot(
            pick_ref[...],
            jnp.concatenate([difference, below], axis=0),
            preferred_element_type=jnp.float32,
        ).astype(jnp.bfloat16)

    inputs = (
        [arrived]
        + ([coefs] if k else [])
        + [shown, *residuals, *images, start, robin_coef, collect, pick, shell_inverse]
    )
    own = jax.ShapeDtypeStruct((height, LANES), jnp.float32)
    if last:
        out_shape = [jax.ShapeDtypeStruct((ROWS, LANES), jnp.bfloat16), own]
    else:
        out_shape = [jax.ShapeDtypeStruct(arrived.shape, jnp.bfloat16), own, own, own]
    return pl.pallas_call(
        body,
        in_specs=[vmem()] * len(inputs),
        out_specs=[vmem()] * len(out_shape),
        out_shape=out_shape,
        compiler_params=pltpu.CompilerParams(vmem_limit_bytes=VMEM_LIMIT),
        name="shell_side",
    )(*inputs)


def closing_call(line, sums, images, shells, count):
    height = images[0].shape[0]
    chunks = height // shells
    n_sums = len(sums)

    def body(*refs):
        refs = list(refs)
        line_ref = refs.pop(0)
        sum_refs = [refs.pop(0) for _ in range(n_sums)]
        image_refs = [refs.pop(0) for _ in range(len(images))]
        current_ref, norm_ref = refs
        fresh = spread_sums(line_ref[0:1, :])
        every = [ref[...] for ref in sum_refs] + [fresh]
        coefs = solve_coefficients(every[1:])
        moving = image_refs[-1][...]
        for i, coef in enumerate(coefs):
            moving = moving + coef * (image_refs[i + 1][...] - image_refs[i][...])
        for t in range(chunks):
            current_ref[:, t * LANES : (t + 1) * LANES] = moving[t * shells : (t + 1) * shells]
        lane = lax.broadcasted_iota(jnp.int32, (1, LANES), 1)
        squares = jnp.zeros((1, LANES), jnp.float32)
        for i, part in enumerate(every):
            squares = jnp.where(lane == i, part[SQUARES_AT : SQUARES_AT + 1], squares)
        norm_ref[...] = jnp.sqrt(squares / count + EPSILON)

    return pl.pallas_call(
        body,
        out_shape=[
            jax.ShapeDtypeStruct((shells, chunks * LANES), jnp.float32),
            jax.ShapeDtypeStruct((1, LANES), jnp.float32),
        ],
        name="closing",
    )(line, *sums, *images)


def spread_components(array, blocks, nodes):
    wide = array.astype(jnp.float32).reshape(blocks, 3, nodes)
    return jnp.pad(wide, ((0, 0), (0, 5), (0, 0))).reshape(blocks * 8, nodes)


def by_chunks(array, shells):
    return array.reshape(shells, -1, LANES).transpose(1, 0, 2).reshape(-1, LANES)


def per_device(
    rbf_blocks, fluid_traction, fluid_mass, route, slot, shell_inverse, robin_coef, shell_start
):
    devices = lax.axis_size(FLUID) * lax.axis_size("solid")
    blocks = rbf_blocks.shape[0]
    nodes = rbf_blocks.shape[1]
    breadth = 3 * nodes
    chunks = breadth // LANES
    shells = shell_inverse.shape[0]
    height = chunks * shells
    capacity = 2
    count = shells * devices * breadth

    def exchange(array):
        return lax.all_to_all(array, FLUID_SOLID, split_axis=0, concat_axis=0, tiled=True)

    def transport(buffer):
        return exchange(buffer.reshape(devices, TILE, LANES)).reshape(devices * TILE, LANES)

    destination = route[:, 0]
    block_order = jnp.arange(blocks, dtype=jnp.int32)
    earlier = (destination[:, None] == destination[None, :]) & (
        block_order[None, :] < block_order[:, None]
    )
    slot_rank = jnp.sum(earlier.astype(jnp.int32), axis=1)
    position = destination * capacity + slot_rank
    positions = jnp.arange(devices * capacity, dtype=jnp.int32)
    placing = positions[:, None] == position[None, :]
    wanted = jnp.max(jnp.where(placing, slot[None, :] + 1, 0), axis=1) - 1
    asked = exchange(wanted.reshape(devices, capacity))
    places = destination * TILE + slot_rank * chunks

    order = jnp.arange(TILE, dtype=jnp.int32)[None, :]
    named = jnp.where(order < chunks, asked[:, :1], asked[:, 1:2])
    shows = jnp.where(
        (named >= 0) & (order < capacity * chunks), (order % chunks) * shells + named, -1
    )
    shows = jnp.where(order == capacity * chunks, height, shows).reshape(devices * TILE)
    stacked = jnp.arange(height + ROWS, dtype=jnp.int32)
    pick = (shows[:, None] == stacked[None, :]).astype(jnp.bfloat16)
    collect = (stacked[:, None] == shows[None, :]).astype(jnp.bfloat16)

    traction = spread_components(fluid_traction, blocks, nodes)
    massive = spread_components(fluid_mass, blocks, nodes)
    start = by_chunks(shell_start, shells)
    robin = by_chunks(robin_coef, shells)
    group = next(n for n in (8, 4, 2, 1) if blocks % n == 0)

    start_half = start.astype(jnp.bfloat16)
    shown = start_half.astype(jnp.float32)
    outgoing = jnp.dot(
        pick, jnp.pad(start_half, ((0, ROWS), (0, 0))), preferred_element_type=jnp.float32
    ).astype(jnp.bfloat16)
    messages = []
    sums = []
    residuals = []
    images = []
    last_load = None
    for iteration in range(ITERS):
        last = iteration == ITERS - 1
        messages.append(transport(outgoing))
        sending, last_load, fresh, coefs = fluid_call(
            places, collect, messages, sums[1:], rbf_blocks, traction, massive, group, last
        )
        if iteration:
            sums.append(fresh)
        made = shell_call(
            transport(sending),
            coefs,
            shown,
            residuals,
            images,
            start,
            robin,
            collect,
            pick,
            shell_inverse,
            last,
        )
        outgoing, image = made[:2]
        images.append(image)
        if not last:
            residuals.append(made[2])
            shown = made[3]
    ending = exchange(jnp.broadcast_to(outgoing[:1], (devices, 1, LANES)))
    line = jnp.sum(ending.astype(jnp.float32), axis=0)
    current, norms = closing_call(line, sums, images, shells, count)
    return (current, last_load, norms[0, :ITERS])


def solution(mesh):
    split = Mesh(
        mesh.devices.reshape(4, 4, 2, mesh.shape["solid"]),
        ("fluid_0", "fluid_1", "fluid_2", "solid"),
    )
    placed = (
        P(FLUID_SOLID, None, None),
        P(FLUID_SOLID, None),
        P(FLUID_SOLID, None),
        P(FLUID_SOLID, None),
        P(FLUID_SOLID),
        P(FLUID_SOLID, None, None),
        P(FLUID_SOLID, None),
        P(FLUID_SOLID, None),
    )
    return jax.shard_map(
        per_device,
        mesh=split,
        in_specs=placed,
        out_specs=(P(FLUID_SOLID, None), P(FLUID_SOLID, None), P()),
        check_vma=False,
    )
```

time: 576 us -> 338 us (0.59); the launches traced: 566 us -> 337 us
  matrix products: 134 us -> 1.26 us
  blocking collectives: 316 us -> 192 us
  Pallas kernels: 0 us -> 65.3 us
  between operations: 39.4 us -> 0.97 us
  starting transfers between devices: 12.5 us -> 19.8 us
    psum x20 -> x0, blocking collectives: 140 us -> none  [over_axes(): array = lax.psum(array, axis)]
    dot_general x54 -> x1, matrix products: 134 us -> 1.26 us  [per_device(): jnp.dot(pick, jnp.pad(start_half, ((0, ROWS), (0, 0))), preferred_element...]
    pallas_call x0 -> x13, Pallas kernels: none -> 65.3 us  [the longest x6 49.8 us: fluid_call(): pl.pallas_call(body, in_specs=[pl.BlockSpec(memory_space=pltpu.SMEM)] + [...]
    all_to_all x10 -> x11, blocking collectives: 176 us -> 192 us  [exchange(): lax.all_to_all(array, FLUID_SOLID, split_axis=0, concat_axis=0, tiled=True)]
    unnamed x16 -> x50, local copies, waits for them, and re-layouts: 3.25 us -> 17.9 us
    reshape x36 -> x2, local copies, waits for them, and re-layouts: 7.94 us -> 0.37 us  [spread_components(): wide = array.astype(jnp.float32).reshape(blocks, 3, nodes)]
    all_to_all x3, starting transfers between devices: 12.5 us -> 19.8 us  [exchange(): lax.all_to_all(array, FLUID_SOLID, split_axis=0, concat_axis=0, tiled=True)]
where the time goes in v2:
time: 338 us; the launch traced here: 337 us
  blocking collectives  192 us (57%)
  Pallas kernels  65.3 us (19%)
  waiting for transfers between devices  33 us (10%)
  local copies, waits for them, and re-layouts  20.4 us (6%)
  starting transfers between devices  19.8 us (6%)
  other arithmetic  4.29 us (1%)
    all_to_all x11, blocking collectives, exchange(): lax.all_to_all(array, FLUID_SOLID, split_axis=0, concat_axis=0, tiled=True)  192 us
    pallas_call x6, Pallas kernels, fluid_call(): pl.pallas_call(body, in_specs=[pl.BlockSpec(memory_space=pltpu.SMEM)] + [...  49.8 us
    all_to_all x3, waiting for transfers between devices, exchange(): lax.all_to_all(array, FLUID_SOLID, split_axis=0, concat_axis=0, tiled=True)  33 us
    all_to_all x3, starting transfers between devices, exchange(): lax.all_to_all(array, FLUID_SOLID, split_axis=0, concat_axis=0, tiled=True)  19.8 us
    unnamed x50, local copies, waits for them, and re-layouts  17.9 us
    pallas_call x6, Pallas kernels, shell_call(): pl.pallas_call(body, in_specs=[vmem()] * len(inputs), out_specs=[vmem()]...  13.8 us
  transfers between devices with their start and end apart: 3, of which 3 were waited for; matrix products, arithmetic and copies ran while one was open for 1% of the time, Pallas kernels for 0%

profile of v2, /device:TPU:1, one launch (start us, length us, event | category | flops | bytes accessed | tf_op | source)
XLA Modules:
  0.0 337.3 jit_solution(2644534302953489310)
XLA Ops:
  0.6 0.9 convert_reduce_fusion.1
  1.5 0.7 multiply_add_fusion
  2.4 0.8 sub.7
  3.1 11.5 %all-to-all-start = ((s32[128,1,2]{2,1,0:T(1,128)}), s32[128,1,2]{2,1,0:T(1,128)S(1)}, u32[]{:S(2)}, u32[]{:S(2)}) async-start(s32[128,1,2]{2,1,0:T(1,128)} %bitcast.1), calls=%async_computation | async-start | bytes 131072 | tf_op jit(solution)/shard_map/all_to_all | solution.py:349
  14.7 1.3 fusion.10
  16.0 1.1 copy.36
  17.1 0.2 copy.37
  17.3 1.1 copy.38
  18.4 0.2 copy.39
  18.6 5.7 %all-to-all-done = s32[128,1,2]{2,1,0:T(1,128)S(1)} async-done(((s32[128,1,2]{2,1,0:T(1,128)}), s32[128,1,2]{2,1,0:T(1,128)S(1)}, u32[]{:S(2)}, u32[]{:S(2)}) %all-to-all-start) | async-done | bytes 1056 | tf_op jit(solution)/shard_map/all_to_all | solution.py:349
  24.6 1.3 convolution_convert_fusion
  25.9 4.3 %all-to-all-start.1 = ((bf16[128,16,128]{2,1,0:T(8,128)(2,1)}), bf16[128,16,128]{2,1,0:T(8,128)(2,1)S(1)}, u32[]{:S(2)}, u32[]{:S(2)}) async-start(bf16[128,16,128]{2,1,0:T(8,128)(2,1)} %bitcast.6), calls=%async_computation.1 | async-start | bytes 1048576 | tf_op jit(solution)/shard_map/all_to_all | solution.py:349
  30.4 13.7 %all-to-all-done.1 = bf16[128,16,128]{2,1,0:T(8,128)(2,1)S(1)} async-done(((bf16[128,16,128]{2,1,0:T(8,128)(2,1)}), bf16[128,16,128]{2,1,0:T(8,128)(2,1)S(1)}, u32[]{:S(2)}, u32[]{:S(2)}) %all-to-all-start.1) | async-done | bytes 524320 | tf_op jit(solution)/shard_map/all_to_all | solution.py:349
  44.1 4.9 %copy-done = bf16[104,256,256]{2,1,0:T(8,128)(2,1)S(1)} copy-done((bf16[104,256,256]{2,1,0:T(8,128)(2,1)S(1)}, bf16[104,256,256]{2,1,0:T(8,128)(2,1)}, u32[]{:S(2)}) %copy-start) | copy-done | bytes 13631512
  49.0 8.4 %fluid_side.6 = bf16[2048,128]{1,0:T(8,128)(2,1)} custom-call(s32[104]{0:T(128)S(1)} %get-tuple-element.88.refs_0_, bf16[64,2048]{1,0:T(8,128)(2,1)S(1)} %fusion.2.refs_1_.refs_4_.refs_7_.refs_9_.refs_11_.refs_13_.refs_15_, bf16[2048,128]{1,0:T(8,128)(2,1)S(1)} %bitcast.56, bf16[104,256,256]{2,1,0:T(8,128)(2,1)S(1)} %copy-done, ...), custom_call_target="tpu_custom_call" | custom-call | tf_op jit(solution)/shard_map/fluid_side/pallas_call | solution.py:176
  57.4 4.1 %all-to-all-start.2 = ((bf16[128,16,128]{2,1,0:T(8,128)(2,1)}), bf16[128,16,128]{2,1,0:T(8,128)(2,1)S(1)}, u32[]{:S(2)}, u32[]{:S(2)}) async-start(bf16[128,16,128]{2,1,0:T(8,128)(2,1)} %bitcast.12), calls=%async_computation.2 | async-start | bytes 1048576 | tf_op jit(solution)/shard_map/all_to_all | solution.py:349
  61.5 0.3 fusion.refs_5_.refs_8_.refs_10_.refs_12_.refs_14_.refs_16_
  61.8 13.6 %all-to-all-done.2 = bf16[128,16,128]{2,1,0:T(8,128)(2,1)S(1)} async-done(((bf16[128,16,128]{2,1,0:T(8,128)(2,1)}), bf16[128,16,128]{2,1,0:T(8,128)(2,1)S(1)}, u32[]{:S(2)}, u32[]{:S(2)}) %all-to-all-start.2) | async-done | bytes 524320 | tf_op jit(solution)/shard_map/all_to_all | solution.py:349
  75.5 3.7 %copy-done.2 = bf16[8,768,768]{2,1,0:T(8,128)(2,1)S(1)} copy-done((bf16[8,768,768]{2,1,0:T(8,128)(2,1)S(1)}, bf16[8,768,768]{2,1,0:T(8,128)(2,1)}, u32[]{:S(2)}) %copy-start.2) | copy-done | bytes 9437208
  79.1 0.7 copy-done.4
  79.9 0.7 copy-done.6
  80.6 0.7 copy-done.13
  81.3 2.3 shell_side.6
  83.7 17.9 %all_to_all.74 = bf16[128,16,128]{2,1,0:T(8,128)(2,1)S(1)} all-to-all(bf16[128,16,128]{2,1,0:T(8,128)(2,1)S(1)} %bitcast.100), channel_id=1, replica_groups=mesh['fluid_0'=4,'fluid_1'=4,'fluid_2'=2,'solid'=4] {'fluid_0','fluid_1'..., dimensions={0} | all-to-all | bytes 1048576 | tf_op jit(solution)/shard_map/all_to_all | solution.py:349
  101.6 4.9 %copy-done.1 = bf16[104,256,256]{2,1,0:T(8,128)(2,1)S(1)} copy-done((bf16[104,256,256]{2,1,0:T(8,128)(2,1)S(1)}, bf16[104,256,256]{2,1,0:T(8,128)(2,1)}, u32[]{:S(2)}) %copy-start.1) | copy-done | bytes 13631512
  106.4 7.9 %fluid_side.7 = (bf16[2048,128]{1,0:T(8,128)(2,1)S(1)}, f32[16,128]{1,0:T(8,128)S(1)}, f32[16,128]{1,0:T(8,128)S(1)}) custom-call(s32[104]{0:T(128)S(1)} %get-tuple-element.88.refs_0_, bf16[64,2048]{1,0:T(8,128)(2,1)S(1)} %fusion.2.refs_1_.refs_4_.refs_7_.refs_9_.refs_11_.refs_13_.refs_15_, bf16[2048,128]{1,0:T(8,128)(2,1)S(1)} %bitcast.57, ...), custom_call_target="tpu_custom_call" | custom-call | tf_op jit(solution)/shard_map/fluid_side/pallas_call | solution.py:176
  114.4 17.9 %all_to_all.75 = bf16[128,16,128]{2,1,0:T(8,128)(2,1)S(1)} all-to-all(bf16[128,16,128]{2,1,0:T(8,128)(2,1)S(1)} %bitcast.101), channel_id=1, replica_groups=mesh['fluid_0'=4,'fluid_1'=4,'fluid_2'=2,'solid'=4] {'fluid_0','fluid_1'..., dimensions={0} | all-to-all | bytes 1048576 | tf_op jit(solution)/shard_map/all_to_all | solution.py:349
  132.3 2.3 shell_side.7
  134.6 17.9 %all_to_all.76 = bf16[128,16,128]{2,1,0:T(8,128)(2,1)S(1)} all-to-all(bf16[128,16,128]{2,1,0:T(8,128)(2,1)S(1)} %bitcast.96), channel_id=1, replica_groups=mesh['fluid_0'=4,'fluid_1'=4,'fluid_2'=2,'solid'=4] {'fluid_0','fluid_1'..., dimensions={0} | all-to-all | bytes 1048576 | tf_op jit(solution)/shard_map/all_to_all | solution.py:349
  152.5 8.0 %fluid_side.8 = (bf16[2048,128]{1,0:T(8,128)(2,1)S(1)}, f32[16,128]{1,0:T(8,128)S(1)}, f32[16,128]{1,0:T(8,128)S(1)}) custom-call(s32[104]{0:T(128)S(1)} %get-tuple-element.88.refs_0_, bf16[64,2048]{1,0:T(8,128)(2,1)S(1)} %fusion.2.refs_1_.refs_4_.refs_7_.refs_9_.refs_11_.refs_13_.refs_15_, bf16[2048,128]{1,0:T(8,128)(2,1)S(1)} %bitcast.58, ...), custom_call_target="tpu_custom_call" | custom-call | tf_op jit(solution)/shard_map/fluid_side/pallas_call | solution.py:176
  160.6 17.9 %all_to_all.77 = bf16[128,16,128]{2,1,0:T(8,128)(2,1)S(1)} all-to-all(bf16[128,16,128]{2,1,0:T(8,128)(2,1)S(1)} %bitcast.102), channel_id=1, replica_groups=mesh['fluid_0'=4,'fluid_1'=4,'fluid_2'=2,'solid'=4] {'fluid_0','fluid_1'..., dimensions={0} | all-to-all | bytes 1048576 | tf_op jit(solution)/shard_map/all_to_all | solution.py:349
  178.5 2.3 shell_side.8
  180.8 17.9 %all_to_all.78 = bf16[128,16,128]{2,1,0:T(8,128)(2,1)S(1)} all-to-all(bf16[128,16,128]{2,1,0:T(8,128)(2,1)S(1)} %bitcast.97), channel_id=1, replica_groups=mesh['fluid_0'=4,'fluid_1'=4,'fluid_2'=2,'solid'=4] {'fluid_0','fluid_1'..., dimensions={0} | all-to-all | bytes 1048576 | tf_op jit(solution)/shard_map/all_to_all | solution.py:349
  198.7 8.2 %fluid_side.9 = (bf16[2048,128]{1,0:T(8,128)(2,1)S(1)}, f32[16,128]{1,0:T(8,128)S(1)}, f32[16,128]{1,0:T(8,128)S(1)}) custom-call(s32[104]{0:T(128)S(1)} %get-tuple-element.88.refs_0_, bf16[64,2048]{1,0:T(8,128)(2,1)S(1)} %fusion.2.refs_1_.refs_4_.refs_7_.refs_9_.refs_11_.refs_13_.refs_15_, bf16[2048,128]{1,0:T(8,128)(2,1)S(1)} %bitcast.59, ...), custom_call_target="tpu_custom_call" | custom-call | tf_op jit(solution)/shard_map/fluid_side/pallas_call | solution.py:176
  206.9 17.9 %all_to_all.79 = bf16[128,16,128]{2,1,0:T(8,128)(2,1)S(1)} all-to-all(bf16[128,16,128]{2,1,0:T(8,128)(2,1)S(1)} %bitcast.103), channel_id=1, replica_groups=mesh['fluid_0'=4,'fluid_1'=4,'fluid_2'=2,'solid'=4] {'fluid_0','fluid_1'..., dimensions={0} | all-to-all | bytes 1048576 | tf_op jit(solution)/shard_map/all_to_all | solution.py:349
  224.7 2.4 shell_side.9
  227.1 17.9 %all_to_all.80 = bf16[128,16,128]{2,1,0:T(8,128)(2,1)S(1)} all-to-all(bf16[128,16,128]{2,1,0:T(8,128)(2,1)S(1)} %bitcast.98), channel_id=1, replica_groups=mesh['fluid_0'=4,'fluid_1'=4,'fluid_2'=2,'solid'=4] {'fluid_0','fluid_1'..., dimensions={0} | all-to-all | bytes 1048576 | tf_op jit(solution)/shard_map/all_to_all | solution.py:349
  245.0 8.3 %fluid_side.10 = (bf16[2048,128]{1,0:T(8,128)(2,1)S(1)}, f32[16,128]{1,0:T(8,128)S(1)}, f32[16,128]{1,0:T(8,128)S(1)}) custom-call(s32[104]{0:T(128)S(1)} %get-tuple-element.88.refs_0_, bf16[64,2048]{1,0:T(8,128)(2,1)S(1)} %fusion.2.refs_1_.refs_4_.refs_7_.refs_9_.refs_11_.refs_13_.refs_15_, bf16[2048,128]{1,0:T(8,128)(2,1)S(1)} %bitcast.60, ...), custom_call_target="tpu_custom_call" | custom-call | tf_op jit(solution)/shard_map/fluid_side/pallas_call | solution.py:176
  253.2 17.9 %all_to_all.81 = bf16[128,16,128]{2,1,0:T(8,128)(2,1)S(1)} all-to-all(bf16[128,16,128]{2,1,0:T(8,128)(2,1)S(1)} %bitcast.104), channel_id=1, replica_groups=mesh['fluid_0'=4,'fluid_1'=4,'fluid_2'=2,'solid'=4] {'fluid_0','fluid_1'..., dimensions={0} | all-to-all | bytes 1048576 | tf_op jit(solution)/shard_map/all_to_all | solution.py:349
  271.1 2.3 shell_side.10
  273.5 17.9 %all_to_all.82 = bf16[128,16,128]{2,1,0:T(8,128)(2,1)S(1)} all-to-all(bf16[128,16,128]{2,1,0:T(8,128)(2,1)S(1)} %bitcast.99), channel_id=1, replica_groups=mesh['fluid_0'=4,'fluid_1'=4,'fluid_2'=2,'solid'=4] {'fluid_0','fluid_1'..., dimensions={0} | all-to-all | bytes 1048576 | tf_op jit(solution)/shard_map/all_to_all | solution.py:349
  291.3 9.0 %fluid_side.11 = (bf16[2048,128]{1,0:T(8,128)(2,1)S(1)}, bf16[104,768]{1,0:T(8,128)(2,1)}, f32[16,128]{1,0:T(8,128)S(1)}, f32[16,128]{1,0:T(8,128)S(1)}) custom-call(s32[104]{0:T(128)S(1)} %get-tuple-element.88.refs_0_, bf16[64,2048]{1,0:T(8,128)(2,1)S(1)} %fusion.2.refs_1_.refs_4_.refs_7_.refs_9_.refs_11_.refs_13_.refs_15_, bf16[2048,128]{1,0:T(8,128)(2,1)S(1)} %bitcast.61, ...), custom_call_target="tpu_custom_call" | custom-call | tf_op jit(solution)/shard_map/fluid_side/pallas_call | solution.py:176
  300.3 17.9 %all_to_all.83 = bf16[128,16,128]{2,1,0:T(8,128)(2,1)S(1)} all-to-all(bf16[128,16,128]{2,1,0:T(8,128)(2,1)S(1)} %bitcast.95), channel_id=1, replica_groups=mesh['fluid_0'=4,'fluid_1'=4,'fluid_2'=2,'solid'=4] {'fluid_0','fluid_1'..., dimensions={0} | all-to-all | bytes 1048576 | tf_op jit(solution)/shard_map/all_to_all | solution.py:349
  318.2 2.1 shell_side.11
  320.4 13.6 %all_to_all.84 = bf16[128,1,128]{2,1,0:T(2,128)(2,1)S(1)} all-to-all(bf16[128,1,128]{2,1,0:T(2,128)(2,1)S(1)} %broadcast_in_dim.80), channel_id=1, replica_groups=mesh['fluid_0'=4,'fluid_1'=4,'fluid_2'=2,'solid'=4] {'fluid_0','fluid_1'..., dimensions={0} | all-to-all | bytes 65536 | tf_op jit(solution)/shard_map/all_to_all | solution.py:349
  334.0 0.5 convert_reduce_fusion
  334.5 1.7 closing.1
  336.2 1.1 slice_bitcast_fusion
  (55 shorter events, 0.8 us)
Async XLA Ops:
  3.1 21.1 %all-to-all-start = ((s32[128,1,2]{2,1,0:T(1,128)}), s32[128,1,2]{2,1,0:T(1,128)S(1)}, u32[]{:S(2)}, u32[]{:S(2)}) async-start(s32[128,1,2]{2,1,0:T(1,128)} %bitcast.1), calls=%async_computation | async-start | bytes 131072 | tf_op jit(solution)/shard_map/all_to_all | solution.py:349
  25.9 18.2 %all-to-all-start.1 = ((bf16[128,16,128]{2,1,0:T(8,128)(2,1)}), bf16[128,16,128]{2,1,0:T(8,128)(2,1)S(1)}, u32[]{:S(2)}, u32[]{:S(2)}) async-start(bf16[128,16,128]{2,1,0:T(8,128)(2,1)} %bitcast.6), calls=%async_computation.1 | async-start | bytes 1048576 | tf_op jit(solution)/shard_map/all_to_all | solution.py:349
  44.1 4.9 %copy-start = (bf16[104,256,256]{2,1,0:T(8,128)(2,1)S(1)}, bf16[104,256,256]{2,1,0:T(8,128)(2,1)}, u32[]{:S(2)}) copy-start(bf16[104,256,256]{2,1,0:T(8,128)(2,1)} %refs_11_.3) | copy-start | bytes 40894468
  57.4 18.1 %all-to-all-start.2 = ((bf16[128,16,128]{2,1,0:T(8,128)(2,1)}), bf16[128,16,128]{2,1,0:T(8,128)(2,1)S(1)}, u32[]{:S(2)}, u32[]{:S(2)}) async-start(bf16[128,16,128]{2,1,0:T(8,128)(2,1)} %bitcast.12), calls=%async_computation.2 | async-start | bytes 1048576 | tf_op jit(solution)/shard_map/all_to_all | solution.py:349
  75.4 3.7 %copy-start.2 = (bf16[8,768,768]{2,1,0:T(8,128)(2,1)S(1)}, bf16[8,768,768]{2,1,0:T(8,128)(2,1)}, u32[]{:S(2)}) copy-start(bf16[8,768,768]{2,1,0:T(8,128)(2,1)} %refs_17_.1) | copy-start | bytes 28311556
  79.1 0.7 copy-start.4
  79.9 0.7 copy-start.6
  80.6 0.7 copy-start.13
  81.3 50.9 %copy-start.3 = (bf16[8,768,768]{2,1,0:T(8,128)(2,1)S(1)}, bf16[8,768,768]{2,1,0:T(8,128)(2,1)}, u32[]{:S(2)}) copy-start(bf16[8,768,768]{2,1,0:T(8,128)(2,1)} %refs_17_.1) | copy-start | bytes 28311556
  81.3 50.9 %copy-start.5 = (f32[8,768]{1,0:T(8,128)S(1)}, f32[8,768]{1,0:T(8,128)}, u32[]{:S(2)}) copy-start(f32[8,768]{1,0:T(8,128)} %param.15) | copy-start | bytes 73732
  81.3 50.9 %copy-start.7 = (f32[8,768]{1,0:T(8,128)S(1)}, f32[8,768]{1,0:T(8,128)}, u32[]{:S(2)}) copy-start(f32[8,768]{1,0:T(8,128)} %param.14) | copy-start | bytes 73732
  83.7 234.5 %copy-start.8 = (f32[48,128]{1,0:T(8,128)}, f32[48,128]{1,0:T(8,128)S(1)}, u32[]{:S(2)}) copy-start(f32[48,128]{1,0:T(8,128)S(1)} %get-tuple-element.48.refs_4_.refs_5_.refs_6_.refs_7_.refs_8_) | copy-start | bytes 73732
  101.6 4.9 %copy-start.1 = (bf16[104,256,256]{2,1,0:T(8,128)(2,1)S(1)}, bf16[104,256,256]{2,1,0:T(8,128)(2,1)}, u32[]{:S(2)}) copy-start(bf16[104,256,256]{2,1,0:T(8,128)(2,1)} %refs_11_.3) | copy-start | bytes 40894468
  106.4 46.1 %slice-start = ((s8[13631488]{0:T(1024)(128)(4,1)}), s8[4194304]{0:T(1024)(128)(4,1)S(1)}, s32[]{:S(2)}) async-start(s8[13631488]{0:T(1024)(128)(4,1)} %bitcast.54), calls=%async_computation.14 | async-start | bytes 8388608
  106.4 46.1 %slice-start.1 = ((s8[13631488]{0:T(1024)(128)(4,1)}), s8[4194304]{0:T(1024)(128)(4,1)S(1)}, s32[]{:S(2)}) async-start(s8[13631488]{0:T(1024)(128)(4,1)} %bitcast.54), calls=%async_computation.15 | async-start | bytes 8388608
  106.4 46.1 %slice-start.2 = ((s8[13631488]{0:T(1024)(128)(4,1)}), s8[4194304]{0:T(1024)(128)(4,1)S(1)}, s32[]{:S(2)}) async-start(s8[13631488]{0:T(1024)(128)(4,1)} %bitcast.54), calls=%async_computation.16 | async-start | bytes 8388608
  114.4 46.2 %copy-start.18 = (f32[16,128]{1,0:T(8,128)}, f32[16,128]{1,0:T(8,128)S(1)}, u32[]{:S(2)}) copy-start(f32[16,128]{1,0:T(8,128)S(1)} %get-tuple-element.77.refs_1_) | copy-start | bytes 24580
  132.3 20.3 %slice-start.3 = ((s8[13631488]{0:T(1024)(128)(4,1)}), s8[1048576]{0:T(1024)(128)(4,1)S(1)}, s32[]{:S(2)}) async-start(s8[13631488]{0:T(1024)(128)(4,1)} %bitcast.54), calls=%async_computation.17 | async-start | bytes 2097152
  134.6 183.6 %copy-start.9 = (f32[48,128]{1,0:T(8,128)}, f32[48,128]{1,0:T(8,128)S(1)}, u32[]{:S(2)}) copy-start(f32[48,128]{1,0:T(8,128)S(1)} %get-tuple-element.54.refs_6_.refs_7_.refs_8_.refs_9_) | copy-start | bytes 73732
  160.6 130.7 %copy-start.12 = (f32[16,128]{1,0:T(8,128)}, f32[16,128]{1,0:T(8,128)S(1)}, u32[]{:S(2)}) copy-start(f32[16,128]{1,0:T(8,128)S(1)} %get-tuple-element.56.refs_6_.refs_7_.refs_8_.refs_2_) | copy-start | bytes 24580
  180.8 137.4 %copy-start.10 = (f32[48,128]{1,0:T(8,128)}, f32[48,128]{1,0:T(8,128)S(1)}, u32[]{:S(2)}) copy-start(f32[48,128]{1,0:T(8,128)S(1)} %get-tuple-element.61.refs_8_.refs_9_.refs_10_) | copy-start | bytes 73732
  206.9 84.5 %copy-start.15 = (f32[16,128]{1,0:T(8,128)}, f32[16,128]{1,0:T(8,128)S(1)}, u32[]{:S(2)}) copy-start(f32[16,128]{1,0:T(8,128)S(1)} %get-tuple-element.63.refs_8_.refs_9_.refs_3_) | copy-start | bytes 24580
  227.1 91.1 %copy-start.11 = (f32[48,128]{1,0:T(8,128)}, f32[48,128]{1,0:T(8,128)S(1)}, u32[]{:S(2)}) copy-start(f32[48,128]{1,0:T(8,128)S(1)} %get-tuple-element.68.refs_10_.refs_11_.refs_9_) | copy-start | bytes 73732
  253.2 47.1 %copy-start.16 = (f32[16,128]{1,0:T(8,128)}, f32[16,128]{1,0:T(8,128)S(1)}, u32[]{:S(2)}) copy-start(f32[16,128]{1,0:T(8,128)S(1)} %get-tuple-element.70.refs_10_.refs_4_) | copy-start | bytes 24580
  273.5 46.9 %copy-start.14 = (f32[48,128]{1,0:T(8,128)}, f32[48,128]{1,0:T(8,128)S(1)}, u32[]{:S(2)}) copy-start(f32[48,128]{1,0:T(8,128)S(1)} %get-tuple-element.75.refs_12_.refs_10_) | copy-start | bytes 73732
  300.3 20.0 %copy-start.19 = (f32[16,128]{1,0:T(8,128)}, f32[16,128]{1,0:T(8,128)S(1)}, u32[]{:S(2)}) copy-start(f32[16,128]{1,0:T(8,128)S(1)} %get-tuple-element.78.refs_5_) | copy-start | bytes 24580
  320.3 14.2 %copy-start.17 = (f32[48,128]{1,0:T(8,128)}, f32[48,128]{1,0:T(8,128)S(1)}, u32[]{:S(2)}) copy-start(f32[48,128]{1,0:T(8,128)S(1)} %get-tuple-element.79.refs_11_) | copy-start | bytes 73732

commit v3 on v2

--- a/solution.py
+++ b/solution.py
@@ -12,14 +12,19 @@
 
 RELAX = 0.3
 EPSILON = 1e-06
-VMEM_LIMIT = 16 * 2**20
+SMALL_LIMIT = 12 * 2**20
+STREAM_LIMIT = 24 * 2**20
 
 LANES = 128
-TILE = 16
 RHS_AT = 5
 SQUARES_AT = 10
 PIECE = 32
 ROWS = 16
+FORTH = 14
+BACK = 12
+FOLD = 256
+FLUID_STREAMS = 2
+SHELL_STREAMS = 1
 
 
 def least_squares(gram, target_side):
@@ -68,32 +73,43 @@
     return pl.BlockSpec(memory_space=pltpu.VMEM)
 
 
-def fluid_call(places, collect, messages, sums, rbf_blocks, traction, massive, group, last):
+def fluid_call(places, add_up, messages, sums, rbf_blocks, traction, massive, stream, last):
     blocks, nodes, _ = rbf_blocks.shape
     rows_all = messages[0].shape[0]
     chunks = 3 * nodes // LANES
     halves = nodes // LANES
-    sum_row = collect.shape[0] - ROWS
+    rows_back = add_up.shape[1] // FORTH * BACK
     k = len(messages) - 1
     n_sums = len(sums)
-    fold = 256
+    group = next(n for n in (26, 16, 8, 4, 2, 1) if blocks % n == 0)
+    lag = min(group, 13)
+    steps = blocks // group
 
     def body(*refs):
         refs = list(refs)
-        place_ref, collect_ref = refs.pop(0), refs.pop(0)
+        place_ref, add_ref = refs.pop(0), refs.pop(0)
         message_refs = [refs.pop(0) for _ in range(k + 1)]
         sum_refs = [refs.pop(0) for _ in range(n_sums)]
-        rbf_ref, traction_ref, mass_ref = refs.pop(0), refs.pop(0), refs.pop(0)
+        source_ref, traction_ref, mass_ref = refs.pop(0), refs.pop(0), refs.pop(0)
         sending_ref = refs.pop(0)
         load_ref = refs.pop(0) if last else None
         sums_out, coefs_out = (refs.pop(0), refs.pop(0)) if k else (None, None)
         shown_ref, result_ref = refs.pop(0), refs.pop(0)
         kept_ref = refs.pop(0) if last else None
+        rbf_ref, landed = (refs.pop(0), refs.pop(0)) if stream else (source_ref, None)
+
+        def piece(at):
+            rows = pl.ds(at * group, group)
+            return pltpu.make_async_copy(source_ref.at[rows], rbf_ref.at[rows], landed.at[at])
+
+        if stream:
+            for at in range(steps):
+                piece(at).start()
 
         weights = []
         if k:
             line = jnp.dot(
-                collect_ref[sum_row:, :], message_refs[-1][...], preferred_element_type=jnp.float32
+                add_ref[...], message_refs[-1][...], preferred_element_type=jnp.float32
             )
             fresh = spread_sums(line[:1])
             sums_out[...] = fresh
@@ -106,53 +122,56 @@
                 weights = [None] + [1.0 + coef for coef in coefs]
 
         def show(at, carry):
-            rows = pl.ds(pl.multiple_of(at * fold, fold), fold)
+            rows = pl.ds(pl.multiple_of(at * FOLD, FOLD), FOLD)
             shown = message_refs[0][rows, :].astype(jnp.float32)
             for weight, ref in zip(weights, message_refs[1:]):
                 change = ref[rows, :].astype(jnp.float32)
                 shown = shown + (change if weight is None else weight * change)
             shown_ref[rows, :] = shown
-            result_ref[rows, :] = jnp.zeros((fold, LANES), jnp.float32)
             return carry
 
-        lax.fori_loop(0, rows_all // fold, show, 0)
-        shown_ref[rows_all:, :] = jnp.zeros((TILE, LANES), jnp.float32)
+        lax.fori_loop(0, rows_all // FOLD, show, 0)
+        shown_ref[rows_all:, :] = jnp.zeros((16, LANES), jnp.float32)
+        result_ref[...] = jnp.zeros_like(result_ref)
+
+        def load_of(block):
+            spot = place_ref[0, block]
+            shown = jnp.concatenate(
+                [shown_ref[pl.ds(spot + half, 8, stride=halves), :] for half in range(halves)],
+                axis=1,
+            ).astype(jnp.bfloat16)
+            moved = lax.dot_general(
+                shown, rbf_ref[block], (((1,), (1,)), ((), ())), preferred_element_type=jnp.float32
+            )
+            rows = pl.ds(pl.multiple_of(block * 8, 8), 8)
+            load = (traction_ref[rows, :] - mass_ref[rows, :] * moved).astype(jnp.bfloat16)
+            if last:
+                for half in range(halves):
+                    lanes = slice(half * LANES, (half + 1) * LANES)
+                    kept_ref[half, rows, :] = load[:, lanes].astype(jnp.float32)
+            return load
+
+        def map_back(block, load):
+            spot = place_ref[1, block]
+            result = jnp.dot(load, rbf_ref[block], preferred_element_type=jnp.float32)
+            for half in range(halves):
+                result_ref[pl.ds(spot + half, 3, stride=halves), :] = result[
+                    :3, half * LANES : (half + 1) * LANES
+                ]
 
         def contract(at, carry):
-            loads, spots = [], []
-            for inner in range(group):
-                block = at * group + inner
-                spot = place_ref[block]
-                spots.append(spot)
-                shown = jnp.concatenate(
-                    [shown_ref[pl.ds(spot + half, 8, stride=halves), :] for half in range(halves)],
-                    axis=1,
-                ).astype(jnp.bfloat16)
-                moved = lax.dot_general(
-                    shown,
-                    rbf_ref[block],
-                    (((1,), (1,)), ((), ())),
-                    preferred_element_type=jnp.float32,
-                )
-                rows = pl.ds(pl.multiple_of(block * 8, 8), 8)
-                load = (traction_ref[rows, :] - mass_ref[rows, :] * moved).astype(jnp.bfloat16)
-                loads.append(load)
-                if last:
-                    for half in range(halves):
-                        lanes = slice(half * LANES, (half + 1) * LANES)
-                        kept_ref[half, rows, :] = load[:, lanes].astype(jnp.float32)
-            for inner in range(group):
-                block = at * group + inner
-                result = jnp.dot(
-                    loads[inner], rbf_ref[block], preferred_element_type=jnp.float32
-                )
-                for half in range(halves):
-                    result_ref[pl.ds(spots[inner] + half, 3, stride=halves), :] = result[
-                        :3, half * LANES : (half + 1) * LANES
-                    ]
+            if stream:
+                piece(at).wait()
+            first = at * group
+            loads = {}
+            for inner in range(group + lag):
+                if inner < group:
+                    loads[inner] = load_of(first + inner)
+                if inner >= lag:
+                    map_back(first + inner - lag, loads.pop(inner - lag))
             return carry
 
-        lax.fori_loop(0, blocks // group, contract, 0)
+        lax.fori_loop(0, steps, contract, 0)
         sending_ref[...] = result_ref[...].astype(jnp.bfloat16)
         if last:
             for at in range(chunks):
@@ -161,25 +180,37 @@
                     half, pl.ds(component, blocks, stride=8), :
                 ].astype(jnp.bfloat16)
 
-    out_shape = [jax.ShapeDtypeStruct((rows_all, LANES), jnp.bfloat16)]
+    out_shape = [jax.ShapeDtypeStruct((rows_back, LANES), jnp.bfloat16)]
     if last:
         out_shape.append(jax.ShapeDtypeStruct((blocks, 3 * nodes), jnp.bfloat16))
     if k:
         out_shape += [jax.ShapeDtypeStruct((ROWS, LANES), jnp.float32)] * 2
     scratch = [
-        pltpu.VMEM((rows_all + TILE, LANES), jnp.float32),
-        pltpu.VMEM((rows_all, LANES), jnp.float32),
+        pltpu.VMEM((rows_all + 16, LANES), jnp.float32),
+        pltpu.VMEM((rows_back, LANES), jnp.float32),
     ]
     if last:
         scratch.append(pltpu.VMEM((halves, blocks * 8, LANES), jnp.float32))
-    inputs = (collect, *messages, *sums, rbf_blocks, traction, massive)
+    if stream:
+        scratch += [
+            pltpu.VMEM(rbf_blocks.shape, rbf_blocks.dtype),
+            pltpu.SemaphoreType.DMA((steps,)),
+        ]
+    inputs = (add_up, *messages, *sums, rbf_blocks, traction, massive)
+    in_specs = [vmem()] * len(inputs)
+    if stream:
+        rbf_blocks = pltpu.with_memory_space_constraint(rbf_blocks, pltpu.HBM)
+        inputs = (add_up, *messages, *sums, rbf_blocks, traction, massive)
+        in_specs[-3] = pl.BlockSpec(memory_space=pltpu.HBM)
     out = pl.pallas_call(
         body,
-        in_specs=[pl.BlockSpec(memory_space=pltpu.SMEM)] + [vmem()] * len(inputs),
+        in_specs=[pl.BlockSpec(memory_space=pltpu.SMEM)] + in_specs,
         out_specs=[vmem()] * len(out_shape),
         out_shape=out_shape,
         scratch_shapes=scratch,
-        compiler_params=pltpu.CompilerParams(vmem_limit_bytes=VMEM_LIMIT),
+        compiler_params=pltpu.CompilerParams(
+            vmem_limit_bytes=STREAM_LIMIT if stream else SMALL_LIMIT
+        ),
         name="fluid_side",
     )(places, *inputs)
     out = list(out)
@@ -194,7 +225,18 @@
 
 
 def shell_call(
-    arrived, coefs, shown, residuals, images, start, robin_coef, collect, pick, shell_inverse, last
+    arrived,
+    coefs,
+    shown,
+    residuals,
+    images,
+    start,
+    robin_coef,
+    collect,
+    pick,
+    shell_inverse,
+    stream,
+    last,
 ):
     shells, breadth, _ = shell_inverse.shape
     chunks = breadth // LANES
@@ -211,10 +253,16 @@
         start_ref, robin_ref, collect_ref, pick_ref, inverse_ref = [refs.pop(0) for _ in range(5)]
         message_ref, image_out = refs.pop(0), refs.pop(0)
         residual_out, shown_out = (None, None) if last else (refs.pop(0), refs.pop(0))
-
-        load = jnp.dot(
-            collect_ref[:height, :], arrived_ref[...], preferred_element_type=jnp.float32
-        )
+        near_ref, landed = refs if stream else (inverse_ref, None)
+        copies = []
+        if stream:
+            for s in range(shells):
+                copies.append(
+                    pltpu.make_async_copy(inverse_ref.at[s], near_ref.at[s], landed.at[s])
+                )
+                copies[-1].start()
+
+        load = jnp.dot(collect_ref[...], arrived_ref[...], preferred_element_type=jnp.float32)
         if k == 0:
             current = start_ref[...]
         elif k == 1:
@@ -231,13 +279,12 @@
         ).astype(jnp.bfloat16)
         row = lax.broadcasted_iota(jnp.int32, (shells, breadth), 0)
 
-        def contract(s, picked):
-            product = jnp.dot(forcing, inverse_ref[s], preferred_element_type=jnp.float32)
-            return jnp.where(row == s, product, picked)
-
-        wide = lax.fori_loop(
-            0, shells, contract, jnp.zeros((shells, breadth), jnp.float32), unroll=2
-        )
+        wide = jnp.zeros((shells, breadth), jnp.float32)
+        for s in range(shells):
+            if stream:
+                copies[s].wait()
+            product = jnp.dot(forcing, near_ref[s], preferred_element_type=jnp.float32)
+            wide = jnp.where(row == s, product, wide)
         image = jnp.concatenate([wide[:, t * LANES : (t + 1) * LANES] for t in range(chunks)], axis=0)
         image_out[...] = image
         residual = image - current
@@ -277,13 +324,26 @@
     if last:
         out_shape = [jax.ShapeDtypeStruct((ROWS, LANES), jnp.bfloat16), own]
     else:
-        out_shape = [jax.ShapeDtypeStruct(arrived.shape, jnp.bfloat16), own, own, own]
+        rows_out = pick.shape[0]
+        out_shape = [jax.ShapeDtypeStruct((rows_out, LANES), jnp.bfloat16), own, own, own]
+    in_specs = [vmem()] * len(inputs)
+    scratch = []
+    if stream:
+        inputs[-1] = pltpu.with_memory_space_constraint(shell_inverse, pltpu.HBM)
+        in_specs[-1] = pl.BlockSpec(memory_space=pltpu.HBM)
+        scratch = [
+            pltpu.VMEM(shell_inverse.shape, shell_inverse.dtype),
+            pltpu.SemaphoreType.DMA((shells,)),
+        ]
     return pl.pallas_call(
         body,
-        in_specs=[vmem()] * len(inputs),
+        in_specs=in_specs,
         out_specs=[vmem()] * len(out_shape),
         out_shape=out_shape,
-        compiler_params=pltpu.CompilerParams(vmem_limit_bytes=VMEM_LIMIT),
+        scratch_shapes=scratch,
+        compiler_params=pltpu.CompilerParams(
+            vmem_limit_bytes=STREAM_LIMIT if stream else SMALL_LIMIT
+        ),
         name="shell_side",
     )(*inputs)
 
@@ -348,8 +408,9 @@
     def exchange(array):
         return lax.all_to_all(array, FLUID_SOLID, split_axis=0, concat_axis=0, tiled=True)
 
-    def transport(buffer):
-        return exchange(buffer.reshape(devices, TILE, LANES)).reshape(devices * TILE, LANES)
+    def transport(buffer, part):
+        moved = exchange(buffer.reshape(devices, -1, part, LANES))
+        return moved.reshape(-1, LANES)
 
     destination = route[:, 0]
     block_order = jnp.arange(blocks, dtype=jnp.int32)
@@ -362,23 +423,29 @@
     placing = positions[:, None] == position[None, :]
     wanted = jnp.max(jnp.where(placing, slot[None, :] + 1, 0), axis=1) - 1
     asked = exchange(wanted.reshape(devices, capacity))
-    places = destination * TILE + slot_rank * chunks
-
-    order = jnp.arange(TILE, dtype=jnp.int32)[None, :]
-    named = jnp.where(order < chunks, asked[:, :1], asked[:, 1:2])
-    shows = jnp.where(
-        (named >= 0) & (order < capacity * chunks), (order % chunks) * shells + named, -1
+    places = jnp.stack(
+        [destination * FORTH + slot_rank * chunks, destination * BACK + slot_rank * chunks]
     )
-    shows = jnp.where(order == capacity * chunks, height, shows).reshape(devices * TILE)
+
     stacked = jnp.arange(height + ROWS, dtype=jnp.int32)
-    pick = (shows[:, None] == stacked[None, :]).astype(jnp.bfloat16)
-    collect = (stacked[:, None] == shows[None, :]).astype(jnp.bfloat16)
+
+    def shows(size):
+        order = jnp.arange(size, dtype=jnp.int32)[None, :]
+        named = jnp.where(order < chunks, asked[:, :1], asked[:, 1:2])
+        rows = jnp.where(
+            (named >= 0) & (order < capacity * chunks), (order % chunks) * shells + named, -1
+        )
+        return jnp.where(order == capacity * chunks, height, rows).reshape(-1)
+
+    pick = (shows(FORTH)[:, None] == stacked[None, :]).astype(jnp.bfloat16)
+    collect = (stacked[:height, None] == shows(BACK)[None, :]).astype(jnp.bfloat16)
+    summed = jnp.arange(devices * FORTH, dtype=jnp.int32)[None, :] % FORTH == capacity * chunks
+    add_up = jnp.broadcast_to(summed, (ROWS, devices * FORTH)).astype(jnp.bfloat16)
 
     traction = spread_components(fluid_traction, blocks, nodes)
     massive = spread_components(fluid_mass, blocks, nodes)
     start = by_chunks(shell_start, shells)
     robin = by_chunks(robin_coef, shells)
-    group = next(n for n in (8, 4, 2, 1) if blocks % n == 0)
 
     start_half = start.astype(jnp.bfloat16)
     shown = start_half.astype(jnp.float32)
@@ -392,14 +459,22 @@
     last_load = None
     for iteration in range(ITERS):
         last = iteration == ITERS - 1
-        messages.append(transport(outgoing))
+        messages.append(transport(outgoing, 2))
         sending, last_load, fresh, coefs = fluid_call(
-            places, collect, messages, sums[1:], rbf_blocks, traction, massive, group, last
+            places,
+            add_up,
+            messages,
+            sums[1:],
+            rbf_blocks,
+            traction,
+            massive,
+            iteration < FLUID_STREAMS,
+            last,
         )
         if iteration:
             sums.append(fresh)
         made = shell_call(
-            transport(sending),
+            transport(sending, 4),
             coefs,
             shown,
             residuals,
@@ -409,6 +484,7 @@
             collect,
             pick,
             shell_inverse,
+            iteration < SHELL_STREAMS,
             last,
         )
         outgoing, image = made[:2]

time: 338 us -> 309 us (0.914)
  local copies, waits for them, and re-layouts: 20.4 us -> 6.36 us
  blocking collectives: 192 us -> 182 us
    unnamed x50 -> x40, local copies, waits for them, and re-layouts: 17.9 us -> 3.59 us
    all_to_all x11, blocking collectives: 192 us -> 182 us  [exchange(): lax.all_to_all(array, FLUID_SOLID, split_axis=0, concat_axis=0, tiled=True)]
where the time goes in v3:
time: 309 us
  blocking collectives  182 us (59%)
  Pallas kernels  62.6 us (20%)
  waiting for transfers between devices  30.8 us (10%)
  starting transfers between devices  20 us (6%)
  local copies, waits for them, and re-layouts  6.36 us (2%)
  other arithmetic  4.5 us (1%)
    all_to_all x11, blocking collectives, exchange(): lax.all_to_all(array, FLUID_SOLID, split_axis=0, concat_axis=0, tiled=True)  182 us
    pallas_call x6, Pallas kernels, fluid_call(): pl.pallas_call(body, in_specs=[pl.BlockSpec(memory_space=pltpu.SMEM)] + i...  46.9 us
    all_to_all x3, waiting for transfers between devices, exchange(): lax.all_to_all(array, FLUID_SOLID, split_axis=0, concat_axis=0, tiled=True)  30.8 us
    all_to_all x3, starting transfers between devices, exchange(): lax.all_to_all(array, FLUID_SOLID, split_axis=0, concat_axis=0, tiled=True)  20 us
    pallas_call x6, Pallas kernels, shell_call(): pl.pallas_call(body, in_specs=in_specs, out_specs=[vmem()] * len(out_shap...  14 us
  transfers between devices with their start and end apart: 3, of which 3 were waited for; matrix products, arithmetic and copies ran while one was open for 1% of the time, Pallas kernels for 0%

profile of v3, /device:TPU:1, one launch (start us, length us, event | category | flops | bytes accessed | tf_op | source)
XLA Modules:
  0.0 308.6 jit_solution(10380372714587540650)
XLA Ops:
  0.7 0.9 convert_reduce_fusion.1
  1.6 0.7 multiply_add_fusion
  2.4 0.8 sub.7
  3.1 11.5 %all-to-all-start = ((s32[128,1,2]{2,1,0:T(1,128)}), s32[128,1,2]{2,1,0:T(1,128)S(1)}, u32[]{:S(2)}, u32[]{:S(2)}) async-start(s32[128,1,2]{2,1,0:T(1,128)} %bitcast.4), calls=%async_computation | async-start | bytes 131072 | tf_op jit(solution)/shard_map/all_to_all | solution.py:409
  14.7 0.7 bitcast_add_fusion.1
  15.4 0.7 fusion.18
  16.1 1.1 copy.36
  17.2 0.2 copy.37
  17.4 1.1 copy.38
  18.5 0.2 copy.39
  18.7 0.2 bitcast_convert_fusion
  18.9 5.4 %all-to-all-done = s32[128,1,2]{2,1,0:T(1,128)S(1)} async-done(((s32[128,1,2]{2,1,0:T(1,128)}), s32[128,1,2]{2,1,0:T(1,128)S(1)}, u32[]{:S(2)}, u32[]{:S(2)}) %all-to-all-start) | async-done | bytes 1056 | tf_op jit(solution)/shard_map/all_to_all | solution.py:409
  24.3 0.2 slice_reduce_fusion.1
  24.8 0.1 reshape.395
  24.9 1.2 convolution_convert_fusion
  26.1 4.4 %all-to-all-start.1 = ((bf16[128,7,2,128]{3,2,1,0:T(2,128)(2,1)}), bf16[128,7,2,128]{3,2,1,0:T(2,128)(2,1)S(1)}, u32[]{:S(2)}, u32[]{:S(2)}) async-start(bf16[128,7,2,128]{3,2,1,0:T(2,128)(2,1)} %bitcast.9), calls=%async_computation.1 | async-start | bytes 917504 | tf_op jit(solution)/shard_map/all_to_all | solution.py:409
  30.5 0.3 fusion.refs_5_.refs_8_.refs_10_.refs_12_.refs_14_.refs_16_
  30.8 13.0 %all-to-all-done.1 = bf16[128,7,2,128]{3,2,1,0:T(2,128)(2,1)S(1)} async-done(((bf16[128,7,2,128]{3,2,1,0:T(2,128)(2,1)}), bf16[128,7,2,128]{3,2,1,0:T(2,128)(2,1)S(1)}, u32[]{:S(2)}, u32[]{:S(2)}) %all-to-all-start.1) | async-done | bytes 458784 | tf_op jit(solution)/shard_map/all_to_all | solution.py:409
  43.8 8.5 %fluid_side.6 = bf16[1536,128]{1,0:T(8,128)(2,1)S(1)} custom-call(s32[2,104]{1,0:T(2,128)S(1)} %pad_add_fusion.refs_0_, bf16[16,1792]{1,0:T(8,128)(2,1)S(1)} %broadcast_in_dim.128.refs_1_, bf16[1792,128]{1,0:T(8,128)(2,1)S(1)} %bitcast.63, bf16[104,256,256]{2,1,0:T(8,128)(2,1)} %refs_11_.3, ...), custom_call_target="tpu_custom_call" | custom-call | tf_op jit(solution)/shard_map/fluid_side/pallas_call | solution.py:205
  52.3 0.7 copy-done.1
  53.0 4.1 %all-to-all-start.2 = ((bf16[128,3,4,128]{3,2,1,0:T(4,128)(2,1)}), bf16[128,3,4,128]{3,2,1,0:T(4,128)(2,1)S(1)}, u32[]{:S(2)}, u32[]{:S(2)}) async-start(bf16[128,3,4,128]{3,2,1,0:T(4,128)(2,1)} %bitcast.87), calls=%async_computation.2 | async-start | bytes 786432 | tf_op jit(solution)/shard_map/all_to_all | solution.py:409
  57.2 12.5 %all-to-all-done.2 = bf16[128,3,4,128]{3,2,1,0:T(4,128)(2,1)S(1)} async-done(((bf16[128,3,4,128]{3,2,1,0:T(4,128)(2,1)}), bf16[128,3,4,128]{3,2,1,0:T(4,128)(2,1)S(1)}, u32[]{:S(2)}, u32[]{:S(2)}) %all-to-all-start.2) | async-done | bytes 393248 | tf_op jit(solution)/shard_map/all_to_all | solution.py:409
  69.7 4.7 %shell_side.6 = (bf16[1792,128]{1,0:T(8,128)(2,1)S(1)}, f32[48,128]{1,0:T(8,128)S(1)}, f32[48,128]{1,0:T(8,128)S(1)}, f32[48,128]{1,0:T(8,128)S(1)}) custom-call(bf16[1536,128]{1,0:T(8,128)(2,1)S(1)} %bitcast.84, f32[48,128]{1,0:T(8,128)S(1)} %get-tuple-element.85.refs_1_, f32[48,128]{1,0:T(8,128)S(1)} %bitcast.91, f32[48,128]{1,0:T(8,128)S(1)} %bitcast.97, ...), custom_call_target="tpu_custom_call" | custom-call | tf_op jit(solution)/shard_map/shell_side/pallas_call | solution.py:338
  74.4 17.2 %all_to_all.74 = bf16[128,7,2,128]{3,2,1,0:T(2,128)(2,1)S(1)} all-to-all(bf16[128,7,2,128]{3,2,1,0:T(2,128)(2,1)S(1)} %bitcast.107), channel_id=1, replica_groups=mesh['fluid_0'=4,'fluid_1'=4,'fluid_2'=2,'solid'=4] {'fluid_0','fluid_1'..., dimensions={0} | all-to-all | bytes 917504 | tf_op jit(solution)/shard_map/all_to_all | solution.py:409
  91.6 9.1 %fluid_side.7 = (bf16[1536,128]{1,0:T(8,128)(2,1)S(1)}, f32[16,128]{1,0:T(8,128)S(1)}, f32[16,128]{1,0:T(8,128)S(1)}) custom-call(s32[2,104]{1,0:T(2,128)S(1)} %pad_add_fusion.refs_0_, bf16[16,1792]{1,0:T(8,128)(2,1)S(1)} %broadcast_in_dim.128.refs_1_, bf16[1792,128]{1,0:T(8,128)(2,1)S(1)} %bitcast.64, bf16[1792,128]{1,0:T(8,128)(2,1)S(1)} %bitcast.69, ...), custom_call_target="tpu_custom_call" | custom-call | tf_op jit(solution)/shard_map/fluid_side/pallas_call | solution.py:205
  100.8 16.5 %all_to_all.75 = bf16[128,3,4,128]{3,2,1,0:T(4,128)(2,1)S(1)} all-to-all(bf16[128,3,4,128]{3,2,1,0:T(4,128)(2,1)S(1)} %bitcast.109), channel_id=1, replica_groups=mesh['fluid_0'=4,'fluid_1'=4,'fluid_2'=2,'solid'=4] {'fluid_0','fluid_1'..., dimensions={0} | all-to-all | bytes 786432 | tf_op jit(solution)/shard_map/all_to_all | solution.py:409
  117.3 1.9 shell_side.7
  119.2 17.2 %all_to_all.76 = bf16[128,7,2,128]{3,2,1,0:T(2,128)(2,1)S(1)} all-to-all(bf16[128,7,2,128]{3,2,1,0:T(2,128)(2,1)S(1)} %bitcast.103), channel_id=1, replica_groups=mesh['fluid_0'=4,'fluid_1'=4,'fluid_2'=2,'solid'=4] {'fluid_0','fluid_1'..., dimensions={0} | all-to-all | bytes 917504 | tf_op jit(solution)/shard_map/all_to_all | solution.py:409
  136.4 7.0 %fluid_side.8 = (bf16[1536,128]{1,0:T(8,128)(2,1)S(1)}, f32[16,128]{1,0:T(8,128)S(1)}, f32[16,128]{1,0:T(8,128)S(1)}) custom-call(s32[2,104]{1,0:T(2,128)S(1)} %pad_add_fusion.refs_0_, bf16[16,1792]{1,0:T(8,128)(2,1)S(1)} %broadcast_in_dim.128.refs_1_, bf16[1792,128]{1,0:T(8,128)(2,1)S(1)} %bitcast.65, bf16[1792,128]{1,0:T(8,128)(2,1)S(1)} %bitcast.70, ...), custom_call_target="tpu_custom_call" | custom-call | tf_op jit(solution)/shard_map/fluid_side/pallas_call | solution.py:205
  143.5 16.5 %all_to_all.77 = bf16[128,3,4,128]{3,2,1,0:T(4,128)(2,1)S(1)} all-to-all(bf16[128,3,4,128]{3,2,1,0:T(4,128)(2,1)S(1)} %bitcast.110), channel_id=1, replica_groups=mesh['fluid_0'=4,'fluid_1'=4,'fluid_2'=2,'solid'=4] {'fluid_0','fluid_1'..., dimensions={0} | all-to-all | bytes 786432 | tf_op jit(solution)/shard_map/all_to_all | solution.py:409
  160.0 1.9 shell_side.8
  161.9 17.2 %all_to_all.78 = bf16[128,7,2,128]{3,2,1,0:T(2,128)(2,1)S(1)} all-to-all(bf16[128,7,2,128]{3,2,1,0:T(2,128)(2,1)S(1)} %bitcast.104), channel_id=1, replica_groups=mesh['fluid_0'=4,'fluid_1'=4,'fluid_2'=2,'solid'=4] {'fluid_0','fluid_1'..., dimensions={0} | all-to-all | bytes 917504 | tf_op jit(solution)/shard_map/all_to_all | solution.py:409
  179.1 7.1 %fluid_side.9 = (bf16[1536,128]{1,0:T(8,128)(2,1)S(1)}, f32[16,128]{1,0:T(8,128)S(1)}, f32[16,128]{1,0:T(8,128)S(1)}) custom-call(s32[2,104]{1,0:T(2,128)S(1)} %pad_add_fusion.refs_0_, bf16[16,1792]{1,0:T(8,128)(2,1)S(1)} %broadcast_in_dim.128.refs_1_, bf16[1792,128]{1,0:T(8,128)(2,1)S(1)} %bitcast.66, bf16[1792,128]{1,0:T(8,128)(2,1)S(1)} %bitcast.71, ...), custom_call_target="tpu_custom_call" | custom-call | tf_op jit(solution)/shard_map/fluid_side/pallas_call | solution.py:205
  186.3 16.5 %all_to_all.79 = bf16[128,3,4,128]{3,2,1,0:T(4,128)(2,1)S(1)} all-to-all(bf16[128,3,4,128]{3,2,1,0:T(4,128)(2,1)S(1)} %bitcast.111), channel_id=1, replica_groups=mesh['fluid_0'=4,'fluid_1'=4,'fluid_2'=2,'solid'=4] {'fluid_0','fluid_1'..., dimensions={0} | all-to-all | bytes 786432 | tf_op jit(solution)/shard_map/all_to_all | solution.py:409
  202.7 1.9 shell_side.9
  204.7 17.2 %all_to_all.80 = bf16[128,7,2,128]{3,2,1,0:T(2,128)(2,1)S(1)} all-to-all(bf16[128,7,2,128]{3,2,1,0:T(2,128)(2,1)S(1)} %bitcast.105), channel_id=1, replica_groups=mesh['fluid_0'=4,'fluid_1'=4,'fluid_2'=2,'solid'=4] {'fluid_0','fluid_1'..., dimensions={0} | all-to-all | bytes 917504 | tf_op jit(solution)/shard_map/all_to_all | solution.py:409
  221.9 7.2 %fluid_side.10 = (bf16[1536,128]{1,0:T(8,128)(2,1)S(1)}, f32[16,128]{1,0:T(8,128)S(1)}, f32[16,128]{1,0:T(8,128)S(1)}) custom-call(s32[2,104]{1,0:T(2,128)S(1)} %pad_add_fusion.refs_0_, bf16[16,1792]{1,0:T(8,128)(2,1)S(1)} %broadcast_in_dim.128.refs_1_, bf16[1792,128]{1,0:T(8,128)(2,1)S(1)} %bitcast.67, bf16[1792,128]{1,0:T(8,128)(2,1)S(1)} %bitcast.72, ...), custom_call_target="tpu_custom_call" | custom-call | tf_op jit(solution)/shard_map/fluid_side/pallas_call | solution.py:205
  229.1 16.5 %all_to_all.81 = bf16[128,3,4,128]{3,2,1,0:T(4,128)(2,1)S(1)} all-to-all(bf16[128,3,4,128]{3,2,1,0:T(4,128)(2,1)S(1)} %bitcast.112), channel_id=1, replica_groups=mesh['fluid_0'=4,'fluid_1'=4,'fluid_2'=2,'solid'=4] {'fluid_0','fluid_1'..., dimensions={0} | all-to-all | bytes 786432 | tf_op jit(solution)/shard_map/all_to_all | solution.py:409
  245.6 1.9 shell_side.10
  247.5 17.2 %all_to_all.82 = bf16[128,7,2,128]{3,2,1,0:T(2,128)(2,1)S(1)} all-to-all(bf16[128,7,2,128]{3,2,1,0:T(2,128)(2,1)S(1)} %bitcast.106), channel_id=1, replica_groups=mesh['fluid_0'=4,'fluid_1'=4,'fluid_2'=2,'solid'=4] {'fluid_0','fluid_1'..., dimensions={0} | all-to-all | bytes 917504 | tf_op jit(solution)/shard_map/all_to_all | solution.py:409
  264.8 8.0 %fluid_side.11 = (bf16[1536,128]{1,0:T(8,128)(2,1)S(1)}, bf16[104,768]{1,0:T(8,128)(2,1)}, f32[16,128]{1,0:T(8,128)S(1)}, f32[16,128]{1,0:T(8,128)S(1)}) custom-call(s32[2,104]{1,0:T(2,128)S(1)} %pad_add_fusion.refs_0_, bf16[16,1792]{1,0:T(8,128)(2,1)S(1)} %broadcast_in_dim.128.refs_1_, bf16[1792,128]{1,0:T(8,128)(2,1)S(1)} %bitcast.68, ...), custom_call_target="tpu_custom_call" | custom-call | tf_op jit(solution)/shard_map/fluid_side/pallas_call | solution.py:205
  272.7 16.5 %all_to_all.83 = bf16[128,3,4,128]{3,2,1,0:T(4,128)(2,1)S(1)} all-to-all(bf16[128,3,4,128]{3,2,1,0:T(4,128)(2,1)S(1)} %bitcast.108), channel_id=1, replica_groups=mesh['fluid_0'=4,'fluid_1'=4,'fluid_2'=2,'solid'=4] {'fluid_0','fluid_1'..., dimensions={0} | all-to-all | bytes 786432 | tf_op jit(solution)/shard_map/all_to_all | solution.py:409
  289.2 1.7 shell_side.11
  290.9 0.6 copy-done.12
  291.6 13.6 %all_to_all.84 = bf16[128,1,128]{2,1,0:T(2,128)(2,1)S(1)} all-to-all(bf16[128,1,128]{2,1,0:T(2,128)(2,1)S(1)} %broadcast_in_dim.147), channel_id=1, replica_groups=mesh['fluid_0'=4,'fluid_1'=4,'fluid_2'=2,'solid'=4] {'fluid_0','fluid_1'..., dimensions={0} | all-to-all | bytes 65536 | tf_op jit(solution)/shard_map/all_to_all | solution.py:409
  305.2 0.5 convert_reduce_fusion
  305.7 1.7 closing.1
  307.5 1.2 slice_bitcast_fusion
  (55 shorter events, 0.7 us)
Async XLA Ops:
  0.6 69.1 %copy-start.2 = (f32[8,768]{1,0:T(8,128)S(1)}, f32[8,768]{1,0:T(8,128)}, u32[]{:S(2)}) copy-start(f32[8,768]{1,0:T(8,128)} %param.15) | copy-start | bytes 73732
  0.6 69.1 %copy-start.4 = (f32[8,768]{1,0:T(8,128)S(1)}, f32[8,768]{1,0:T(8,128)}, u32[]{:S(2)}) copy-start(f32[8,768]{1,0:T(8,128)} %param.14) | copy-start | bytes 73732
  3.1 21.1 %all-to-all-start = ((s32[128,1,2]{2,1,0:T(1,128)}), s32[128,1,2]{2,1,0:T(1,128)S(1)}, u32[]{:S(2)}, u32[]{:S(2)}) async-start(s32[128,1,2]{2,1,0:T(1,128)} %bitcast.4), calls=%async_computation | async-start | bytes 131072 | tf_op jit(solution)/shard_map/all_to_all | solution.py:409
  26.1 17.7 %all-to-all-start.1 = ((bf16[128,7,2,128]{3,2,1,0:T(2,128)(2,1)}), bf16[128,7,2,128]{3,2,1,0:T(2,128)(2,1)S(1)}, u32[]{:S(2)}, u32[]{:S(2)}) async-start(bf16[128,7,2,128]{3,2,1,0:T(2,128)(2,1)} %bitcast.9), calls=%async_computation.1 | async-start | bytes 917504 | tf_op jit(solution)/shard_map/all_to_all | solution.py:409
  52.3 0.7 copy-start.1
  53.0 16.7 %all-to-all-start.2 = ((bf16[128,3,4,128]{3,2,1,0:T(4,128)(2,1)}), bf16[128,3,4,128]{3,2,1,0:T(4,128)(2,1)S(1)}, u32[]{:S(2)}, u32[]{:S(2)}) async-start(bf16[128,3,4,128]{3,2,1,0:T(4,128)(2,1)} %bitcast.87), calls=%async_computation.2 | async-start | bytes 786432 | tf_op jit(solution)/shard_map/all_to_all | solution.py:409
  69.7 47.5 %copy-start = (bf16[8,768,768]{2,1,0:T(8,128)(2,1)S(1)}, bf16[8,768,768]{2,1,0:T(8,128)(2,1)}, u32[]{:S(2)}) copy-start(bf16[8,768,768]{2,1,0:T(8,128)(2,1)} %refs_17_.1) | copy-start | bytes 28311556
  74.4 214.8 %copy-start.3 = (f32[48,128]{1,0:T(8,128)}, f32[48,128]{1,0:T(8,128)S(1)}, u32[]{:S(2)}) copy-start(f32[48,128]{1,0:T(8,128)S(1)} %get-tuple-element.48.refs_4_.refs_5_.refs_6_.refs_7_.refs_8_) | copy-start | bytes 73732
  91.6 44.8 %slice-start = ((s8[13631488]{0:T(1024)(128)(4,1)}), s8[4194304]{0:T(1024)(128)(4,1)S(1)}, s32[]{:S(2)}) async-start(s8[13631488]{0:T(1024)(128)(4,1)} %bitcast.61), calls=%async_computation.14 | async-start | bytes 8388608
  91.6 44.8 %slice-start.1 = ((s8[13631488]{0:T(1024)(128)(4,1)}), s8[4194304]{0:T(1024)(128)(4,1)S(1)}, s32[]{:S(2)}) async-start(s8[13631488]{0:T(1024)(128)(4,1)} %bitcast.61), calls=%async_computation.15 | async-start | bytes 8388608
  91.6 44.8 %slice-start.2 = ((s8[13631488]{0:T(1024)(128)(4,1)}), s8[4194304]{0:T(1024)(128)(4,1)S(1)}, s32[]{:S(2)}) async-start(s8[13631488]{0:T(1024)(128)(4,1)} %bitcast.61), calls=%async_computation.16 | async-start | bytes 8388608
  100.8 16.5 %copy-start.13 = (f32[16,128]{1,0:T(8,128)}, f32[16,128]{1,0:T(8,128)S(1)}, u32[]{:S(2)}) copy-start(f32[16,128]{1,0:T(8,128)S(1)} %get-tuple-element.77.refs_1_) | copy-start | bytes 24580
  117.3 19.2 %slice-start.3 = ((s8[13631488]{0:T(1024)(128)(4,1)}), s8[1048576]{0:T(1024)(128)(4,1)S(1)}, s32[]{:S(2)}) async-start(s8[13631488]{0:T(1024)(128)(4,1)} %bitcast.61), calls=%async_computation.17 | async-start | bytes 2097152
  119.2 170.0 %copy-start.5 = (f32[48,128]{1,0:T(8,128)}, f32[48,128]{1,0:T(8,128)S(1)}, u32[]{:S(2)}) copy-start(f32[48,128]{1,0:T(8,128)S(1)} %get-tuple-element.54.refs_6_.refs_7_.refs_8_.refs_9_) | copy-start | bytes 73732
  143.5 121.3 %copy-start.8 = (f32[16,128]{1,0:T(8,128)}, f32[16,128]{1,0:T(8,128)S(1)}, u32[]{:S(2)}) copy-start(f32[16,128]{1,0:T(8,128)S(1)} %get-tuple-element.56.refs_6_.refs_7_.refs_8_.refs_2_) | copy-start | bytes 24580
  161.9 127.3 %copy-start.6 = (f32[48,128]{1,0:T(8,128)}, f32[48,128]{1,0:T(8,128)S(1)}, u32[]{:S(2)}) copy-start(f32[48,128]{1,0:T(8,128)S(1)} %get-tuple-element.61.refs_8_.refs_9_.refs_10_) | copy-start | bytes 73732
  186.2 78.5 %copy-start.10 = (f32[16,128]{1,0:T(8,128)}, f32[16,128]{1,0:T(8,128)S(1)}, u32[]{:S(2)}) copy-start(f32[16,128]{1,0:T(8,128)S(1)} %get-tuple-element.63.refs_8_.refs_9_.refs_3_) | copy-start | bytes 24580
  204.7 84.6 %copy-start.7 = (f32[48,128]{1,0:T(8,128)}, f32[48,128]{1,0:T(8,128)S(1)}, u32[]{:S(2)}) copy-start(f32[48,128]{1,0:T(8,128)S(1)} %get-tuple-element.68.refs_10_.refs_11_.refs_9_) | copy-start | bytes 73732
  229.1 43.6 %copy-start.11 = (f32[16,128]{1,0:T(8,128)}, f32[16,128]{1,0:T(8,128)S(1)}, u32[]{:S(2)}) copy-start(f32[16,128]{1,0:T(8,128)S(1)} %get-tuple-element.70.refs_10_.refs_4_) | copy-start | bytes 24580
  247.5 43.4 %copy-start.9 = (f32[48,128]{1,0:T(8,128)}, f32[48,128]{1,0:T(8,128)S(1)}, u32[]{:S(2)}) copy-start(f32[48,128]{1,0:T(8,128)S(1)} %get-tuple-element.75.refs_12_.refs_10_) | copy-start | bytes 73732
  272.7 18.8 %copy-start.14 = (f32[16,128]{1,0:T(8,128)}, f32[16,128]{1,0:T(8,128)S(1)}, u32[]{:S(2)}) copy-start(f32[16,128]{1,0:T(8,128)S(1)} %get-tuple-element.78.refs_5_) | copy-start | bytes 24580
  290.9 0.6 copy-start.12

commit v4 on v3

--- a/solution.py
+++ b/solution.py
@@ -30,27 +30,28 @@
 def least_squares(gram, target_side):
     order = len(target_side)
     lower = [[None] * order for _ in range(order)]
+    scale = []
     for row in range(order):
         for column in range(row + 1):
             total = gram[row][column]
             for inner in range(column):
                 total = total - lower[row][inner] * lower[column][inner]
             if row == column:
-                lower[row][row] = jnp.sqrt(total)
+                scale.append(1.0 / jnp.sqrt(total))
             else:
-                lower[row][column] = total / lower[column][column]
+                lower[row][column] = total * scale[column]
     middle = []
     for row in range(order):
         total = target_side[row]
         for inner in range(row):
             total = total - lower[row][inner] * middle[inner]
-        middle.append(total / lower[row][row])
+        middle.append(total * scale[row])
     result = [None] * order
     for row in reversed(range(order)):
         total = middle[row]
         for inner in range(row + 1, order):
             total = total - lower[inner][row] * result[inner]
-        result[row] = total / lower[row][row]
+        result[row] = total * scale[row]
     return result
 
 
@@ -71,6 +72,39 @@
 
 def vmem():
     return pl.BlockSpec(memory_space=pltpu.VMEM)
+
+
+def asking_call(route, slot, devices, chunks):
+    blocks = slot.shape[1]
+
+    def body(route_ref, slot_ref, wanted_ref, places_ref):
+        line = route_ref[...].astype(jnp.float32)
+        down = lax.broadcasted_iota(jnp.int32, (blocks, blocks), 0)
+        across = lax.broadcasted_iota(jnp.int32, (blocks, blocks), 1)
+        wide = jnp.broadcast_to(line, (blocks, blocks))
+        column = jnp.sum(jnp.where(down == across, wide, 0.0), axis=1, keepdims=True)
+        earlier = jnp.where((column == wide) & (down < across), 1.0, 0.0)
+        rank = jnp.sum(earlier, axis=0, keepdims=True)
+        peer = lax.broadcasted_iota(jnp.int32, (devices, blocks), 0).astype(jnp.float32)
+        mine = peer == jnp.broadcast_to(line, (devices, blocks))
+        number = slot_ref[...].astype(jnp.float32) + 1.0
+        for q in range(2):
+            named = jnp.broadcast_to(jnp.where(rank == q, number, 0.0), (devices, blocks))
+            found = jnp.sum(jnp.where(mine, named, 0.0), axis=1, keepdims=True)
+            wanted_ref[:, q : q + 1] = found.astype(jnp.int32) - 1
+        places_ref[0:1, :] = (line * FORTH + rank * chunks).astype(jnp.int32)
+        places_ref[1:2, :] = (line * BACK + rank * chunks).astype(jnp.int32)
+
+    return pl.pallas_call(
+        body,
+        in_specs=[vmem()] * 2,
+        out_specs=[vmem()] * 2,
+        out_shape=[
+            jax.ShapeDtypeStruct((devices, 2), jnp.int32),
+            jax.ShapeDtypeStruct((2, blocks), jnp.int32),
+        ],
+        name="asking",
+    )(route, slot)
 
 
 def fluid_call(places, add_up, messages, sums, rbf_blocks, traction, massive, stream, last):
@@ -84,6 +118,9 @@
     group = next(n for n in (26, 16, 8, 4, 2, 1) if blocks % n == 0)
     lag = min(group, 13)
     steps = blocks // group
+    pieces = [(at * group, group) for at in range(steps)]
+    if blocks == 104:
+        pieces = [(0, 8), (8, 16), (24, 24), (48, 28), (76, 28)]
 
     def body(*refs):
         refs = list(refs)
@@ -99,11 +136,11 @@
         rbf_ref, landed = (refs.pop(0), refs.pop(0)) if stream else (source_ref, None)
 
         def piece(at):
-            rows = pl.ds(at * group, group)
+            rows = pl.ds(*pieces[at])
             return pltpu.make_async_copy(source_ref.at[rows], rbf_ref.at[rows], landed.at[at])
 
         if stream:
-            for at in range(steps):
+            for at in range(len(pieces)):
                 piece(at).start()
 
         weights = []
@@ -159,19 +196,24 @@
                     :3, half * LANES : (half + 1) * LANES
                 ]
 
-        def contract(at, carry):
-            if stream:
+        def contract(first, amount, behind):
+            loads = {}
+            for inner in range(amount + behind):
+                if inner < amount:
+                    loads[inner] = load_of(first + inner)
+                if inner >= behind:
+                    map_back(first + inner - behind, loads.pop(inner - behind))
+
+        def contract_group(at, carry):
+            contract(at * group, group, lag)
+            return carry
+
+        if stream:
+            for at, (first, amount) in enumerate(pieces):
                 piece(at).wait()
-            first = at * group
-            loads = {}
-            for inner in range(group + lag):
-                if inner < group:
-                    loads[inner] = load_of(first + inner)
-                if inner >= lag:
-                    map_back(first + inner - lag, loads.pop(inner - lag))
-            return carry
-
-        lax.fori_loop(0, steps, contract, 0)
+                contract(first, amount, min(amount, lag))
+        else:
+            lax.fori_loop(0, steps, contract_group, 0)
         sending_ref[...] = result_ref[...].astype(jnp.bfloat16)
         if last:
             for at in range(chunks):
@@ -194,7 +236,7 @@
     if stream:
         scratch += [
             pltpu.VMEM(rbf_blocks.shape, rbf_blocks.dtype),
-            pltpu.SemaphoreType.DMA((steps,)),
+            pltpu.SemaphoreType.DMA((len(pieces),)),
         ]
     inputs = (add_up, *messages, *sums, rbf_blocks, traction, massive)
     in_specs = [vmem()] * len(inputs)
@@ -348,18 +390,19 @@
     )(*inputs)
 
 
-def closing_call(line, sums, images, shells, count):
+def closing_call(ending, sums, images, shells, count):
     height = images[0].shape[0]
     chunks = height // shells
     n_sums = len(sums)
 
     def body(*refs):
         refs = list(refs)
-        line_ref = refs.pop(0)
+        ending_ref = refs.pop(0)
         sum_refs = [refs.pop(0) for _ in range(n_sums)]
         image_refs = [refs.pop(0) for _ in range(len(images))]
         current_ref, norm_ref = refs
-        fresh = spread_sums(line_ref[0:1, :])
+        pieces = jnp.sum(ending_ref[...].astype(jnp.float32), axis=0, keepdims=True)
+        fresh = spread_sums(pieces * 0.5)
         every = [ref[...] for ref in sum_refs] + [fresh]
         coefs = solve_coefficients(every[1:])
         moving = image_refs[-1][...]
@@ -367,20 +410,20 @@
             moving = moving + coef * (image_refs[i + 1][...] - image_refs[i][...])
         for t in range(chunks):
             current_ref[:, t * LANES : (t + 1) * LANES] = moving[t * shells : (t + 1) * shells]
-        lane = lax.broadcasted_iota(jnp.int32, (1, LANES), 1)
-        squares = jnp.zeros((1, LANES), jnp.float32)
         for i, part in enumerate(every):
-            squares = jnp.where(lane == i, part[SQUARES_AT : SQUARES_AT + 1], squares)
-        norm_ref[...] = jnp.sqrt(squares / count + EPSILON)
+            norm = jnp.sqrt(part[SQUARES_AT : SQUARES_AT + 1] / count + EPSILON)
+            norm_ref[i] = norm[0, 0]
 
     return pl.pallas_call(
         body,
+        in_specs=[vmem()] * (1 + n_sums + len(images)),
+        out_specs=[vmem(), pl.BlockSpec(memory_space=pltpu.SMEM)],
         out_shape=[
             jax.ShapeDtypeStruct((shells, chunks * LANES), jnp.float32),
-            jax.ShapeDtypeStruct((1, LANES), jnp.float32),
+            jax.ShapeDtypeStruct((n_sums + 1,), jnp.float32),
         ],
         name="closing",
-    )(line, *sums, *images)
+    )(ending, *sums, *images)
 
 
 def spread_components(array, blocks, nodes):
@@ -412,20 +455,12 @@
         moved = exchange(buffer.reshape(devices, -1, part, LANES))
         return moved.reshape(-1, LANES)
 
-    destination = route[:, 0]
-    block_order = jnp.arange(blocks, dtype=jnp.int32)
-    earlier = (destination[:, None] == destination[None, :]) & (
-        block_order[None, :] < block_order[:, None]
+    start = by_chunks(shell_start, shells)
+    start_half = start.astype(jnp.bfloat16)
+    wanted, places = asking_call(
+        route.reshape(1, blocks), slot.reshape(1, blocks), devices, chunks
     )
-    slot_rank = jnp.sum(earlier.astype(jnp.int32), axis=1)
-    position = destination * capacity + slot_rank
-    positions = jnp.arange(devices * capacity, dtype=jnp.int32)
-    placing = positions[:, None] == position[None, :]
-    wanted = jnp.max(jnp.where(placing, slot[None, :] + 1, 0), axis=1) - 1
-    asked = exchange(wanted.reshape(devices, capacity))
-    places = jnp.stack(
-        [destination * FORTH + slot_rank * chunks, destination * BACK + slot_rank * chunks]
-    )
+    asked = exchange(wanted.reshape(devices, 1, capacity)).reshape(devices, capacity)
 
     stacked = jnp.arange(height + ROWS, dtype=jnp.int32)
 
@@ -444,10 +479,8 @@
 
     traction = spread_components(fluid_traction, blocks, nodes)
     massive = spread_components(fluid_mass, blocks, nodes)
-    start = by_chunks(shell_start, shells)
     robin = by_chunks(robin_coef, shells)
 
-    start_half = start.astype(jnp.bfloat16)
     shown = start_half.astype(jnp.float32)
     outgoing = jnp.dot(
         pick, jnp.pad(start_half, ((0, ROWS), (0, 0))), preferred_element_type=jnp.float32
@@ -492,10 +525,9 @@
         if not last:
             residuals.append(made[2])
             shown = made[3]
-    ending = exchange(jnp.broadcast_to(outgoing[:1], (devices, 1, LANES)))
-    line = jnp.sum(ending.astype(jnp.float32), axis=0)
-    current, norms = closing_call(line, sums, images, shells, count)
-    return (current, last_load, norms[0, :ITERS])
+    ending = transport(jnp.broadcast_to(outgoing[:1], (devices * 2, LANES)), 2)
+    current, norms = closing_call(ending, sums, images, shells, count)
+    return (current, last_load, norms)
 
 
 def solution(mesh):

time: 309 us -> 306 us (level)
  no operation moved by 1% of the time
where the time goes in v4:
time: 306 us; the launch traced here: 305 us
  blocking collectives  183 us (60%)
  Pallas kernels  62.9 us (21%)
  waiting for transfers between devices  31.5 us (10%)
  starting transfers between devices  19.9 us (7%)
  local copies, waits for them, and re-layouts  4.46 us (1%)
    all_to_all x11, blocking collectives, exchange(): lax.all_to_all(array, FLUID_SOLID, split_axis=0, concat_axis=0, tiled=True)  183 us
    pallas_call x6, Pallas kernels, fluid_call(): pl.pallas_call(body, in_specs=[pl.BlockSpec(memory_space=pltpu.SMEM)] + i...  45.6 us
    all_to_all x3, waiting for transfers between devices, exchange(): lax.all_to_all(array, FLUID_SOLID, split_axis=0, concat_axis=0, tiled=True)  31.5 us
    all_to_all x3, starting transfers between devices, exchange(): lax.all_to_all(array, FLUID_SOLID, split_axis=0, concat_axis=0, tiled=True)  19.9 us
    pallas_call x6, Pallas kernels, shell_call(): pl.pallas_call(body, in_specs=in_specs, out_specs=[vmem()] * len(out_shap...  14 us
  transfers between devices with their start and end apart: 3, of which 3 were waited for; matrix products, arithmetic and copies ran while one was open for 1% of the time, Pallas kernels for 0%

profile of v4, /device:TPU:1, one launch (start us, length us, event | category | flops | bytes accessed | tf_op | source)
XLA Modules:
  0.0 305.2 jit_solution(10319152825755008113)
XLA Ops:
  0.6 0.0 copy-start.2
  0.7 1.5 asking.1
  2.2 11.5 %all-to-all-start = ((s32[128,1,2]{2,1,0:T(1,128)}), s32[128,1,2]{2,1,0:T(1,128)S(1)}, u32[]{:S(2)}, u32[]{:S(2)}) async-start(s32[128,1,2]{2,1,0:T(1,128)} %bitcast.110), calls=%async_computation | async-start | bytes 131072 | tf_op jit(solution)/shard_map/all_to_all | solution.py:452
  13.8 0.7 fusion.17
  14.5 1.1 copy.21
  15.6 0.2 copy.22
  15.8 1.1 copy.23
  16.9 0.2 copy.24
  17.0 0.2 bitcast_convert_fusion
  17.2 6.1 %all-to-all-done = s32[128,1,2]{2,1,0:T(1,128)S(1)} async-done(((s32[128,1,2]{2,1,0:T(1,128)}), s32[128,1,2]{2,1,0:T(1,128)S(1)}, u32[]{:S(2)}, u32[]{:S(2)}) %all-to-all-start) | async-done | bytes 1056 | tf_op jit(solution)/shard_map/all_to_all | solution.py:452
  23.3 0.2 slice_reduce_fusion.1
  23.5 0.1 fusion.5
  23.6 0.1 reshape.353
  23.7 0.1 fusion.3
  23.8 0.1 reshape.347
  23.9 1.2 convolution_convert_fusion
  25.1 4.3 %all-to-all-start.1 = ((bf16[128,7,2,128]{3,2,1,0:T(2,128)(2,1)}), bf16[128,7,2,128]{3,2,1,0:T(2,128)(2,1)S(1)}, u32[]{:S(2)}, u32[]{:S(2)}) async-start(bf16[128,7,2,128]{3,2,1,0:T(2,128)(2,1)} %bitcast.8), calls=%async_computation.1 | async-start | bytes 917504 | tf_op jit(solution)/shard_map/all_to_all | solution.py:452
  29.4 0.3 fusion.refs_5_.refs_8_.refs_10_.refs_12_.refs_14_.refs_16_
  29.7 13.0 %all-to-all-done.1 = bf16[128,7,2,128]{3,2,1,0:T(2,128)(2,1)S(1)} async-done(((bf16[128,7,2,128]{3,2,1,0:T(2,128)(2,1)}), bf16[128,7,2,128]{3,2,1,0:T(2,128)(2,1)S(1)}, u32[]{:S(2)}, u32[]{:S(2)}) %all-to-all-start.1) | async-done | bytes 458784 | tf_op jit(solution)/shard_map/all_to_all | solution.py:452
  42.7 0.7 copy-done.11
  43.4 8.0 %fluid_side.6 = bf16[1536,128]{1,0:T(8,128)(2,1)S(1)} custom-call(s32[2,104]{1,0:T(2,128)S(1)} %copy-done.11, bf16[16,1792]{1,0:T(8,128)(2,1)S(1)} %broadcast_in_dim.113.refs_1_, bf16[1792,128]{1,0:T(8,128)(2,1)S(1)} %bitcast.56, bf16[104,256,256]{2,1,0:T(8,128)(2,1)} %refs_11_.3, ...), custom_call_target="tpu_custom_call" | custom-call | tf_op jit(solution)/shard_map/fluid_side/pallas_call | solution.py:247
  51.4 0.7 copy-done.1
  52.1 4.1 %all-to-all-start.2 = ((bf16[128,3,4,128]{3,2,1,0:T(4,128)(2,1)}), bf16[128,3,4,128]{3,2,1,0:T(4,128)(2,1)S(1)}, u32[]{:S(2)}, u32[]{:S(2)}) async-start(bf16[128,3,4,128]{3,2,1,0:T(4,128)(2,1)} %bitcast.80), calls=%async_computation.2 | async-start | bytes 786432 | tf_op jit(solution)/shard_map/all_to_all | solution.py:452
  56.2 0.1 compare_convert_fusion.refs_4_.refs_7_.refs_9_.refs_11_.refs_13_.refs_15_
  56.3 12.5 %all-to-all-done.2 = bf16[128,3,4,128]{3,2,1,0:T(4,128)(2,1)S(1)} async-done(((bf16[128,3,4,128]{3,2,1,0:T(4,128)(2,1)}), bf16[128,3,4,128]{3,2,1,0:T(4,128)(2,1)S(1)}, u32[]{:S(2)}, u32[]{:S(2)}) %all-to-all-start.2) | async-done | bytes 393248 | tf_op jit(solution)/shard_map/all_to_all | solution.py:452
  68.8 4.7 %shell_side.6 = (bf16[1792,128]{1,0:T(8,128)(2,1)S(1)}, f32[48,128]{1,0:T(8,128)S(1)}, f32[48,128]{1,0:T(8,128)S(1)}, f32[48,128]{1,0:T(8,128)S(1)}) custom-call(bf16[1536,128]{1,0:T(8,128)(2,1)S(1)} %bitcast.77, f32[48,128]{1,0:T(8,128)S(1)} %get-tuple-element.89.refs_1_, f32[48,128]{1,0:T(8,128)S(1)} %bitcast.84, f32[48,128]{1,0:T(8,128)S(1)} %bitcast.90, ...), custom_call_target="tpu_custom_call" | custom-call | tf_op jit(solution)/shard_map/shell_side/pallas_call | solution.py:380
  73.5 17.2 %all_to_all.70 = bf16[128,7,2,128]{3,2,1,0:T(2,128)(2,1)S(1)} all-to-all(bf16[128,7,2,128]{3,2,1,0:T(2,128)(2,1)S(1)} %bitcast.100), channel_id=1, replica_groups=mesh['fluid_0'=4,'fluid_1'=4,'fluid_2'=2,'solid'=4] {'fluid_0','fluid_1'..., dimensions={0} | all-to-all | bytes 917504 | tf_op jit(solution)/shard_map/all_to_all | solution.py:452
  90.7 8.2 %fluid_side.7 = (bf16[1536,128]{1,0:T(8,128)(2,1)S(1)}, f32[16,128]{1,0:T(8,128)S(1)}, f32[16,128]{1,0:T(8,128)S(1)}) custom-call(s32[2,104]{1,0:T(2,128)S(1)} %copy-done.12, bf16[16,1792]{1,0:T(8,128)(2,1)S(1)} %broadcast_in_dim.113.refs_1_, bf16[1792,128]{1,0:T(8,128)(2,1)S(1)} %bitcast.57, bf16[1792,128]{1,0:T(8,128)(2,1)S(1)} %bitcast.62, ...), custom_call_target="tpu_custom_call" | custom-call | tf_op jit(solution)/shard_map/fluid_side/pallas_call | solution.py:247
  98.9 16.5 %all_to_all.71 = bf16[128,3,4,128]{3,2,1,0:T(4,128)(2,1)S(1)} all-to-all(bf16[128,3,4,128]{3,2,1,0:T(4,128)(2,1)S(1)} %bitcast.102), channel_id=1, replica_groups=mesh['fluid_0'=4,'fluid_1'=4,'fluid_2'=2,'solid'=4] {'fluid_0','fluid_1'..., dimensions={0} | all-to-all | bytes 786432 | tf_op jit(solution)/shard_map/all_to_all | solution.py:452
  115.4 1.9 shell_side.7
  117.4 17.2 %all_to_all.72 = bf16[128,7,2,128]{3,2,1,0:T(2,128)(2,1)S(1)} all-to-all(bf16[128,7,2,128]{3,2,1,0:T(2,128)(2,1)S(1)} %bitcast.96), channel_id=1, replica_groups=mesh['fluid_0'=4,'fluid_1'=4,'fluid_2'=2,'solid'=4] {'fluid_0','fluid_1'..., dimensions={0} | all-to-all | bytes 917504 | tf_op jit(solution)/shard_map/all_to_all | solution.py:452
  134.6 7.0 %fluid_side.8 = (bf16[1536,128]{1,0:T(8,128)(2,1)S(1)}, f32[16,128]{1,0:T(8,128)S(1)}, f32[16,128]{1,0:T(8,128)S(1)}) custom-call(s32[2,104]{1,0:T(2,128)S(1)} %copy-done.12, bf16[16,1792]{1,0:T(8,128)(2,1)S(1)} %broadcast_in_dim.113.refs_1_, bf16[1792,128]{1,0:T(8,128)(2,1)S(1)} %bitcast.58, bf16[1792,128]{1,0:T(8,128)(2,1)S(1)} %bitcast.63, ...), custom_call_target="tpu_custom_call" | custom-call | tf_op jit(solution)/shard_map/fluid_side/pallas_call | solution.py:247
  141.7 16.5 %all_to_all.73 = bf16[128,3,4,128]{3,2,1,0:T(4,128)(2,1)S(1)} all-to-all(bf16[128,3,4,128]{3,2,1,0:T(4,128)(2,1)S(1)} %bitcast.103), channel_id=1, replica_groups=mesh['fluid_0'=4,'fluid_1'=4,'fluid_2'=2,'solid'=4] {'fluid_0','fluid_1'..., dimensions={0} | all-to-all | bytes 786432 | tf_op jit(solution)/shard_map/all_to_all | solution.py:452
  158.2 1.9 shell_side.8
  160.1 17.2 %all_to_all.74 = bf16[128,7,2,128]{3,2,1,0:T(2,128)(2,1)S(1)} all-to-all(bf16[128,7,2,128]{3,2,1,0:T(2,128)(2,1)S(1)} %bitcast.97), channel_id=1, replica_groups=mesh['fluid_0'=4,'fluid_1'=4,'fluid_2'=2,'solid'=4] {'fluid_0','fluid_1'..., dimensions={0} | all-to-all | bytes 917504 | tf_op jit(solution)/shard_map/all_to_all | solution.py:452
  177.3 7.1 %fluid_side.9 = (bf16[1536,128]{1,0:T(8,128)(2,1)S(1)}, f32[16,128]{1,0:T(8,128)S(1)}, f32[16,128]{1,0:T(8,128)S(1)}) custom-call(s32[2,104]{1,0:T(2,128)S(1)} %copy-done.12, bf16[16,1792]{1,0:T(8,128)(2,1)S(1)} %broadcast_in_dim.113.refs_1_, bf16[1792,128]{1,0:T(8,128)(2,1)S(1)} %bitcast.59, bf16[1792,128]{1,0:T(8,128)(2,1)S(1)} %bitcast.64, ...), custom_call_target="tpu_custom_call" | custom-call | tf_op jit(solution)/shard_map/fluid_side/pallas_call | solution.py:247
  184.5 16.5 %all_to_all.75 = bf16[128,3,4,128]{3,2,1,0:T(4,128)(2,1)S(1)} all-to-all(bf16[128,3,4,128]{3,2,1,0:T(4,128)(2,1)S(1)} %bitcast.104), channel_id=1, replica_groups=mesh['fluid_0'=4,'fluid_1'=4,'fluid_2'=2,'solid'=4] {'fluid_0','fluid_1'..., dimensions={0} | all-to-all | bytes 786432 | tf_op jit(solution)/shard_map/all_to_all | solution.py:452
  201.0 1.9 shell_side.9
  202.9 17.2 %all_to_all.76 = bf16[128,7,2,128]{3,2,1,0:T(2,128)(2,1)S(1)} all-to-all(bf16[128,7,2,128]{3,2,1,0:T(2,128)(2,1)S(1)} %bitcast.98), channel_id=1, replica_groups=mesh['fluid_0'=4,'fluid_1'=4,'fluid_2'=2,'solid'=4] {'fluid_0','fluid_1'..., dimensions={0} | all-to-all | bytes 917504 | tf_op jit(solution)/shard_map/all_to_all | solution.py:452
  220.1 7.2 %fluid_side.10 = (bf16[1536,128]{1,0:T(8,128)(2,1)S(1)}, f32[16,128]{1,0:T(8,128)S(1)}, f32[16,128]{1,0:T(8,128)S(1)}) custom-call(s32[2,104]{1,0:T(2,128)S(1)} %copy-done.12, bf16[16,1792]{1,0:T(8,128)(2,1)S(1)} %broadcast_in_dim.113.refs_1_, bf16[1792,128]{1,0:T(8,128)(2,1)S(1)} %bitcast.60, bf16[1792,128]{1,0:T(8,128)(2,1)S(1)} %bitcast.65, ...), custom_call_target="tpu_custom_call" | custom-call | tf_op jit(solution)/shard_map/fluid_side/pallas_call | solution.py:247
  227.4 16.5 %all_to_all.77 = bf16[128,3,4,128]{3,2,1,0:T(4,128)(2,1)S(1)} all-to-all(bf16[128,3,4,128]{3,2,1,0:T(4,128)(2,1)S(1)} %bitcast.105), channel_id=1, replica_groups=mesh['fluid_0'=4,'fluid_1'=4,'fluid_2'=2,'solid'=4] {'fluid_0','fluid_1'..., dimensions={0} | all-to-all | bytes 786432 | tf_op jit(solution)/shard_map/all_to_all | solution.py:452
  243.9 1.9 shell_side.10
  245.8 17.2 %all_to_all.78 = bf16[128,7,2,128]{3,2,1,0:T(2,128)(2,1)S(1)} all-to-all(bf16[128,7,2,128]{3,2,1,0:T(2,128)(2,1)S(1)} %bitcast.99), channel_id=1, replica_groups=mesh['fluid_0'=4,'fluid_1'=4,'fluid_2'=2,'solid'=4] {'fluid_0','fluid_1'..., dimensions={0} | all-to-all | bytes 917504 | tf_op jit(solution)/shard_map/all_to_all | solution.py:452
  263.0 8.0 %fluid_side.11 = (bf16[1536,128]{1,0:T(8,128)(2,1)S(1)}, bf16[104,768]{1,0:T(8,128)(2,1)}, f32[16,128]{1,0:T(8,128)S(1)}, f32[16,128]{1,0:T(8,128)S(1)}) custom-call(s32[2,104]{1,0:T(2,128)S(1)} %copy-done.12, bf16[16,1792]{1,0:T(8,128)(2,1)S(1)} %broadcast_in_dim.113.refs_1_, bf16[1792,128]{1,0:T(8,128)(2,1)S(1)} %bitcast.61, ...), custom_call_target="tpu_custom_call" | custom-call | tf_op jit(solution)/shard_map/fluid_side/pallas_call | solution.py:247
  271.0 16.5 %all_to_all.79 = bf16[128,3,4,128]{3,2,1,0:T(4,128)(2,1)S(1)} all-to-all(bf16[128,3,4,128]{3,2,1,0:T(4,128)(2,1)S(1)} %bitcast.101), channel_id=1, replica_groups=mesh['fluid_0'=4,'fluid_1'=4,'fluid_2'=2,'solid'=4] {'fluid_0','fluid_1'..., dimensions={0} | all-to-all | bytes 786432 | tf_op jit(solution)/shard_map/all_to_all | solution.py:452
  287.5 1.7 shell_side.11
  289.2 14.0 %all_to_all.80 = bf16[128,1,2,128]{3,2,1,0:T(2,128)(2,1)} all-to-all(bf16[128,1,2,128]{3,2,1,0:T(2,128)(2,1)S(1)} %reshape.344), channel_id=1, replica_groups=mesh['fluid_0'=4,'fluid_1'=4,'fluid_2'=2,'solid'=4] {'fluid_0','fluid_1'..., dimensions={0} | all-to-all | bytes 131072 | tf_op jit(solution)/shard_map/all_to_all | solution.py:452
  303.2 1.8 closing.1
  (51 shorter events, 0.2 us)
Async XLA Ops:
  0.6 68.1 %copy-start.2 = (f32[8,768]{1,0:T(8,128)S(1)}, f32[8,768]{1,0:T(8,128)}, u32[]{:S(2)}) copy-start(f32[8,768]{1,0:T(8,128)} %param.15) | copy-start | bytes 73732
  0.6 68.1 %copy-start.4 = (f32[8,768]{1,0:T(8,128)S(1)}, f32[8,768]{1,0:T(8,128)}, u32[]{:S(2)}) copy-start(f32[8,768]{1,0:T(8,128)} %param.14) | copy-start | bytes 73732
  2.2 21.1 %all-to-all-start = ((s32[128,1,2]{2,1,0:T(1,128)}), s32[128,1,2]{2,1,0:T(1,128)S(1)}, u32[]{:S(2)}, u32[]{:S(2)}) async-start(s32[128,1,2]{2,1,0:T(1,128)} %bitcast.110), calls=%async_computation | async-start | bytes 131072 | tf_op jit(solution)/shard_map/all_to_all | solution.py:452
  25.1 17.5 %all-to-all-start.1 = ((bf16[128,7,2,128]{3,2,1,0:T(2,128)(2,1)}), bf16[128,7,2,128]{3,2,1,0:T(2,128)(2,1)S(1)}, u32[]{:S(2)}, u32[]{:S(2)}) async-start(bf16[128,7,2,128]{3,2,1,0:T(2,128)(2,1)} %bitcast.8), calls=%async_computation.1 | async-start | bytes 917504 | tf_op jit(solution)/shard_map/all_to_all | solution.py:452
  42.7 0.7 copy-start.11
  43.4 47.3 %copy-start.12 = (s32[2,104]{1,0:T(2,128)S(1)}, s32[2,104]{1,0:T(2,128)}, u32[]{:S(2)}) copy-start(s32[2,104]{1,0:T(2,128)} %get-tuple-element.45.refs_0_) | copy-start | bytes 2500
  51.3 0.7 copy-start.1
  52.1 16.7 %all-to-all-start.2 = ((bf16[128,3,4,128]{3,2,1,0:T(4,128)(2,1)}), bf16[128,3,4,128]{3,2,1,0:T(4,128)(2,1)S(1)}, u32[]{:S(2)}, u32[]{:S(2)}) async-start(bf16[128,3,4,128]{3,2,1,0:T(4,128)(2,1)} %bitcast.80), calls=%async_computation.2 | async-start | bytes 786432 | tf_op jit(solution)/shard_map/all_to_all | solution.py:452
  68.8 46.7 %copy-start = (bf16[8,768,768]{2,1,0:T(8,128)(2,1)S(1)}, bf16[8,768,768]{2,1,0:T(8,128)(2,1)}, u32[]{:S(2)}) copy-start(bf16[8,768,768]{2,1,0:T(8,128)(2,1)} %refs_17_.1) | copy-start | bytes 28311556
  73.5 214.0 %copy-start.3 = (f32[48,128]{1,0:T(8,128)}, f32[48,128]{1,0:T(8,128)S(1)}, u32[]{:S(2)}) copy-start(f32[48,128]{1,0:T(8,128)S(1)} %get-tuple-element.52.refs_4_.refs_5_.refs_6_.refs_7_.refs_8_) | copy-start | bytes 73732
  90.7 43.9 %slice-start = ((s8[13631488]{0:T(1024)(128)(4,1)}), s8[4194304]{0:T(1024)(128)(4,1)S(1)}, s32[]{:S(2)}) async-start(s8[13631488]{0:T(1024)(128)(4,1)} %bitcast.54), calls=%async_computation.14 | async-start | bytes 8388608
  90.7 43.9 %slice-start.1 = ((s8[13631488]{0:T(1024)(128)(4,1)}), s8[4194304]{0:T(1024)(128)(4,1)S(1)}, s32[]{:S(2)}) async-start(s8[13631488]{0:T(1024)(128)(4,1)} %bitcast.54), calls=%async_computation.15 | async-start | bytes 8388608
  90.7 43.9 %slice-start.2 = ((s8[13631488]{0:T(1024)(128)(4,1)}), s8[4194304]{0:T(1024)(128)(4,1)S(1)}, s32[]{:S(2)}) async-start(s8[13631488]{0:T(1024)(128)(4,1)} %bitcast.54), calls=%async_computation.16 | async-start | bytes 8388608
  98.9 42.7 %copy-start.15 = (f32[16,128]{1,0:T(8,128)}, f32[16,128]{1,0:T(8,128)S(1)}, u32[]{:S(2)}) copy-start(f32[16,128]{1,0:T(8,128)S(1)} %get-tuple-element.81.refs_1_) | copy-start | bytes 24580
  115.4 19.2 %slice-start.3 = ((s8[13631488]{0:T(1024)(128)(4,1)}), s8[1048576]{0:T(1024)(128)(4,1)S(1)}, s32[]{:S(2)}) async-start(s8[13631488]{0:T(1024)(128)(4,1)} %bitcast.54), calls=%async_computation.17 | async-start | bytes 2097152
  117.4 170.1 %copy-start.5 = (f32[48,128]{1,0:T(8,128)}, f32[48,128]{1,0:T(8,128)S(1)}, u32[]{:S(2)}) copy-start(f32[48,128]{1,0:T(8,128)S(1)} %get-tuple-element.58.refs_6_.refs_7_.refs_8_.refs_9_) | copy-start | bytes 73732
  141.7 121.3 %copy-start.8 = (f32[16,128]{1,0:T(8,128)}, f32[16,128]{1,0:T(8,128)S(1)}, u32[]{:S(2)}) copy-start(f32[16,128]{1,0:T(8,128)S(1)} %get-tuple-element.60.refs_6_.refs_7_.refs_8_.refs_2_) | copy-start | bytes 24580
  160.1 127.4 %copy-start.6 = (f32[48,128]{1,0:T(8,128)}, f32[48,128]{1,0:T(8,128)S(1)}, u32[]{:S(2)}) copy-start(f32[48,128]{1,0:T(8,128)S(1)} %get-tuple-element.65.refs_8_.refs_9_.refs_10_) | copy-start | bytes 73732
  184.5 78.5 %copy-start.10 = (f32[16,128]{1,0:T(8,128)}, f32[16,128]{1,0:T(8,128)S(1)}, u32[]{:S(2)}) copy-start(f32[16,128]{1,0:T(8,128)S(1)} %get-tuple-element.67.refs_8_.refs_9_.refs_3_) | copy-start | bytes 24580
  202.9 84.6 %copy-start.7 = (f32[48,128]{1,0:T(8,128)}, f32[48,128]{1,0:T(8,128)S(1)}, u32[]{:S(2)}) copy-start(f32[48,128]{1,0:T(8,128)S(1)} %get-tuple-element.72.refs_10_.refs_11_.refs_9_) | copy-start | bytes 73732
  227.4 43.6 %copy-start.13 = (f32[16,128]{1,0:T(8,128)}, f32[16,128]{1,0:T(8,128)S(1)}, u32[]{:S(2)}) copy-start(f32[16,128]{1,0:T(8,128)S(1)} %get-tuple-element.74.refs_10_.refs_4_) | copy-start | bytes 24580
  245.8 43.4 %copy-start.9 = (f32[48,128]{1,0:T(8,128)}, f32[48,128]{1,0:T(8,128)S(1)}, u32[]{:S(2)}) copy-start(f32[48,128]{1,0:T(8,128)S(1)} %get-tuple-element.79.refs_12_.refs_10_) | copy-start | bytes 73732
  271.0 18.2 %copy-start.16 = (f32[16,128]{1,0:T(8,128)}, f32[16,128]{1,0:T(8,128)S(1)}, u32[]{:S(2)}) copy-start(f32[16,128]{1,0:T(8,128)S(1)} %get-tuple-element.82.refs_5_) | copy-start | bytes 24580
  289.2 14.1 %copy-start.14 = (f32[48,128]{1,0:T(8,128)}, f32[48,128]{1,0:T(8,128)S(1)}, u32[]{:S(2)}) copy-start(f32[48,128]{1,0:T(8,128)S(1)} %get-tuple-element.83.refs_11_) | copy-start | bytes 73732

commit v5 on v4

--- a/solution.py
+++ b/solution.py
@@ -24,7 +24,7 @@
 BACK = 12
 FOLD = 256
 FLUID_STREAMS = 2
-SHELL_STREAMS = 1
+SHELL_STREAMS = 2
 
 
 def least_squares(gram, target_side):
@@ -74,46 +74,19 @@
     return pl.BlockSpec(memory_space=pltpu.VMEM)
 
 
-def asking_call(route, slot, devices, chunks):
-    blocks = slot.shape[1]
-
-    def body(route_ref, slot_ref, wanted_ref, places_ref):
-        line = route_ref[...].astype(jnp.float32)
-        down = lax.broadcasted_iota(jnp.int32, (blocks, blocks), 0)
-        across = lax.broadcasted_iota(jnp.int32, (blocks, blocks), 1)
-        wide = jnp.broadcast_to(line, (blocks, blocks))
-        column = jnp.sum(jnp.where(down == across, wide, 0.0), axis=1, keepdims=True)
-        earlier = jnp.where((column == wide) & (down < across), 1.0, 0.0)
-        rank = jnp.sum(earlier, axis=0, keepdims=True)
-        peer = lax.broadcasted_iota(jnp.int32, (devices, blocks), 0).astype(jnp.float32)
-        mine = peer == jnp.broadcast_to(line, (devices, blocks))
-        number = slot_ref[...].astype(jnp.float32) + 1.0
-        for q in range(2):
-            named = jnp.broadcast_to(jnp.where(rank == q, number, 0.0), (devices, blocks))
-            found = jnp.sum(jnp.where(mine, named, 0.0), axis=1, keepdims=True)
-            wanted_ref[:, q : q + 1] = found.astype(jnp.int32) - 1
-        places_ref[0:1, :] = (line * FORTH + rank * chunks).astype(jnp.int32)
-        places_ref[1:2, :] = (line * BACK + rank * chunks).astype(jnp.int32)
-
-    return pl.pallas_call(
-        body,
-        in_specs=[vmem()] * 2,
-        out_specs=[vmem()] * 2,
-        out_shape=[
-            jax.ShapeDtypeStruct((devices, 2), jnp.int32),
-            jax.ShapeDtypeStruct((2, blocks), jnp.int32),
-        ],
-        name="asking",
-    )(route, slot)
-
-
-def fluid_call(places, add_up, messages, sums, rbf_blocks, traction, massive, stream, last):
+def fluid_call(
+    places, add_up, messages, sums, rbf_blocks, traction, massive, shells, stream, last
+):
     blocks, nodes, _ = rbf_blocks.shape
-    rows_all = messages[0].shape[0]
+    rows_all = messages[-1].shape[0]
     chunks = 3 * nodes // LANES
     halves = nodes // LANES
-    rows_back = add_up.shape[1] // FORTH * BACK
     k = len(messages) - 1
+    first_time = k == 0
+    devices = rows_all // (chunks * shells if first_time else FORTH)
+    rows_back = devices * (FORTH if first_time else BACK)
+    apart = shells if first_time else 1
+    over = 16 * apart
     n_sums = len(sums)
     group = next(n for n in (26, 16, 8, 4, 2, 1) if blocks % n == 0)
     lag = min(group, 13)
@@ -124,15 +97,19 @@
 
     def body(*refs):
         refs = list(refs)
-        place_ref, add_ref = refs.pop(0), refs.pop(0)
+        place_ref = refs.pop(0)
+        add_ref = None if first_time else refs.pop(0)
+        slot_ref = refs.pop(0) if first_time else None
         message_refs = [refs.pop(0) for _ in range(k + 1)]
         sum_refs = [refs.pop(0) for _ in range(n_sums)]
         source_ref, traction_ref, mass_ref = refs.pop(0), refs.pop(0), refs.pop(0)
         sending_ref = refs.pop(0)
         load_ref = refs.pop(0) if last else None
+        start_out = refs.pop(0) if first_time else None
         sums_out, coefs_out = (refs.pop(0), refs.pop(0)) if k else (None, None)
         shown_ref, result_ref = refs.pop(0), refs.pop(0)
         kept_ref = refs.pop(0) if last else None
+        begun_ref = refs.pop(0) if first_time else None
         rbf_ref, landed = (refs.pop(0), refs.pop(0)) if stream else (source_ref, None)
 
         def piece(at):
@@ -168,15 +145,22 @@
             return carry
 
         lax.fori_loop(0, rows_all // FOLD, show, 0)
-        shown_ref[rows_all:, :] = jnp.zeros((16, LANES), jnp.float32)
+        shown_ref[rows_all:, :] = jnp.zeros((over, LANES), jnp.float32)
         result_ref[...] = jnp.zeros_like(result_ref)
+        if first_time:
+            begun_ref[...] = jnp.zeros_like(begun_ref)
 
         def load_of(block):
             spot = place_ref[0, block]
-            shown = jnp.concatenate(
-                [shown_ref[pl.ds(spot + half, 8, stride=halves), :] for half in range(halves)],
-                axis=1,
-            ).astype(jnp.bfloat16)
+            rows = [
+                shown_ref[pl.ds(spot + half * apart, 8, stride=halves * apart), :]
+                for half in range(halves)
+            ]
+            if first_time:
+                again = place_ref[2, block]
+                for half in range(halves):
+                    begun_ref[pl.ds(again + half, 3, stride=halves), :] = rows[half][:3]
+            shown = jnp.concatenate(rows, axis=1).astype(jnp.bfloat16)
             moved = lax.dot_general(
                 shown, rbf_ref[block], (((1,), (1,)), ((), ())), preferred_element_type=jnp.float32
             )
@@ -214,6 +198,9 @@
                 contract(first, amount, min(amount, lag))
         else:
             lax.fori_loop(0, steps, contract_group, 0)
+        if first_time:
+            start_out[...] = begun_ref[...].astype(jnp.bfloat16)
+            result_ref[pl.ds(2 * chunks, devices, stride=FORTH), :] = slot_ref[...]
         sending_ref[...] = result_ref[...].astype(jnp.bfloat16)
         if last:
             for at in range(chunks):
@@ -225,14 +212,18 @@
     out_shape = [jax.ShapeDtypeStruct((rows_back, LANES), jnp.bfloat16)]
     if last:
         out_shape.append(jax.ShapeDtypeStruct((blocks, 3 * nodes), jnp.bfloat16))
+    if first_time:
+        out_shape.append(jax.ShapeDtypeStruct((devices * FORTH, LANES), jnp.bfloat16))
     if k:
         out_shape += [jax.ShapeDtypeStruct((ROWS, LANES), jnp.float32)] * 2
     scratch = [
-        pltpu.VMEM((rows_all + 16, LANES), jnp.float32),
+        pltpu.VMEM((rows_all + over, LANES), jnp.float32),
         pltpu.VMEM((rows_back, LANES), jnp.float32),
     ]
     if last:
         scratch.append(pltpu.VMEM((halves, blocks * 8, LANES), jnp.float32))
+    if first_time:
+        scratch.append(pltpu.VMEM((devices * FORTH, LANES), jnp.float32))
     if stream:
         scratch += [
             pltpu.VMEM(rbf_blocks.shape, rbf_blocks.dtype),
@@ -257,9 +248,10 @@
     )(places, *inputs)
     out = list(out)
     sending = out.pop(0)
+    if first_time:
+        return sending, out[0]
     load = out.pop(0) if last else None
-    fresh, coefs = (out.pop(0), out.pop(0)) if k else (None, None)
-    return sending, load, fresh, coefs
+    return sending, load, *out
 
 
 def full_sum(array):
@@ -457,34 +449,66 @@
 
     start = by_chunks(shell_start, shells)
     start_half = start.astype(jnp.bfloat16)
-    wanted, places = asking_call(
-        route.reshape(1, blocks), slot.reshape(1, blocks), devices, chunks
-    )
-    asked = exchange(wanted.reshape(devices, 1, capacity)).reshape(devices, capacity)
-
+
+    destination = route[:, 0]
+    block_order = jnp.arange(blocks, dtype=jnp.int32)
+    earlier = (destination[:, None] == destination[None, :]) & (
+        block_order[None, :] < block_order[:, None]
+    )
+    slot_rank = jnp.sum(earlier.astype(jnp.int32), axis=1)
+    places = jnp.stack(
+        [destination * FORTH + slot_rank * chunks, destination * BACK + slot_rank * chunks]
+    )
+    solid = lax.axis_size("solid")
+    upper = destination // solid
+    begun_from = upper % 2 * (devices // 2) + upper // 2 * solid + destination % solid
+    first_places = jnp.stack(
+        [
+            begun_from * height + slot,
+            destination * FORTH + slot_rank * chunks,
+            destination * FORTH + slot_rank * chunks,
+        ]
+    )
+    peers = jnp.arange(devices, dtype=jnp.int32)
+    lanes = jnp.arange(LANES, dtype=jnp.int32)
+    wanted = jnp.where(slot_rank[:, None] == lanes[None, :], slot[:, None] + 1, 0)
+    asking = jnp.dot(
+        (peers[:, None] == destination[None, :]).astype(jnp.bfloat16),
+        wanted.astype(jnp.bfloat16),
+        preferred_element_type=jnp.float32,
+    )
+
+    traction = spread_components(fluid_traction, blocks, nodes)
+    massive = spread_components(fluid_mass, blocks, nodes)
+    robin = by_chunks(robin_coef, shells)
+
+    shown = start_half.astype(jnp.float32)
     stacked = jnp.arange(height + ROWS, dtype=jnp.int32)
-
-    def shows(size):
-        order = jnp.arange(size, dtype=jnp.int32)[None, :]
+    summed = jnp.arange(devices * FORTH, dtype=jnp.int32)[None, :] % FORTH == capacity * chunks
+    add_up = jnp.broadcast_to(summed, (ROWS, devices * FORTH)).astype(jnp.bfloat16)
+
+    def one_hot(asked):
+        order = jnp.arange(FORTH, dtype=jnp.int32)[None, :]
         named = jnp.where(order < chunks, asked[:, :1], asked[:, 1:2])
         rows = jnp.where(
             (named >= 0) & (order < capacity * chunks), (order % chunks) * shells + named, -1
         )
-        return jnp.where(order == capacity * chunks, height, rows).reshape(-1)
-
-    pick = (shows(FORTH)[:, None] == stacked[None, :]).astype(jnp.bfloat16)
-    collect = (stacked[:height, None] == shows(BACK)[None, :]).astype(jnp.bfloat16)
-    summed = jnp.arange(devices * FORTH, dtype=jnp.int32)[None, :] % FORTH == capacity * chunks
-    add_up = jnp.broadcast_to(summed, (ROWS, devices * FORTH)).astype(jnp.bfloat16)
-
-    traction = spread_components(fluid_traction, blocks, nodes)
-    massive = spread_components(fluid_mass, blocks, nodes)
-    robin = by_chunks(robin_coef, shells)
-
-    shown = start_half.astype(jnp.float32)
-    outgoing = jnp.dot(
-        pick, jnp.pad(start_half, ((0, ROWS), (0, 0))), preferred_element_type=jnp.float32
-    ).astype(jnp.bfloat16)
+        forth = jnp.where(order == capacity * chunks, height, rows).reshape(-1)
+        pick = (forth[:, None] == stacked[None, :]).astype(jnp.bfloat16)
+        collect_first = (stacked[:height, None] == rows.reshape(-1)[None, :]).astype(jnp.bfloat16)
+        back = rows[:, :BACK].reshape(-1)
+        collect = (stacked[:height, None] == back[None, :]).astype(jnp.bfloat16)
+        return pick, collect_first, collect
+
+    begun = start_half
+    for axes, amount in ((("fluid_0", "fluid_1", "solid"), devices // 2), (("fluid_2",), 2)):
+        begun = lax.all_to_all(
+            jnp.broadcast_to(begun[None], (amount, *begun.shape)),
+            axes,
+            split_axis=0,
+            concat_axis=0,
+            tiled=True,
+        ).reshape(-1, LANES)
     messages = []
     sums = []
     residuals = []
@@ -492,29 +516,45 @@
     last_load = None
     for iteration in range(ITERS):
         last = iteration == ITERS - 1
-        messages.append(transport(outgoing, 2))
-        sending, last_load, fresh, coefs = fluid_call(
-            places,
-            add_up,
-            messages,
-            sums[1:],
-            rbf_blocks,
-            traction,
-            massive,
-            iteration < FLUID_STREAMS,
-            last,
-        )
+        coefs = None
+        if iteration == 0:
+            sending, message = fluid_call(
+                first_places, asking, [begun], [], rbf_blocks, traction, massive, shells, True, last
+            )
+            arrived = transport(sending, 2)
+            asked = arrived.reshape(devices, FORTH, LANES)[:, capacity * chunks, :capacity]
+            pick, collect_now, collect = one_hot(asked.astype(jnp.int32) - 1)
+            pick, collect_now, collect, add_up, places, arrived = lax.optimization_barrier(
+                (pick, collect_now, collect, add_up, places, arrived)
+            )
+        else:
+            message = transport(outgoing, 2)
+        messages.append(message)
         if iteration:
+            sending, last_load, fresh, coefs = fluid_call(
+                places,
+                add_up,
+                messages,
+                sums[1:],
+                rbf_blocks,
+                traction,
+                massive,
+                shells,
+                iteration < FLUID_STREAMS,
+                last,
+            )
             sums.append(fresh)
+            arrived = transport(sending, 4)
+            collect_now = collect
         made = shell_call(
-            transport(sending, 4),
+            arrived,
             coefs,
             shown,
             residuals,
             images,
             start,
             robin,
-            collect,
+            collect_now,
             pick,
             shell_inverse,
             iteration < SHELL_STREAMS,

time: 306 us -> 304 us (level)
  waiting for transfers between devices: 31.5 us -> 21.3 us
  blocking collectives: 183 us -> 190 us
  starting transfers between devices: 19.9 us -> 15.8 us
    all_to_all x3 -> x1, waiting for transfers between devices: 31.5 us -> 13.2 us  [exchange(): lax.all_to_all(array, FLUID_SOLID, split_axis=0, concat_axis=0, tiled=True)]
    all_to_all x3 -> x1, starting transfers between devices: 19.9 us -> 3.8 us  [exchange(): lax.all_to_all(array, FLUID_SOLID, split_axis=0, concat_axis=0, tiled=True)]
    all_to_all x0 -> x1, starting transfers between devices: none -> 12 us  [per_device(): lax.all_to_all(jnp.broadcast_to(begun[None], (amount, *begun.shape)), axe...]
    all_to_all x0 -> x1, waiting for transfers between devices: none -> 8.16 us  [per_device(): lax.all_to_all(jnp.broadcast_to(begun[None], (amount, *begun.shape)), axe...]
    all_to_all x0 -> x1, blocking collectives: none -> 7.37 us  [per_device(): lax.all_to_all(jnp.broadcast_to(begun[None], (amount, *begun.shape)), axe...]
  transfers between devices with their start and end apart: 3 -> 2, of which waited for: 3 -> 2; matrix products, arithmetic and copies ran while one was open for 1% -> 2% of each run, Pallas kernels for 0% -> 0%
where the time goes in v5:
time: 304 us; the launch traced here: 303 us
  blocking collectives  190 us (62%)
  Pallas kernels  64.8 us (21%)
  waiting for transfers between devices  21.3 us (7%)
  starting transfers between devices  15.8 us (5%)
  local copies, waits for them, and re-layouts  4.99 us (2%)
  other arithmetic  3.84 us (1%)
    all_to_all x11, blocking collectives, exchange(): lax.all_to_all(array, FLUID_SOLID, split_axis=0, concat_axis=0, tiled=True)  183 us
    pallas_call x6, Pallas kernels, fluid_call(): pl.pallas_call(body, in_specs=[pl.BlockSpec(memory_space=pltpu.SMEM)] + i...  46.4 us
    pallas_call x6, Pallas kernels, shell_call(): pl.pallas_call(body, in_specs=in_specs, out_specs=[vmem()] * len(out_shap...  16.6 us
    all_to_all x1, waiting for transfers between devices, exchange(): lax.all_to_all(array, FLUID_SOLID, split_axis=0, concat_axis=0, tiled=True)  13.2 us
    all_to_all x1, starting transfers between devices, per_device(): lax.all_to_all(jnp.broadcast_to(begun[None], (amount, *begun.shape)), axe...  12 us
    all_to_all x1, waiting for transfers between devices, per_device(): lax.all_to_all(jnp.broadcast_to(begun[None], (amount, *begun.shape)), axe...  8.16 us
    all_to_all x1, blocking collectives, per_device(): lax.all_to_all(jnp.broadcast_to(begun[None], (amount, *begun.shape)), axe...  7.37 us
  transfers between devices with their start and end apart: 2, of which 2 were waited for; matrix products, arithmetic and copies ran while one was open for 2% of the time, Pallas kernels for 0%

profile of v5, /device:TPU:1, one launch (start us, length us, event | category | flops | bytes accessed | tf_op | source)
XLA Modules:
  0.0 302.9 jit_solution(2823899259345983028)
XLA Ops:
  0.6 0.7 fusion.19
  1.4 1.0 broadcast_in_dim.98
  2.4 12.0 %all-to-all-start = ((bf16[64,48,128]{2,1,0:T(8,128)(2,1)}), bf16[64,48,128]{2,1,0:T(8,128)(2,1)S(1)}, u32[]{:S(2)}, u32[]{:S(2)}) async-start(bf16[64,48,128]{2,1,0:T(8,128)(2,1)} %broadcast_in_dim.98), calls=%async_computation | async-start | bytes 1572864 | tf_op jit(solution)/shard_map/all_to_all | solution.py:505
  14.4 0.7 broadcast_add_fusion
  15.1 0.9 convert_reduce_fusion
  16.0 1.1 copy.27
  17.1 0.2 copy.28
  17.3 1.1 copy.29
  18.4 0.2 copy.30
  18.5 0.7 bitcast_add_fusion
  19.2 0.2 bitcast_convert_fusion
  19.4 0.9 fusion.2.refs_1_
  20.3 8.2 %all-to-all-done = bf16[64,48,128]{2,1,0:T(8,128)(2,1)S(1)} async-done(((bf16[64,48,128]{2,1,0:T(8,128)(2,1)}), bf16[64,48,128]{2,1,0:T(8,128)(2,1)S(1)}, u32[]{:S(2)}, u32[]{:S(2)}) %all-to-all-start) | async-done | bytes 786464 | tf_op jit(solution)/shard_map/all_to_all | solution.py:505
  28.4 0.1 broadcast_in_dim.100
  28.5 7.4 %all_to_all.70 = bf16[2,3072,128]{2,1,0:T(8,128)(2,1)S(1)} all-to-all(bf16[2,3072,128]{2,1,0:T(8,128)(2,1)S(1)} %broadcast_in_dim.100), channel_id=1, replica_groups=mesh['fluid_0'=4,'fluid_1'=4,'fluid_2'=2,'solid'=4] {'fluid_2'}, dimensions={0} | all-to-all | bytes 3145728 | tf_op jit(solution)/shard_map/all_to_all | solution.py:505
  35.9 8.8 %fluid_side.6 = (bf16[1792,128]{1,0:T(8,128)(2,1)}, bf16[1792,128]{1,0:T(8,128)(2,1)S(1)}) custom-call(s32[3,104]{1,0:T(4,128)S(1)} %pad_add_fusion.refs_0_, f32[128,128]{1,0:T(8,128)S(1)} %fusion.2.refs_1_, bf16[6144,128]{1,0:T(8,128)(2,1)S(1)} %bitcast.83, bf16[104,256,256]{2,1,0:T(8,128)(2,1)} %refs_11_.3, ...), custom_call_target="tpu_custom_call" | custom-call | tf_op jit(solution)/shard_map/fluid_side/pallas_call | solution.py:238
  44.8 3.8 %all-to-all-start.2 = ((bf16[128,7,2,128]{3,2,1,0:T(2,128)(2,1)}), bf16[128,7,2,128]{3,2,1,0:T(2,128)(2,1)S(1)}, u32[]{:S(2)}, u32[]{:S(2)}) async-start(bf16[128,7,2,128]{3,2,1,0:T(2,128)(2,1)} %bitcast.13), calls=%async_computation.2 | async-start | bytes 917504 | tf_op jit(solution)/shard_map/all_to_all | solution.py:444
  48.6 0.1 broadcast_in_dim.93
  48.8 13.2 %all-to-all-done.2 = bf16[128,7,2,128]{3,2,1,0:T(2,128)(2,1)S(1)} async-done(((bf16[128,7,2,128]{3,2,1,0:T(2,128)(2,1)}), bf16[128,7,2,128]{3,2,1,0:T(2,128)(2,1)S(1)}, u32[]{:S(2)}, u32[]{:S(2)}) %all-to-all-start.2) | async-done | bytes 458784 | tf_op jit(solution)/shard_map/all_to_all | solution.py:444
  62.0 0.8 copy.31
  62.8 0.1 fusion.1
  62.9 0.1 select_n.89
  63.0 0.1 eq.123
  63.2 0.1 compare_convert_fusion.refs_4_
  63.4 0.3 fusion.refs_5_.refs_8_.refs_10_.refs_12_.refs_14_.refs_16_
  63.7 4.6 %shell_side.6 = (bf16[1792,128]{1,0:T(8,128)(2,1)S(1)}, f32[48,128]{1,0:T(8,128)S(1)}, f32[48,128]{1,0:T(8,128)S(1)}, f32[48,128]{1,0:T(8,128)S(1)}) custom-call(bf16[1792,128]{1,0:T(8,128)(2,1)S(1)} %bitcast.86, f32[48,128]{1,0:T(8,128)S(1)} %get-tuple-element.99.refs_1_, f32[48,128]{1,0:T(8,128)S(1)} %bitcast.93, f32[48,128]{1,0:T(8,128)S(1)} %bitcast.99, ...), custom_call_target="tpu_custom_call" | custom-call | tf_op jit(solution)/shard_map/shell_side/pallas_call | solution.py:372
  68.3 17.2 %all_to_all.71 = bf16[128,7,2,128]{3,2,1,0:T(2,128)(2,1)S(1)} all-to-all(bf16[128,7,2,128]{3,2,1,0:T(2,128)(2,1)S(1)} %bitcast.105), channel_id=1, replica_groups=mesh['fluid_0'=4,'fluid_1'=4,'fluid_2'=2,'solid'=4] {'fluid_0','fluid_1'..., dimensions={0} | all-to-all | bytes 917504 | tf_op jit(solution)/shard_map/all_to_all | solution.py:444
  85.5 8.2 %fluid_side.7 = (bf16[1536,128]{1,0:T(8,128)(2,1)S(1)}, f32[16,128]{1,0:T(8,128)S(1)}, f32[16,128]{1,0:T(8,128)S(1)}) custom-call(s32[2,104]{1,0:T(2,128)S(1)} %pad_add_fusion.1.refs_0_, bf16[16,1792]{1,0:T(8,128)(2,1)S(1)} %broadcast_in_dim.106.refs_1_, bf16[1792,128]{1,0:T(8,128)(2,1)S(1)} %get-tuple-element.54.refs_2_, bf16[1792,128]{1,0:T(8,128)(2,1)S(1)} %bitcast.71, ...), custom_call_target="tpu_custom_call" | custom-call | tf_op jit(solution)/shard_map/fluid_side/pallas_call | solution.py:238
  93.8 16.5 %all_to_all.72 = bf16[128,3,4,128]{3,2,1,0:T(4,128)(2,1)S(1)} all-to-all(bf16[128,3,4,128]{3,2,1,0:T(4,128)(2,1)S(1)} %bitcast.111), channel_id=1, replica_groups=mesh['fluid_0'=4,'fluid_1'=4,'fluid_2'=2,'solid'=4] {'fluid_0','fluid_1'..., dimensions={0} | all-to-all | bytes 786432 | tf_op jit(solution)/shard_map/all_to_all | solution.py:444
  110.3 4.6 %shell_side.7 = (bf16[1792,128]{1,0:T(8,128)(2,1)S(1)}, f32[48,128]{1,0:T(8,128)S(1)}, f32[48,128]{1,0:T(8,128)S(1)}, f32[48,128]{1,0:T(8,128)S(1)}) custom-call(bf16[1536,128]{1,0:T(8,128)(2,1)S(1)} %bitcast.88, f32[16,128]{1,0:T(8,128)S(1)} %get-tuple-element.60.refs_1_, f32[48,128]{1,0:T(8,128)S(1)} %get-tuple-element.61.refs_2_, ...), custom_call_target="tpu_custom_call" | custom-call | tf_op jit(solution)/shard_map/shell_side/pallas_call | solution.py:372
  114.9 17.2 %all_to_all.73 = bf16[128,7,2,128]{3,2,1,0:T(2,128)(2,1)S(1)} all-to-all(bf16[128,7,2,128]{3,2,1,0:T(2,128)(2,1)S(1)} %bitcast.106), channel_id=1, replica_groups=mesh['fluid_0'=4,'fluid_1'=4,'fluid_2'=2,'solid'=4] {'fluid_0','fluid_1'..., dimensions={0} | all-to-all | bytes 917504 | tf_op jit(solution)/shard_map/all_to_all | solution.py:444
  132.2 7.0 %fluid_side.8 = (bf16[1536,128]{1,0:T(8,128)(2,1)S(1)}, f32[16,128]{1,0:T(8,128)S(1)}, f32[16,128]{1,0:T(8,128)S(1)}) custom-call(s32[2,104]{1,0:T(2,128)S(1)} %pad_add_fusion.1.refs_0_, bf16[16,1792]{1,0:T(8,128)(2,1)S(1)} %broadcast_in_dim.106.refs_1_, bf16[1792,128]{1,0:T(8,128)(2,1)S(1)} %get-tuple-element.54.refs_2_, bf16[1792,128]{1,0:T(8,128)(2,1)S(1)} %bitcast.72, ...), custom_call_target="tpu_custom_call" | custom-call | tf_op jit(solution)/shard_map/fluid_side/pallas_call | solution.py:238
  139.2 16.5 %all_to_all.74 = bf16[128,3,4,128]{3,2,1,0:T(4,128)(2,1)S(1)} all-to-all(bf16[128,3,4,128]{3,2,1,0:T(4,128)(2,1)S(1)} %bitcast.112), channel_id=1, replica_groups=mesh['fluid_0'=4,'fluid_1'=4,'fluid_2'=2,'solid'=4] {'fluid_0','fluid_1'..., dimensions={0} | all-to-all | bytes 786432 | tf_op jit(solution)/shard_map/all_to_all | solution.py:444
  155.7 1.9 shell_side.8
  157.7 17.2 %all_to_all.75 = bf16[128,7,2,128]{3,2,1,0:T(2,128)(2,1)S(1)} all-to-all(bf16[128,7,2,128]{3,2,1,0:T(2,128)(2,1)S(1)} %bitcast.107), channel_id=1, replica_groups=mesh['fluid_0'=4,'fluid_1'=4,'fluid_2'=2,'solid'=4] {'fluid_0','fluid_1'..., dimensions={0} | all-to-all | bytes 917504 | tf_op jit(solution)/shard_map/all_to_all | solution.py:444
  174.9 7.1 %fluid_side.9 = (bf16[1536,128]{1,0:T(8,128)(2,1)S(1)}, f32[16,128]{1,0:T(8,128)S(1)}, f32[16,128]{1,0:T(8,128)S(1)}) custom-call(s32[2,104]{1,0:T(2,128)S(1)} %pad_add_fusion.1.refs_0_, bf16[16,1792]{1,0:T(8,128)(2,1)S(1)} %broadcast_in_dim.106.refs_1_, bf16[1792,128]{1,0:T(8,128)(2,1)S(1)} %get-tuple-element.54.refs_2_, bf16[1792,128]{1,0:T(8,128)(2,1)S(1)} %bitcast.73, ...), custom_call_target="tpu_custom_call" | custom-call | tf_op jit(solution)/shard_map/fluid_side/pallas_call | solution.py:238
  182.0 16.5 %all_to_all.76 = bf16[128,3,4,128]{3,2,1,0:T(4,128)(2,1)S(1)} all-to-all(bf16[128,3,4,128]{3,2,1,0:T(4,128)(2,1)S(1)} %bitcast.113), channel_id=1, replica_groups=mesh['fluid_0'=4,'fluid_1'=4,'fluid_2'=2,'solid'=4] {'fluid_0','fluid_1'..., dimensions={0} | all-to-all | bytes 786432 | tf_op jit(solution)/shard_map/all_to_all | solution.py:444
  198.5 1.9 shell_side.9
  200.5 17.2 %all_to_all.77 = bf16[128,7,2,128]{3,2,1,0:T(2,128)(2,1)S(1)} all-to-all(bf16[128,7,2,128]{3,2,1,0:T(2,128)(2,1)S(1)} %bitcast.108), channel_id=1, replica_groups=mesh['fluid_0'=4,'fluid_1'=4,'fluid_2'=2,'solid'=4] {'fluid_0','fluid_1'..., dimensions={0} | all-to-all | bytes 917504 | tf_op jit(solution)/shard_map/all_to_all | solution.py:444
  217.7 7.2 %fluid_side.10 = (bf16[1536,128]{1,0:T(8,128)(2,1)S(1)}, f32[16,128]{1,0:T(8,128)S(1)}, f32[16,128]{1,0:T(8,128)S(1)}) custom-call(s32[2,104]{1,0:T(2,128)S(1)} %pad_add_fusion.1.refs_0_, bf16[16,1792]{1,0:T(8,128)(2,1)S(1)} %broadcast_in_dim.106.refs_1_, bf16[1792,128]{1,0:T(8,128)(2,1)S(1)} %get-tuple-element.54.refs_2_, bf16[1792,128]{1,0:T(8,128)(2,1)S(1)} %bitcast.74, ...), custom_call_target="tpu_custom_call" | custom-call | tf_op jit(solution)/shard_map/fluid_side/pallas_call | solution.py:238
  224.9 16.5 %all_to_all.78 = bf16[128,3,4,128]{3,2,1,0:T(4,128)(2,1)S(1)} all-to-all(bf16[128,3,4,128]{3,2,1,0:T(4,128)(2,1)S(1)} %bitcast.114), channel_id=1, replica_groups=mesh['fluid_0'=4,'fluid_1'=4,'fluid_2'=2,'solid'=4] {'fluid_0','fluid_1'..., dimensions={0} | all-to-all | bytes 786432 | tf_op jit(solution)/shard_map/all_to_all | solution.py:444
  241.4 1.9 shell_side.10
  243.3 17.2 %all_to_all.79 = bf16[128,7,2,128]{3,2,1,0:T(2,128)(2,1)S(1)} all-to-all(bf16[128,7,2,128]{3,2,1,0:T(2,128)(2,1)S(1)} %bitcast.109), channel_id=1, replica_groups=mesh['fluid_0'=4,'fluid_1'=4,'fluid_2'=2,'solid'=4] {'fluid_0','fluid_1'..., dimensions={0} | all-to-all | bytes 917504 | tf_op jit(solution)/shard_map/all_to_all | solution.py:444
  260.5 8.0 %fluid_side.11 = (bf16[1536,128]{1,0:T(8,128)(2,1)S(1)}, bf16[104,768]{1,0:T(8,128)(2,1)}, f32[16,128]{1,0:T(8,128)S(1)}, f32[16,128]{1,0:T(8,128)S(1)}) custom-call(s32[2,104]{1,0:T(2,128)S(1)} %pad_add_fusion.1.refs_0_, bf16[16,1792]{1,0:T(8,128)(2,1)S(1)} %broadcast_in_dim.106.refs_1_, bf16[1792,128]{1,0:T(8,128)(2,1)S(1)} %get-tuple-element.54.refs_2_, ...), custom_call_target="tpu_custom_call" | custom-call | tf_op jit(solution)/shard_map/fluid_side/pallas_call | solution.py:238
  268.5 16.5 %all_to_all.80 = bf16[128,3,4,128]{3,2,1,0:T(4,128)(2,1)S(1)} all-to-all(bf16[128,3,4,128]{3,2,1,0:T(4,128)(2,1)S(1)} %bitcast.110), channel_id=1, replica_groups=mesh['fluid_0'=4,'fluid_1'=4,'fluid_2'=2,'solid'=4] {'fluid_0','fluid_1'..., dimensions={0} | all-to-all | bytes 786432 | tf_op jit(solution)/shard_map/all_to_all | solution.py:444
  285.0 1.7 shell_side.11
  286.8 14.1 %all_to_all.81 = bf16[128,1,2,128]{3,2,1,0:T(2,128)(2,1)} all-to-all(bf16[128,1,2,128]{3,2,1,0:T(2,128)(2,1)S(1)} %reshape.335), channel_id=1, replica_groups=mesh['fluid_0'=4,'fluid_1'=4,'fluid_2'=2,'solid'=4] {'fluid_0','fluid_1'..., dimensions={0} | all-to-all | bytes 131072 | tf_op jit(solution)/shard_map/all_to_all | solution.py:444
  300.9 1.8 closing.1
  (57 shorter events, 0.3 us)
Async XLA Ops:
  2.4 26.0 %all-to-all-start = ((bf16[64,48,128]{2,1,0:T(8,128)(2,1)}), bf16[64,48,128]{2,1,0:T(8,128)(2,1)S(1)}, u32[]{:S(2)}, u32[]{:S(2)}) async-start(bf16[64,48,128]{2,1,0:T(8,128)(2,1)} %broadcast_in_dim.98), calls=%async_computation | async-start | bytes 1572864 | tf_op jit(solution)/shard_map/all_to_all | solution.py:505
  35.9 27.8 %copy-start = (f32[8,768]{1,0:T(8,128)S(1)}, f32[8,768]{1,0:T(8,128)}, u32[]{:S(2)}) copy-start(f32[8,768]{1,0:T(8,128)} %param.15) | copy-start | bytes 73732
  35.9 27.8 %copy-start.2 = (f32[8,768]{1,0:T(8,128)S(1)}, f32[8,768]{1,0:T(8,128)}, u32[]{:S(2)}) copy-start(f32[8,768]{1,0:T(8,128)} %param.14) | copy-start | bytes 73732
  44.8 17.2 %all-to-all-start.2 = ((bf16[128,7,2,128]{3,2,1,0:T(2,128)(2,1)}), bf16[128,7,2,128]{3,2,1,0:T(2,128)(2,1)S(1)}, u32[]{:S(2)}, u32[]{:S(2)}) async-start(bf16[128,7,2,128]{3,2,1,0:T(2,128)(2,1)} %bitcast.13), calls=%async_computation.2 | async-start | bytes 917504 | tf_op jit(solution)/shard_map/all_to_all | solution.py:444
  68.3 216.7 %copy-start.1 = (f32[48,128]{1,0:T(8,128)}, f32[48,128]{1,0:T(8,128)S(1)}, u32[]{:S(2)}) copy-start(f32[48,128]{1,0:T(8,128)S(1)} %get-tuple-element.63.refs_4_.refs_5_.refs_6_.refs_7_.refs_8_) | copy-start | bytes 73732
  85.5 46.6 %slice-start = ((s8[13631488]{0:T(1024)(128)(4,1)}), s8[4194304]{0:T(1024)(128)(4,1)S(1)}, s32[]{:S(2)}) async-start(s8[13631488]{0:T(1024)(128)(4,1)} %bitcast.67), calls=%async_computation.14 | async-start | bytes 8388608
  85.5 46.6 %slice-start.1 = ((s8[13631488]{0:T(1024)(128)(4,1)}), s8[4194304]{0:T(1024)(128)(4,1)S(1)}, s32[]{:S(2)}) async-start(s8[13631488]{0:T(1024)(128)(4,1)} %bitcast.67), calls=%async_computation.15 | async-start | bytes 8388608
  85.5 46.6 %slice-start.2 = ((s8[13631488]{0:T(1024)(128)(4,1)}), s8[4194304]{0:T(1024)(128)(4,1)S(1)}, s32[]{:S(2)}) async-start(s8[13631488]{0:T(1024)(128)(4,1)} %bitcast.67), calls=%async_computation.16 | async-start | bytes 8388608
  93.8 16.5 %copy-start.11 = (f32[16,128]{1,0:T(8,128)}, f32[16,128]{1,0:T(8,128)S(1)}, u32[]{:S(2)}) copy-start(f32[16,128]{1,0:T(8,128)S(1)} %get-tuple-element.93.refs_1_) | copy-start | bytes 24580
  110.3 21.9 %slice-start.3 = ((s8[13631488]{0:T(1024)(128)(4,1)}), s8[1048576]{0:T(1024)(128)(4,1)S(1)}, s32[]{:S(2)}) async-start(s8[13631488]{0:T(1024)(128)(4,1)} %bitcast.67), calls=%async_computation.17 | async-start | bytes 2097152
  114.9 170.1 %copy-start.3 = (f32[48,128]{1,0:T(8,128)}, f32[48,128]{1,0:T(8,128)S(1)}, u32[]{:S(2)}) copy-start(f32[48,128]{1,0:T(8,128)S(1)} %get-tuple-element.70.refs_6_.refs_7_.refs_8_.refs_9_) | copy-start | bytes 73732
  114.9 40.8 %slice-start.4 = ((s8[9437184]{0:T(1024)(128)(4,1)}), s8[4194304]{0:T(1024)(128)(4,1)S(1)}, s32[]{:S(2)}) async-start(s8[9437184]{0:T(1024)(128)(4,1)} %bitcast.69), calls=%async_computation.18 | async-start | bytes 8388608
  132.1 23.6 %slice-start.5 = ((s8[9437184]{0:T(1024)(128)(4,1)}), s8[4194304]{0:T(1024)(128)(4,1)S(1)}, s32[]{:S(2)}) async-start(s8[9437184]{0:T(1024)(128)(4,1)} %bitcast.69), calls=%async_computation.19 | async-start | bytes 8388608
  132.2 23.6 %slice-start.6 = ((s8[9437184]{0:T(1024)(128)(4,1)}), s8[1048576]{0:T(1024)(128)(4,1)S(1)}, s32[]{:S(2)}) async-start(s8[9437184]{0:T(1024)(128)(4,1)} %bitcast.69), calls=%async_computation.20 | async-start | bytes 2097152
  139.2 121.3 %copy-start.6 = (f32[16,128]{1,0:T(8,128)}, f32[16,128]{1,0:T(8,128)S(1)}, u32[]{:S(2)}) copy-start(f32[16,128]{1,0:T(8,128)S(1)} %get-tuple-element.72.refs_6_.refs_7_.refs_8_.refs_2_) | copy-start | bytes 24580
  157.7 127.3 %copy-start.4 = (f32[48,128]{1,0:T(8,128)}, f32[48,128]{1,0:T(8,128)S(1)}, u32[]{:S(2)}) copy-start(f32[48,128]{1,0:T(8,128)S(1)} %get-tuple-element.77.refs_8_.refs_9_.refs_10_) | copy-start | bytes 73732
  182.0 78.5 %copy-start.8 = (f32[16,128]{1,0:T(8,128)}, f32[16,128]{1,0:T(8,128)S(1)}, u32[]{:S(2)}) copy-start(f32[16,128]{1,0:T(8,128)S(1)} %get-tuple-element.79.refs_8_.refs_9_.refs_3_) | copy-start | bytes 24580
  200.4 84.6 %copy-start.5 = (f32[48,128]{1,0:T(8,128)}, f32[48,128]{1,0:T(8,128)S(1)}, u32[]{:S(2)}) copy-start(f32[48,128]{1,0:T(8,128)S(1)} %get-tuple-element.84.refs_10_.refs_11_.refs_9_) | copy-start | bytes 73732
  224.9 43.6 %copy-start.9 = (f32[16,128]{1,0:T(8,128)}, f32[16,128]{1,0:T(8,128)S(1)}, u32[]{:S(2)}) copy-start(f32[16,128]{1,0:T(8,128)S(1)} %get-tuple-element.86.refs_10_.refs_4_) | copy-start | bytes 24580
  243.3 41.7 %copy-start.7 = (f32[48,128]{1,0:T(8,128)}, f32[48,128]{1,0:T(8,128)S(1)}, u32[]{:S(2)}) copy-start(f32[48,128]{1,0:T(8,128)S(1)} %get-tuple-element.91.refs_12_.refs_10_) | copy-start | bytes 73732
  268.5 18.2 %copy-start.12 = (f32[16,128]{1,0:T(8,128)}, f32[16,128]{1,0:T(8,128)S(1)}, u32[]{:S(2)}) copy-start(f32[16,128]{1,0:T(8,128)S(1)} %get-tuple-element.94.refs_5_) | copy-start | bytes 24580
  286.7 14.2 %copy-start.10 = (f32[48,128]{1,0:T(8,128)}, f32[48,128]{1,0:T(8,128)S(1)}, u32[]{:S(2)}) copy-start(f32[48,128]{1,0:T(8,128)S(1)} %get-tuple-element.95.refs_11_) | copy-start | bytes 73732

commit v6 on v5

--- a/solution.py
+++ b/solution.py
@@ -93,7 +93,7 @@
     steps = blocks // group
     pieces = [(at * group, group) for at in range(steps)]
     if blocks == 104:
-        pieces = [(0, 8), (8, 16), (24, 24), (48, 28), (76, 28)]
+        pieces = [(0, 26), (26, 39), (65, 39)]
 
     def body(*refs):
         refs = list(refs)
@@ -522,7 +522,11 @@
                 first_places, asking, [begun], [], rbf_blocks, traction, massive, shells, True, last
             )
             arrived = transport(sending, 2)
-            asked = arrived.reshape(devices, FORTH, LANES)[:, capacity * chunks, :capacity]
+            rows = jnp.arange(devices * FORTH, dtype=jnp.int32)[None, :]
+            numbers = peers[:, None] * FORTH + capacity * chunks == rows
+            asked = jnp.dot(
+                numbers.astype(jnp.bfloat16), arrived, preferred_element_type=jnp.float32
+            )
             pick, collect_now, collect = one_hot(asked.astype(jnp.int32) - 1)
             pick, collect_now, collect, add_up, places, arrived = lax.optimization_barrier(
                 (pick, collect_now, collect, add_up, places, arrived)

time: 304 us -> 304 us (level)
  no operation moved by 1% of the time
where the time goes in v6:
time: 304 us
  blocking collectives  190 us (62%)
  Pallas kernels  66.1 us (22%)
  waiting for transfers between devices  21.3 us (7%)
  starting transfers between devices  15.8 us (5%)
  local copies, waits for them, and re-layouts  4.19 us (1%)
  other arithmetic  3.85 us (1%)
    all_to_all x11, blocking collectives, exchange(): lax.all_to_all(array, FLUID_SOLID, split_axis=0, concat_axis=0, tiled=True)  183 us
    pallas_call x6, Pallas kernels, fluid_call(): pl.pallas_call(body, in_specs=[pl.BlockSpec(memory_space=pltpu.SMEM)] + i...  47.7 us
    pallas_call x6, Pallas kernels, shell_call(): pl.pallas_call(body, in_specs=in_specs, out_specs=[vmem()] * len(out_shap...  16.6 us
    all_to_all x1, waiting for transfers between devices, exchange(): lax.all_to_all(array, FLUID_SOLID, split_axis=0, concat_axis=0, tiled=True)  13.2 us
    all_to_all x1, starting transfers between devices, per_device(): lax.all_to_all(jnp.broadcast_to(begun[None], (amount, *begun.shape)), axe...  12 us
    all_to_all x1, waiting for transfers between devices, per_device(): lax.all_to_all(jnp.broadcast_to(begun[None], (amount, *begun.shape)), axe...  8.14 us
    all_to_all x1, blocking collectives, per_device(): lax.all_to_all(jnp.broadcast_to(begun[None], (amount, *begun.shape)), axe...  7.37 us
  transfers between devices with their start and end apart: 2, of which 2 were waited for; matrix products, arithmetic and copies ran while one was open for 2% of the time, Pallas kernels for 0%

profile of v6, /device:TPU:1, one launch (start us, length us, event | category | flops | bytes accessed | tf_op | source)
XLA Modules:
  0.0 303.8 jit_solution(14747470699436951916)
XLA Ops:
  0.6 0.7 fusion.21
  1.4 1.0 broadcast_in_dim.100
  2.4 12.0 %all-to-all-start = ((bf16[64,48,128]{2,1,0:T(8,128)(2,1)}), bf16[64,48,128]{2,1,0:T(8,128)(2,1)S(1)}, u32[]{:S(2)}, u32[]{:S(2)}) async-start(bf16[64,48,128]{2,1,0:T(8,128)(2,1)} %broadcast_in_dim.100), calls=%async_computation | async-start | bytes 1572864 | tf_op jit(solution)/shard_map/all_to_all | solution.py:505
  14.4 0.9 convert_reduce_fusion
  15.3 0.7 broadcast_add_fusion
  16.0 1.1 copy.23
  17.1 0.2 copy.24
  17.3 1.1 copy.25
  18.4 0.2 copy.26
  18.6 0.7 bitcast_add_fusion
  19.2 0.2 bitcast_convert_fusion
  19.4 0.9 fusion.4.refs_1_
  20.3 8.1 %all-to-all-done = bf16[64,48,128]{2,1,0:T(8,128)(2,1)S(1)} async-done(((bf16[64,48,128]{2,1,0:T(8,128)(2,1)}), bf16[64,48,128]{2,1,0:T(8,128)(2,1)S(1)}, u32[]{:S(2)}, u32[]{:S(2)}) %all-to-all-start) | async-done | bytes 786464 | tf_op jit(solution)/shard_map/all_to_all | solution.py:505
  28.4 0.1 broadcast_in_dim.102
  28.5 7.4 %all_to_all.70 = bf16[2,3072,128]{2,1,0:T(8,128)(2,1)S(1)} all-to-all(bf16[2,3072,128]{2,1,0:T(8,128)(2,1)S(1)} %broadcast_in_dim.102), channel_id=1, replica_groups=mesh['fluid_0'=4,'fluid_1'=4,'fluid_2'=2,'solid'=4] {'fluid_2'}, dimensions={0} | all-to-all | bytes 3145728 | tf_op jit(solution)/shard_map/all_to_all | solution.py:505
  35.9 9.3 %fluid_side.6 = (bf16[1792,128]{1,0:T(8,128)(2,1)}, bf16[1792,128]{1,0:T(8,128)(2,1)S(1)}) custom-call(s32[3,104]{1,0:T(4,128)S(1)} %pad_add_fusion.refs_0_, f32[128,128]{1,0:T(8,128)S(1)} %fusion.4.refs_1_, bf16[6144,128]{1,0:T(8,128)(2,1)S(1)} %bitcast.81, bf16[104,256,256]{2,1,0:T(8,128)(2,1)} %refs_11_.3, ...), custom_call_target="tpu_custom_call" | custom-call | tf_op jit(solution)/shard_map/fluid_side/pallas_call | solution.py:238
  45.2 3.8 %all-to-all-start.2 = ((bf16[128,7,2,128]{3,2,1,0:T(2,128)(2,1)}), bf16[128,7,2,128]{3,2,1,0:T(2,128)(2,1)S(1)}, u32[]{:S(2)}, u32[]{:S(2)}) async-start(bf16[128,7,2,128]{3,2,1,0:T(2,128)(2,1)} %bitcast.13), calls=%async_computation.2 | async-start | bytes 917504 | tf_op jit(solution)/shard_map/all_to_all | solution.py:444
  49.0 0.1 broadcast_in_dim.95
  49.2 13.2 %all-to-all-done.2 = bf16[128,7,2,128]{3,2,1,0:T(2,128)(2,1)S(1)} async-done(((bf16[128,7,2,128]{3,2,1,0:T(2,128)(2,1)}), bf16[128,7,2,128]{3,2,1,0:T(2,128)(2,1)S(1)}, u32[]{:S(2)}, u32[]{:S(2)}) %all-to-all-start.2) | async-done | bytes 458784 | tf_op jit(solution)/shard_map/all_to_all | solution.py:444
  62.4 0.4 fusion
  62.8 0.1 fusion.3
  63.0 0.1 select_n.89
  63.1 0.1 eq.139
  63.2 0.1 compare_convert_fusion.refs_4_
  63.4 0.3 fusion.1.refs_5_.refs_8_.refs_10_.refs_12_.refs_14_.refs_16_
  63.8 4.6 %shell_side.6 = (bf16[1792,128]{1,0:T(8,128)(2,1)S(1)}, f32[48,128]{1,0:T(8,128)S(1)}, f32[48,128]{1,0:T(8,128)S(1)}, f32[48,128]{1,0:T(8,128)S(1)}) custom-call(bf16[1792,128]{1,0:T(8,128)(2,1)S(1)} %bitcast.86, f32[48,128]{1,0:T(8,128)S(1)} %get-tuple-element.99.refs_1_, f32[48,128]{1,0:T(8,128)S(1)} %bitcast.92, f32[48,128]{1,0:T(8,128)S(1)} %bitcast.98, ...), custom_call_target="tpu_custom_call" | custom-call | tf_op jit(solution)/shard_map/shell_side/pallas_call | solution.py:372
  68.4 17.2 %all_to_all.71 = bf16[128,7,2,128]{3,2,1,0:T(2,128)(2,1)S(1)} all-to-all(bf16[128,7,2,128]{3,2,1,0:T(2,128)(2,1)S(1)} %bitcast.104), channel_id=1, replica_groups=mesh['fluid_0'=4,'fluid_1'=4,'fluid_2'=2,'solid'=4] {'fluid_0','fluid_1'..., dimensions={0} | all-to-all | bytes 917504 | tf_op jit(solution)/shard_map/all_to_all | solution.py:444
  85.6 9.0 %fluid_side.7 = (bf16[1536,128]{1,0:T(8,128)(2,1)S(1)}, f32[16,128]{1,0:T(8,128)S(1)}, f32[16,128]{1,0:T(8,128)S(1)}) custom-call(s32[2,104]{1,0:T(2,128)S(1)} %pad_add_fusion.1.refs_0_, bf16[16,1792]{1,0:T(8,128)(2,1)S(1)} %broadcast_in_dim.108.refs_1_, bf16[1792,128]{1,0:T(8,128)(2,1)S(1)} %get-tuple-element.54.refs_2_, bf16[1792,128]{1,0:T(8,128)(2,1)S(1)} %bitcast.69, ...), custom_call_target="tpu_custom_call" | custom-call | tf_op jit(solution)/shard_map/fluid_side/pallas_call | solution.py:238
  94.6 16.5 %all_to_all.72 = bf16[128,3,4,128]{3,2,1,0:T(4,128)(2,1)S(1)} all-to-all(bf16[128,3,4,128]{3,2,1,0:T(4,128)(2,1)S(1)} %bitcast.110), channel_id=1, replica_groups=mesh['fluid_0'=4,'fluid_1'=4,'fluid_2'=2,'solid'=4] {'fluid_0','fluid_1'..., dimensions={0} | all-to-all | bytes 786432 | tf_op jit(solution)/shard_map/all_to_all | solution.py:444
  111.1 4.6 %shell_side.7 = (bf16[1792,128]{1,0:T(8,128)(2,1)S(1)}, f32[48,128]{1,0:T(8,128)S(1)}, f32[48,128]{1,0:T(8,128)S(1)}, f32[48,128]{1,0:T(8,128)S(1)}) custom-call(bf16[1536,128]{1,0:T(8,128)(2,1)S(1)} %bitcast.87, f32[16,128]{1,0:T(8,128)S(1)} %get-tuple-element.60.refs_1_, f32[48,128]{1,0:T(8,128)S(1)} %get-tuple-element.61.refs_2_, ...), custom_call_target="tpu_custom_call" | custom-call | tf_op jit(solution)/shard_map/shell_side/pallas_call | solution.py:372
  115.8 17.2 %all_to_all.73 = bf16[128,7,2,128]{3,2,1,0:T(2,128)(2,1)S(1)} all-to-all(bf16[128,7,2,128]{3,2,1,0:T(2,128)(2,1)S(1)} %bitcast.105), channel_id=1, replica_groups=mesh['fluid_0'=4,'fluid_1'=4,'fluid_2'=2,'solid'=4] {'fluid_0','fluid_1'..., dimensions={0} | all-to-all | bytes 917504 | tf_op jit(solution)/shard_map/all_to_all | solution.py:444
  133.0 7.0 %fluid_side.8 = (bf16[1536,128]{1,0:T(8,128)(2,1)S(1)}, f32[16,128]{1,0:T(8,128)S(1)}, f32[16,128]{1,0:T(8,128)S(1)}) custom-call(s32[2,104]{1,0:T(2,128)S(1)} %pad_add_fusion.1.refs_0_, bf16[16,1792]{1,0:T(8,128)(2,1)S(1)} %broadcast_in_dim.108.refs_1_, bf16[1792,128]{1,0:T(8,128)(2,1)S(1)} %get-tuple-element.54.refs_2_, bf16[1792,128]{1,0:T(8,128)(2,1)S(1)} %bitcast.70, ...), custom_call_target="tpu_custom_call" | custom-call | tf_op jit(solution)/shard_map/fluid_side/pallas_call | solution.py:238
  140.1 16.5 %all_to_all.74 = bf16[128,3,4,128]{3,2,1,0:T(4,128)(2,1)S(1)} all-to-all(bf16[128,3,4,128]{3,2,1,0:T(4,128)(2,1)S(1)} %bitcast.111), channel_id=1, replica_groups=mesh['fluid_0'=4,'fluid_1'=4,'fluid_2'=2,'solid'=4] {'fluid_0','fluid_1'..., dimensions={0} | all-to-all | bytes 786432 | tf_op jit(solution)/shard_map/all_to_all | solution.py:444
  156.6 1.9 shell_side.8
  158.5 17.2 %all_to_all.75 = bf16[128,7,2,128]{3,2,1,0:T(2,128)(2,1)S(1)} all-to-all(bf16[128,7,2,128]{3,2,1,0:T(2,128)(2,1)S(1)} %bitcast.106), channel_id=1, replica_groups=mesh['fluid_0'=4,'fluid_1'=4,'fluid_2'=2,'solid'=4] {'fluid_0','fluid_1'..., dimensions={0} | all-to-all | bytes 917504 | tf_op jit(solution)/shard_map/all_to_all | solution.py:444
  175.7 7.1 %fluid_side.9 = (bf16[1536,128]{1,0:T(8,128)(2,1)S(1)}, f32[16,128]{1,0:T(8,128)S(1)}, f32[16,128]{1,0:T(8,128)S(1)}) custom-call(s32[2,104]{1,0:T(2,128)S(1)} %pad_add_fusion.1.refs_0_, bf16[16,1792]{1,0:T(8,128)(2,1)S(1)} %broadcast_in_dim.108.refs_1_, bf16[1792,128]{1,0:T(8,128)(2,1)S(1)} %get-tuple-element.54.refs_2_, bf16[1792,128]{1,0:T(8,128)(2,1)S(1)} %bitcast.71, ...), custom_call_target="tpu_custom_call" | custom-call | tf_op jit(solution)/shard_map/fluid_side/pallas_call | solution.py:238
  182.9 16.5 %all_to_all.76 = bf16[128,3,4,128]{3,2,1,0:T(4,128)(2,1)S(1)} all-to-all(bf16[128,3,4,128]{3,2,1,0:T(4,128)(2,1)S(1)} %bitcast.112), channel_id=1, replica_groups=mesh['fluid_0'=4,'fluid_1'=4,'fluid_2'=2,'solid'=4] {'fluid_0','fluid_1'..., dimensions={0} | all-to-all | bytes 786432 | tf_op jit(solution)/shard_map/all_to_all | solution.py:444
  199.4 1.9 shell_side.9
  201.3 17.2 %all_to_all.77 = bf16[128,7,2,128]{3,2,1,0:T(2,128)(2,1)S(1)} all-to-all(bf16[128,7,2,128]{3,2,1,0:T(2,128)(2,1)S(1)} %bitcast.107), channel_id=1, replica_groups=mesh['fluid_0'=4,'fluid_1'=4,'fluid_2'=2,'solid'=4] {'fluid_0','fluid_1'..., dimensions={0} | all-to-all | bytes 917504 | tf_op jit(solution)/shard_map/all_to_all | solution.py:444
  218.5 7.2 %fluid_side.10 = (bf16[1536,128]{1,0:T(8,128)(2,1)S(1)}, f32[16,128]{1,0:T(8,128)S(1)}, f32[16,128]{1,0:T(8,128)S(1)}) custom-call(s32[2,104]{1,0:T(2,128)S(1)} %pad_add_fusion.1.refs_0_, bf16[16,1792]{1,0:T(8,128)(2,1)S(1)} %broadcast_in_dim.108.refs_1_, bf16[1792,128]{1,0:T(8,128)(2,1)S(1)} %get-tuple-element.54.refs_2_, bf16[1792,128]{1,0:T(8,128)(2,1)S(1)} %bitcast.72, ...), custom_call_target="tpu_custom_call" | custom-call | tf_op jit(solution)/shard_map/fluid_side/pallas_call | solution.py:238
  225.8 16.5 %all_to_all.78 = bf16[128,3,4,128]{3,2,1,0:T(4,128)(2,1)S(1)} all-to-all(bf16[128,3,4,128]{3,2,1,0:T(4,128)(2,1)S(1)} %bitcast.113), channel_id=1, replica_groups=mesh['fluid_0'=4,'fluid_1'=4,'fluid_2'=2,'solid'=4] {'fluid_0','fluid_1'..., dimensions={0} | all-to-all | bytes 786432 | tf_op jit(solution)/shard_map/all_to_all | solution.py:444
  242.2 1.9 shell_side.10
  244.2 17.2 %all_to_all.79 = bf16[128,7,2,128]{3,2,1,0:T(2,128)(2,1)S(1)} all-to-all(bf16[128,7,2,128]{3,2,1,0:T(2,128)(2,1)S(1)} %bitcast.108), channel_id=1, replica_groups=mesh['fluid_0'=4,'fluid_1'=4,'fluid_2'=2,'solid'=4] {'fluid_0','fluid_1'..., dimensions={0} | all-to-all | bytes 917504 | tf_op jit(solution)/shard_map/all_to_all | solution.py:444
  261.4 8.0 %fluid_side.11 = (bf16[1536,128]{1,0:T(8,128)(2,1)S(1)}, bf16[104,768]{1,0:T(8,128)(2,1)}, f32[16,128]{1,0:T(8,128)S(1)}, f32[16,128]{1,0:T(8,128)S(1)}) custom-call(s32[2,104]{1,0:T(2,128)S(1)} %pad_add_fusion.1.refs_0_, bf16[16,1792]{1,0:T(8,128)(2,1)S(1)} %broadcast_in_dim.108.refs_1_, bf16[1792,128]{1,0:T(8,128)(2,1)S(1)} %get-tuple-element.54.refs_2_, ...), custom_call_target="tpu_custom_call" | custom-call | tf_op jit(solution)/shard_map/fluid_side/pallas_call | solution.py:238
  269.4 16.5 %all_to_all.80 = bf16[128,3,4,128]{3,2,1,0:T(4,128)(2,1)S(1)} all-to-all(bf16[128,3,4,128]{3,2,1,0:T(4,128)(2,1)S(1)} %bitcast.109), channel_id=1, replica_groups=mesh['fluid_0'=4,'fluid_1'=4,'fluid_2'=2,'solid'=4] {'fluid_0','fluid_1'..., dimensions={0} | all-to-all | bytes 786432 | tf_op jit(solution)/shard_map/all_to_all | solution.py:444
  285.9 1.7 shell_side.11
  287.6 14.1 %all_to_all.81 = bf16[128,1,2,128]{3,2,1,0:T(2,128)(2,1)} all-to-all(bf16[128,1,2,128]{3,2,1,0:T(2,128)(2,1)S(1)} %reshape.339), channel_id=1, replica_groups=mesh['fluid_0'=4,'fluid_1'=4,'fluid_2'=2,'solid'=4] {'fluid_0','fluid_1'..., dimensions={0} | all-to-all | bytes 131072 | tf_op jit(solution)/shard_map/all_to_all | solution.py:444
  301.8 1.8 closing.1
  (57 shorter events, 0.3 us)
Async XLA Ops:
  2.4 26.0 %all-to-all-start = ((bf16[64,48,128]{2,1,0:T(8,128)(2,1)}), bf16[64,48,128]{2,1,0:T(8,128)(2,1)S(1)}, u32[]{:S(2)}, u32[]{:S(2)}) async-start(bf16[64,48,128]{2,1,0:T(8,128)(2,1)} %broadcast_in_dim.100), calls=%async_computation | async-start | bytes 1572864 | tf_op jit(solution)/shard_map/all_to_all | solution.py:505
  35.9 27.8 %copy-start = (f32[8,768]{1,0:T(8,128)S(1)}, f32[8,768]{1,0:T(8,128)}, u32[]{:S(2)}) copy-start(f32[8,768]{1,0:T(8,128)} %param.15) | copy-start | bytes 73732
  35.9 27.8 %copy-start.2 = (f32[8,768]{1,0:T(8,128)S(1)}, f32[8,768]{1,0:T(8,128)}, u32[]{:S(2)}) copy-start(f32[8,768]{1,0:T(8,128)} %param.14) | copy-start | bytes 73732
  45.2 17.2 %all-to-all-start.2 = ((bf16[128,7,2,128]{3,2,1,0:T(2,128)(2,1)}), bf16[128,7,2,128]{3,2,1,0:T(2,128)(2,1)S(1)}, u32[]{:S(2)}, u32[]{:S(2)}) async-start(bf16[128,7,2,128]{3,2,1,0:T(2,128)(2,1)} %bitcast.13), calls=%async_computation.2 | async-start | bytes 917504 | tf_op jit(solution)/shard_map/all_to_all | solution.py:444
  68.3 217.5 %copy-start.1 = (f32[48,128]{1,0:T(8,128)}, f32[48,128]{1,0:T(8,128)S(1)}, u32[]{:S(2)}) copy-start(f32[48,128]{1,0:T(8,128)S(1)} %get-tuple-element.63.refs_4_.refs_5_.refs_6_.refs_7_.refs_8_) | copy-start | bytes 73732
  85.6 47.4 %slice-start = ((s8[13631488]{0:T(1024)(128)(4,1)}), s8[4194304]{0:T(1024)(128)(4,1)S(1)}, s32[]{:S(2)}) async-start(s8[13631488]{0:T(1024)(128)(4,1)} %bitcast.65), calls=%async_computation.14 | async-start | bytes 8388608
  85.6 47.4 %slice-start.1 = ((s8[13631488]{0:T(1024)(128)(4,1)}), s8[4194304]{0:T(1024)(128)(4,1)S(1)}, s32[]{:S(2)}) async-start(s8[13631488]{0:T(1024)(128)(4,1)} %bitcast.65), calls=%async_computation.15 | async-start | bytes 8388608
  85.6 47.4 %slice-start.2 = ((s8[13631488]{0:T(1024)(128)(4,1)}), s8[4194304]{0:T(1024)(128)(4,1)S(1)}, s32[]{:S(2)}) async-start(s8[13631488]{0:T(1024)(128)(4,1)} %bitcast.65), calls=%async_computation.16 | async-start | bytes 8388608
  94.6 16.5 %copy-start.11 = (f32[16,128]{1,0:T(8,128)}, f32[16,128]{1,0:T(8,128)S(1)}, u32[]{:S(2)}) copy-start(f32[16,128]{1,0:T(8,128)S(1)} %get-tuple-element.93.refs_1_) | copy-start | bytes 24580
  111.1 21.9 %slice-start.3 = ((s8[13631488]{0:T(1024)(128)(4,1)}), s8[1048576]{0:T(1024)(128)(4,1)S(1)}, s32[]{:S(2)}) async-start(s8[13631488]{0:T(1024)(128)(4,1)} %bitcast.65), calls=%async_computation.17 | async-start | bytes 2097152
  115.7 170.1 %copy-start.3 = (f32[48,128]{1,0:T(8,128)}, f32[48,128]{1,0:T(8,128)S(1)}, u32[]{:S(2)}) copy-start(f32[48,128]{1,0:T(8,128)S(1)} %get-tuple-element.70.refs_6_.refs_7_.refs_8_.refs_9_) | copy-start | bytes 73732
  115.7 40.8 %slice-start.4 = ((s8[9437184]{0:T(1024)(128)(4,1)}), s8[4194304]{0:T(1024)(128)(4,1)S(1)}, s32[]{:S(2)}) async-start(s8[9437184]{0:T(1024)(128)(4,1)} %bitcast.67), calls=%async_computation.18 | async-start | bytes 8388608
  133.0 23.6 %slice-start.5 = ((s8[9437184]{0:T(1024)(128)(4,1)}), s8[4194304]{0:T(1024)(128)(4,1)S(1)}, s32[]{:S(2)}) async-start(s8[9437184]{0:T(1024)(128)(4,1)} %bitcast.67), calls=%async_computation.19 | async-start | bytes 8388608
  133.0 23.6 %slice-start.6 = ((s8[9437184]{0:T(1024)(128)(4,1)}), s8[1048576]{0:T(1024)(128)(4,1)S(1)}, s32[]{:S(2)}) async-start(s8[9437184]{0:T(1024)(128)(4,1)} %bitcast.67), calls=%async_computation.20 | async-start | bytes 2097152
  140.1 121.3 %copy-start.6 = (f32[16,128]{1,0:T(8,128)}, f32[16,128]{1,0:T(8,128)S(1)}, u32[]{:S(2)}) copy-start(f32[16,128]{1,0:T(8,128)S(1)} %get-tuple-element.72.refs_6_.refs_7_.refs_8_.refs_2_) | copy-start | bytes 24580
  158.5 127.3 %copy-start.4 = (f32[48,128]{1,0:T(8,128)}, f32[48,128]{1,0:T(8,128)S(1)}, u32[]{:S(2)}) copy-start(f32[48,128]{1,0:T(8,128)S(1)} %get-tuple-element.77.refs_8_.refs_9_.refs_10_) | copy-start | bytes 73732
  182.9 78.5 %copy-start.8 = (f32[16,128]{1,0:T(8,128)}, f32[16,128]{1,0:T(8,128)S(1)}, u32[]{:S(2)}) copy-start(f32[16,128]{1,0:T(8,128)S(1)} %get-tuple-element.79.refs_8_.refs_9_.refs_3_) | copy-start | bytes 24580
  201.3 84.6 %copy-start.5 = (f32[48,128]{1,0:T(8,128)}, f32[48,128]{1,0:T(8,128)S(1)}, u32[]{:S(2)}) copy-start(f32[48,128]{1,0:T(8,128)S(1)} %get-tuple-element.84.refs_10_.refs_11_.refs_9_) | copy-start | bytes 73732
  225.7 43.6 %copy-start.9 = (f32[16,128]{1,0:T(8,128)}, f32[16,128]{1,0:T(8,128)S(1)}, u32[]{:S(2)}) copy-start(f32[16,128]{1,0:T(8,128)S(1)} %get-tuple-element.86.refs_10_.refs_4_) | copy-start | bytes 24580
  244.2 41.7 %copy-start.7 = (f32[48,128]{1,0:T(8,128)}, f32[48,128]{1,0:T(8,128)S(1)}, u32[]{:S(2)}) copy-start(f32[48,128]{1,0:T(8,128)S(1)} %get-tuple-element.91.refs_12_.refs_10_) | copy-start | bytes 73732
  269.4 18.2 %copy-start.12 = (f32[16,128]{1,0:T(8,128)}, f32[16,128]{1,0:T(8,128)S(1)}, u32[]{:S(2)}) copy-start(f32[16,128]{1,0:T(8,128)S(1)} %get-tuple-element.94.refs_5_) | copy-start | bytes 24580
  287.6 14.2 %copy-start.10 = (f32[48,128]{1,0:T(8,128)}, f32[48,128]{1,0:T(8,128)S(1)}, u32[]{:S(2)}) copy-start(f32[48,128]{1,0:T(8,128)S(1)} %get-tuple-element.95.refs_11_) | copy-start | bytes 73732
